TPU v7x, 512 devices: a whole 4x8x8 slice. The times are simulated.
512 devices in a mesh: cells: 64 (over y_hi, z, x), tensor: 8 (over y_lo, core).
Axes of the slice: x: 4, y: 8 (y_hi: 2, y_lo: 4; y = y_hi * 4 + y_lo), z: 8, core: 2. Of those that a mesh axis runs over, the one named last changes fastest.
Arguments:
- features: bfloat16 [65536, 512], P(('cells', 'tensor')), may hold values from -48 to 48
- cotangent: bfloat16 [65536, 512], P(('cells', 'tensor')), may hold values from -6 to 6
- first_gain: float32 [512], replicated, may hold values from 0.5 to 1.5
- project_weight: bfloat16 [3, 512, 512], replicated, may hold values from -1 to 1
- output_weight: bfloat16 [512, 512], replicated, may hold values from -0.25 to 0.25
- neighbours: int32 [65536, 64], P(('cells', 'tensor')), may hold values from 0 to 191, as said below
- neighbour_live: int32 [65536, 64], P(('cells', 'tensor')), may hold values from 0 to 1, as said below
- send_rows: int32 [2048, 16], P(('cells', 'tensor')), may hold values from 0 to 127
Outputs:
- layer_output: bfloat16 [65536, 512], P(('cells', 'tensor'))
- grad_features: float32 [65536, 512], P(('cells', 'tensor'))
- grad_project: float32 [786432], P(('cells', 'tensor'))
- grad_output: float32 [262144], P(('cells', 'tensor'))
Inputs may be any that keep to these rules, and one draw needn't show every extreme that they name: `neighbours`: entry 0 of each row is the cell's own row within its block. `neighbour_live`: entry 0 of each row is 1, and the ones of a row come first.
All inputs are finite; a program needn't handle non-finite values.
Results may differ from a plain program's by a relative error of at most 0.0055.
The roundings to bfloat16 on the way count: a program that leaves them out, or rounds other values in their place, can miss the bound.
Values may be sent and summed in bfloat16 or wider, within the bound.
No kernel may reach another device: no remote copies, remote signals or barrier semaphores. Data moves between devices by JAX's collectives and lax.ppermute only.
A program may use at most 64 MiB of HBM per device.

v0:
```python
import jax
import jax.numpy as jnp
from jax import lax
from jax.sharding import PartitionSpec as P

HEADS = 8


EPSILON = 1e-06


def shifted(block, axis, distance):
    devices = range(lax.axis_size(axis))
    route = [((i - distance) % len(devices), i) for i in devices]
    return lax.ppermute(block, axis, route)


def norm_rows(inputs, gain):
    values = inputs.astype(jnp.float32)
    factor = lax.rsqrt(jnp.mean(values * values, axis=-1, keepdims=True) + EPSILON)
    return (values * factor * gain).astype(jnp.bfloat16)


def norm_back(inputs, gain, upstream):
    values = inputs.astype(jnp.float32)
    factor = lax.rsqrt(jnp.mean(values * values, axis=-1, keepdims=True) + EPSILON)
    weighted = upstream * gain
    return factor * weighted - values * factor**3 * jnp.mean(
        values * weighted, axis=-1, keepdims=True
    )


def project(first, project_weight):
    projected = [
        jnp.dot(first, project_weight[part_index], preferred_element_type=jnp.float32).astype(
            jnp.bfloat16
        )
        for part_index in range(3)
    ]
    return (projected[0], jnp.concatenate([projected[1], projected[2]], axis=1))


def halo_table(key_values, send_rows):
    received = [key_values]
    for direction in range(4):
        band_rows = key_values[send_rows[direction]]
        offset = 1 - 2 * (direction % 2)
        if direction < 2:
            received.append(shifted(band_rows, "tensor", offset))
        else:
            received.append(shifted(band_rows, "cells", offset))
    return jnp.concatenate(received, axis=0)


def return_grads(merged, send_rows, own_rows):
    band_size = send_rows.shape[1]
    summed = merged[:own_rows]
    for direction in range(4):
        first_row = own_rows + direction * band_size
        band_rows = merged[first_row : first_row + band_size]
        offset = 1 - 2 * (direction % 2)
        if direction < 2:
            returned = shifted(band_rows.astype(jnp.bfloat16), "tensor", -offset).astype(
                band_rows.dtype
            )
        else:
            returned = shifted(band_rows.astype(jnp.bfloat16), "cells", -offset).astype(
                band_rows.dtype
            )
        summed = summed.at[send_rows[direction]].add(returned)
    return summed


def slot_counts(neighbours, neighbour_live, table_rows):
    own_rows = neighbours.shape[0]
    row_ids = jnp.broadcast_to(jnp.arange(own_rows, dtype=jnp.int32)[:, None], neighbours.shape)
    empty = jnp.zeros((own_rows, table_rows), jnp.float32)
    return empty.at[row_ids, neighbours].add(neighbour_live.astype(jnp.float32))


def by_heads(rows):
    return rows.reshape(rows.shape[0], HEADS, -1).transpose(1, 0, 2)


def from_heads(stacked):
    return stacked.transpose(1, 0, 2).reshape(stacked.shape[1], -1)


def head_weights(query_rows, key_rows, counts):
    scores = lax.dot_general(
        query_rows, key_rows, (((1,), (1,)), ((), ())), preferred_element_type=jnp.float32
    ) * query_rows.shape[1] ** (-0.5)
    is_live = counts > 0
    scores = jnp.where(is_live, scores, -1e30)
    row_max = jnp.max(scores, axis=-1, keepdims=True)
    powers = jnp.where(is_live, jnp.exp(scores - row_max), 0.0)
    probabilities = powers / jnp.sum(counts * powers, axis=-1, keepdims=True)
    rounded = lax.optimization_barrier(probabilities.astype(jnp.bfloat16))
    return (probabilities, counts * rounded.astype(jnp.float32))


def body(
    features,
    cotangent,
    first_gain,
    project_weight,
    output_weight,
    neighbours,
    neighbour_live,
    send_rows,
):
    own_rows = features.shape[0]
    head_span = project_weight.shape[2]
    highest = lax.Precision.HIGHEST
    grad_scale = float(own_rows * lax.axis_size("cells") * lax.axis_size("tensor")) ** (-0.5)
    first = norm_rows(features, first_gain)
    queries, key_values = project(first, project_weight)
    key_table = halo_table(key_values, send_rows)
    counts = slot_counts(neighbours, neighbour_live, key_table.shape[0])

    def head_forward(inputs_head):
        query_rows, key_rows, value_rows = inputs_head
        probabilities, weights = head_weights(query_rows, key_rows, counts)
        return jnp.dot(weights, value_rows.astype(jnp.float32), precision=highest).astype(
            jnp.bfloat16
        )

    mixed = from_heads(
        lax.map(
            head_forward,
            (
                by_heads(queries),
                by_heads(key_table[:, :head_span]),
                by_heads(key_table[:, head_span:]),
            ),
        )
    )
    layer_output = (
        features.astype(jnp.float32)
        + jnp.dot(mixed, output_weight, preferred_element_type=jnp.float32)
    ).astype(jnp.bfloat16)
    grad_mixed = lax.dot_general(
        cotangent, output_weight, (((1,), (1,)), ((), ())), preferred_element_type=jnp.float32
    ).astype(jnp.bfloat16)
    grad_output = (
        lax.dot_general(
            cotangent, mixed, (((0,), (0,)), ((), ())), preferred_element_type=jnp.float32
        )
        * grad_scale
    ).reshape(-1)
    attn_queries, attn_table = (queries, key_table)

    def head_backward(inputs_head):
        query_rows, key_rows, value_rows, upstream = inputs_head
        probabilities, weights = head_weights(query_rows, key_rows, counts)
        grad_probs = lax.dot_general(
            upstream, value_rows, (((1,), (1,)), ((), ())), preferred_element_type=jnp.float32
        )
        spread = counts * probabilities
        grad_scores = spread * (grad_probs - jnp.sum(spread * grad_probs, axis=-1, keepdims=True))
        factor = query_rows.shape[1] ** (-0.5)
        grad_query = jnp.dot(grad_scores, key_rows.astype(jnp.float32), precision=highest) * factor
        grad_keys = (
            lax.dot_general(
                grad_scores,
                query_rows.astype(jnp.float32),
                (((0,), (0,)), ((), ())),
                precision=highest,
            )
            * factor
        )
        grad_values = lax.dot_general(
            weights, upstream.astype(jnp.float32), (((0,), (0,)), ((), ())), precision=highest
        )
        return (grad_query, grad_keys, grad_values)

    grad_query_heads, grad_key_heads, grad_value_heads = lax.map(
        head_backward,
        (
            by_heads(attn_queries),
            by_heads(attn_table[:, :head_span]),
            by_heads(attn_table[:, head_span:]),
            by_heads(grad_mixed),
        ),
    )
    merged = jnp.concatenate([from_heads(grad_key_heads), from_heads(grad_value_heads)], axis=1)
    grad_key_values = return_grads(merged, send_rows, own_rows)
    grad_qkv = jnp.stack(
        [
            from_heads(grad_query_heads),
            grad_key_values[:, :head_span],
            grad_key_values[:, head_span:],
        ]
    ).astype(jnp.bfloat16)
    grad_project = (
        jnp.einsum("nd,cnf->cdf", first, grad_qkv, preferred_element_type=jnp.float32) * grad_scale
    ).reshape(-1)
    grad_first = jnp.einsum(
        "cnf,cdf->nd", grad_qkv, project_weight, preferred_element_type=jnp.float32
    )
    grad_features = cotangent.astype(jnp.float32) + norm_back(features, first_gain, grad_first)
    grad_project, grad_output = (
        lax.psum_scatter(grad_project, ("cells", "tensor"), scatter_dimension=0, tiled=True),
        lax.psum_scatter(grad_output, ("cells", "tensor"), scatter_dimension=0, tiled=True),
    )
    return (layer_output, grad_features, grad_project, grad_output)


def solution(mesh):
    placed = (
        P(("cells", "tensor"), None),
        P(("cells", "tensor"), None),
        P(),
        P(),
        P(),
        P(("cells", "tensor"), None),
        P(("cells", "tensor"), None),
        P(("cells", "tensor"), None),
    )
    return jax.shard_map(
        body,
        mesh=mesh,
        in_specs=placed,
        out_specs=(
            P(("cells", "tensor"), None),
            P(("cells", "tensor"), None),
            P(("cells", "tensor")),
            P(("cells", "tensor")),
        ),
        check_vma=False,
    )
```

profile of v0, /device:TPU:24, one launch (start us, length us, event | category | flops | bytes accessed | tf_op | source)
XLA Modules:
  0.0 429.7 jit_solution(5528652753444829321)
XLA Ops:
  7.2 1.1 fusion.55
  8.8 1.4 convolution_convert_fusion.2
  10.3 1.4 convolution_convert_fusion.3
  12.9 1.9 collective-permute-start
  15.5 3.6 collective-permute-start.1
  19.7 3.4 collective-permute-start.2
  23.7 14.2 %collective-permute-start.3 = (bf16[16,1024]{1,0:T(8,128)(2,1)S(1)}, bf16[16,1024]{1,0:T(8,128)(2,1)S(1)}, u32[]{:S(2)}, u32[]{:S(2)}) collective-permute-start(bf16[16,1024]{1,0:T(8,128)(2,1)S(1)} %gather_fusion.3), channel_id=1, source_target_pairs={{8,0},{16,8},{24,16},{32,24},{40,32},{48,40},{56,48},{64,56},{72,6... | collective-permute-start | bytes 98312 | tf_op jit(solution)/shard_map/ppermute | solution.py:15
  38.0 1.3 convolution_convert_fusion.4
  40.7 43.2 %scatter_custom_fusion.4 = f32[24576]{0:T(1024)S(1)} fusion(s32[8192]{0:T(1024)S(1)} %reshape.263, f32[8192]{0:T(1024)S(1)} %reshape.265, f32[]{:T(128)} %constant.40.clone.1), kind=kCustom, calls=%fused_computation.118 | custom fusion | flops 8192 | bytes 98308
  84.8 4.5 %while.24 = (s32[]{:T(128)}, bf16[8,128,64]{1,2,0:T(8,128)(2,1)S(1)}, f32[128,192]{0,1:T(8,128)S(1)}, bf16[8,128,64]{2,1,0:T(8,128)(2,1)S(1)}, bf16[8,192,64]{2,...) while((s32[]{:T(128)}, bf16[8,128,64]{1,2,0:T(8,128)(2,1)S(1)}, f32[128,192]{0,1:T(8,128)S(1)}, ...), condition=%wide.region_5.6_spmd, body=%wide.region_2.5_spmd.sunk | while | flops 22421248 | bytes 938581 | solution.py:129
  89.3 9.8 %while.25 = (s32[]{:T(128)}, bf16[8,128,64]{1,2,0:T(8,128)(2,1)S(1)}, f32[8,192,64]{1,2,0:T(8,128)S(1)}, f32[8,192,64]{1,2,0:T(8,128)S(1)}, f32[128,192]{0,1:T(8...) while((s32[]{:T(128)}, ...), condition=%wide.region_10.11_spmd, body=%wide.region_6.10_spmd.sunk | while | flops 63499904 | bytes 1795181 | solution.py:177
  99.1 0.6 copy-done.5
  100.9 1.9 collective-permute-start.4
  102.8 2.9 collective-permute-start.5
  105.7 3.7 collective-permute-start.6
  109.4 2.2 collective-permute-start.7
  111.9 0.8 copy.53
  113.0 1.3 copy.60
  114.3 1.2 scatter_custom_fusion
  115.5 1.2 scatter_custom_fusion.1
  116.7 1.2 scatter_custom_fusion.2
  117.9 6.3 %collective-permute-done.7 = bf16[16,1024]{1,0:T(8,128)(2,1)} collective-permute-done((bf16[16,1024]{1,0:T(8,128)(2,1)}, bf16[16,1024]{1,0:T(8,128)(2,1)}, u32[]{:S(2)}, u32[]{:S(2)}) %collective-permute-start.7) | collective-permute-done | bytes 32800 | tf_op jit(solution)/shard_map/ppermute | solution.py:15
  124.2 1.2 scatter_custom_fusion.3
  125.5 2.3 multiply_bitcast_fusion
  127.8 3.6 copy.55
  131.4 4.4 %copy.59 = f32[192,4,8,128]{3,1,2,0:T(4,128)} copy(f32[192,4,8,128]{3,2,1,0:T(8,128)} %bitcast.167) | data formatting | bytes 6291456
  135.8 0.9 fusion.46
  137.2 0.7 fusion.61
  138.0 0.8 fusion.60
  138.8 281.4 %all-reduce.5.cloned.1.call-done = (f32[786432]{0:T(1024)}, f32[262144]{0:T(1024)}) async-done(((f32[786432]{0:T(1024)}, f32[262144]{0:T(1024)}), (f32[786432]{0:T(1024)}, f32[262144]{0:T(1024)})) %all-reduce.5.cloned.1.call-update) | async-done | bytes 4194320
  420.2 1.4 dynamic-slice
  421.5 1.3 dynamic-slice.1
  (172 shorter events, 21.7 us)
Async XLA Ops:
  7.2 32.4 %copy-start = (bf16[512,512]{1,0:T(8,128)(2,1)S(1)}, bf16[512,512]{1,0:T(8,128)(2,1)}, u32[]{:S(2)}) copy-start(bf16[512,512]{1,0:T(8,128)(2,1)} %param.16) | copy-start | bytes 1572868
  7.2 4.5 %copy-start.10 = (s32[4,16]{1,0:T(4,128)S(1)}, s32[4,16]{1,0:T(4,128)}, u32[]{:S(2)}) copy-start(s32[4,16]{1,0:T(4,128)} %param.19) | copy-start | bytes 772
  7.2 413.0 %all-reduce.5.cloned.1.call-start = ((), (), s32[]{:S(2)}) async-start(), calls=%async_computation | async-start | bytes 8388608
  8.8 29.1 %copy-start.12 = (f32[128]{0:T(128)}, f32[128]{0:T(128)S(1)}, u32[]{:S(2)}) copy-start(f32[128]{0:T(128)S(1)} %get-tuple-element.174) | copy-start | bytes 1540
  10.2 27.8 %copy-start.1 = (bf16[128,512]{1,0:T(8,128)(2,1)S(1)}, bf16[128,512]{1,0:T(8,128)(2,1)}, u32[]{:S(2)}) copy-start(bf16[128,512]{1,0:T(8,128)(2,1)} %param.12) | copy-start | bytes 393220
  10.2 27.7 %copy-start.9 = (f32[512]{0:T(512)S(1)}, f32[512]{0:T(512)}, u32[]{:S(2)}) copy-start(f32[512]{0:T(512)} %param.14) | copy-start | bytes 6148
  11.7 27.6 %copy-start.7 = (s32[128,64]{0,1:T(8,128)S(1)}, s32[128,64]{0,1:T(8,128)}, u32[]{:S(2)}) copy-start(s32[128,64]{0,1:T(8,128)} %param.17) | copy-start | bytes 98308
  11.7 27.6 %copy-start.14 = (s32[2]{0:T(128)S(1)}, s32[2]{0:T(128)}, u32[]{:S(2)}) copy-start(s32[2]{0:T(128)} %constant.80) | copy-start | bytes 28
  11.7 27.7 %copy-start.15 = (s32[2]{0:T(128)S(1)}, s32[2]{0:T(128)}, u32[]{:S(2)}) copy-start(s32[2]{0:T(128)} %constant.77) | copy-start | bytes 28
  11.8 0.5 copy-start.11
  12.3 27.3 %copy-start.2 = (bf16[128,512]{1,0:T(8,128)(2,1)S(1)}, bf16[128,512]{1,0:T(8,128)(2,1)}, u32[]{:S(2)}) copy-start(bf16[128,512]{1,0:T(8,128)(2,1)} %param.13) | copy-start | bytes 393220
  12.9 71.0 %collective-permute-start = (bf16[16,1024]{1,0:T(8,128)(2,1)S(1)}, bf16[16,1024]{1,0:T(8,128)(2,1)S(1)}, u32[]{:S(2)}, u32[]{:S(2)}) collective-permute-start(bf16[16,1024]{1,0:T(8,128)(2,1)S(1)} %gather_fusion), channel_id=1, source_target_pairs={{7,0},{0,1},{1,2},{2,3},{3,4},{4,5},{5,6},{6,7},{15,8},{8,9},{9,10... | collective-permute-start | bytes 98312 | tf_op jit(solution)/shard_map/ppermute | solution.py:15
  14.9 25.2 %copy-start.8 = (s32[128,64]{0,1:T(8,128)S(1)}, s32[128,64]{0,1:T(8,128)}, u32[]{:S(2)}) copy-start(s32[128,64]{0,1:T(8,128)} %param.18) | copy-start | bytes 98308
  15.5 68.5 %collective-permute-start.1 = (bf16[16,1024]{1,0:T(8,128)(2,1)S(1)}, bf16[16,1024]{1,0:T(8,128)(2,1)S(1)}, u32[]{:S(2)}, u32[]{:S(2)}) collective-permute-start(bf16[16,1024]{1,0:T(8,128)(2,1)S(1)} %gather_fusion.1), channel_id=1, source_target_pairs={{1,0},{2,1},{3,2},{4,3},{5,4},{6,5},{7,6},{0,7},{9,8},{10,9},{11,1... | collective-permute-start | bytes 98312 | tf_op jit(solution)/shard_map/ppermute | solution.py:15
  19.7 64.3 %collective-permute-start.2 = (bf16[16,1024]{1,0:T(8,128)(2,1)S(1)}, bf16[16,1024]{1,0:T(8,128)(2,1)S(1)}, u32[]{:S(2)}, u32[]{:S(2)}) collective-permute-start(bf16[16,1024]{1,0:T(8,128)(2,1)S(1)} %gather_fusion.2), channel_id=1, source_target_pairs={{504,0},{0,8},{8,16},{16,24},{24,32},{32,40},{40,48},{48,56},{56,6... | collective-permute-start | bytes 98312 | tf_op jit(solution)/shard_map/ppermute | solution.py:15
  23.7 60.3 %collective-permute-start.3 = (bf16[16,1024]{1,0:T(8,128)(2,1)S(1)}, bf16[16,1024]{1,0:T(8,128)(2,1)S(1)}, u32[]{:S(2)}, u32[]{:S(2)}) collective-permute-start(bf16[16,1024]{1,0:T(8,128)(2,1)S(1)} %gather_fusion.3), channel_id=1, source_target_pairs={{8,0},{16,8},{24,16},{32,24},{40,32},{48,40},{56,48},{64,56},{72,6... | collective-permute-start | bytes 98312 | tf_op jit(solution)/shard_map/ppermute | solution.py:15
  84.8 4.5 %copy-start.3 = (f32[8,192,64]{1,2,0:T(8,128)S(1)}, f32[8,192,64]{1,2,0:T(8,128)}, u32[]{:S(2)}) copy-start(f32[8,192,64]{1,2,0:T(8,128)} %custom-call.12) | copy-start | bytes 1179652
  99.1 0.7 copy-start.5
  100.2 11.7 %copy-start.6 = (bf16[8,128,64]{1,2,0:T(8,128)(2,1)S(1)}, bf16[8,128,64]{1,2,0:T(8,128)(2,1)}, u32[]{:S(2)}) copy-start(bf16[8,128,64]{1,2,0:T(8,128)(2,1)} %copy-done.5) | copy-start | bytes 393220
  100.9 13.4 %collective-permute-start.4 = (bf16[16,1024]{1,0:T(8,128)(2,1)}, bf16[16,1024]{1,0:T(8,128)(2,1)}, u32[]{:S(2)}, u32[]{:S(2)}) collective-permute-start(bf16[16,1024]{1,0:T(8,128)(2,1)} %get-tuple-element.162), channel_id=1, source_target_pairs={{1,0},{2,1},{3,2},{4,3},{5,4},{6,5},{7,6},{0,7},{9,8},{10,9},{11,1... | collective-permute-start | bytes 98312 | tf_op jit(solution)/shard_map/ppermute | solution.py:15
  102.8 12.7 %collective-permute-start.5 = (bf16[16,1024]{1,0:T(8,128)(2,1)}, bf16[16,1024]{1,0:T(8,128)(2,1)}, u32[]{:S(2)}, u32[]{:S(2)}) collective-permute-start(bf16[16,1024]{1,0:T(8,128)(2,1)} %get-tuple-element.161), channel_id=1, source_target_pairs={{7,0},{0,1},{1,2},{2,3},{3,4},{4,5},{5,6},{6,7},{15,8},{8,9},{9,10... | collective-permute-start | bytes 98312 | tf_op jit(solution)/shard_map/ppermute | solution.py:15
  105.7 11.0 %collective-permute-start.6 = (bf16[16,1024]{1,0:T(8,128)(2,1)}, bf16[16,1024]{1,0:T(8,128)(2,1)}, u32[]{:S(2)}, u32[]{:S(2)}) collective-permute-start(bf16[16,1024]{1,0:T(8,128)(2,1)} %get-tuple-element.160), channel_id=1, source_target_pairs={{8,0},{16,8},{24,16},{32,24},{40,32},{48,40},{56,48},{64,56},{72,6... | collective-permute-start | bytes 98312 | tf_op jit(solution)/shard_map/ppermute | solution.py:15
  109.4 14.8 %collective-permute-start.7 = (bf16[16,1024]{1,0:T(8,128)(2,1)}, bf16[16,1024]{1,0:T(8,128)(2,1)}, u32[]{:S(2)}, u32[]{:S(2)}) collective-permute-start(bf16[16,1024]{1,0:T(8,128)(2,1)} %get-tuple-element.159), channel_id=1, source_target_pairs={{504,0},{0,8},{8,16},{16,24},{24,32},{32,40},{40,48},{48,56},{56,6... | collective-permute-start | bytes 98312 | tf_op jit(solution)/shard_map/ppermute | solution.py:15
  115.5 10.0 %copy-start.4 = (bf16[1,128,512]{2,1,0:T(8,128)(2,1)S(1)}, bf16[1,128,512]{2,1,0:T(8,128)(2,1)}, u32[]{:S(2)}) copy-start(bf16[1,128,512]{2,1,0:T(8,128)(2,1)} %copy.53) | copy-start | bytes 393220
  115.5 10.0 %copy-start.13 = (f32[128]{0:T(128)S(1)}, f32[128]{0:T(128)}, u32[]{:S(2)}) copy-start(f32[128]{0:T(128)} %copy-done.12) | copy-start | bytes 1540
  135.8 1.5 copy-start.17
  137.2 0.7 copy-start.16
Sparse Core Ops, SparseCore 0:
  135.9 284.2 all-reduce.4
where the time goes:
time: 431 us; the launch traced here: 430 us
  waiting for transfers between devices  288 us (67%)
  other arithmetic  51.9 us (12%)
  starting transfers between devices  33.9 us (8%)
  matrix products  21.3 us (5%)
  local copies, waits for them, and re-layouts  19.7 us (5%)
  between operations  14.7 us (3%)
    unnamed x2, waiting for transfers between devices  281 us
    unnamed x4, other arithmetic  43.4 us
    ppermute x8, starting transfers between devices, shifted(): return lax.ppermute(block, axis, route)  33.9 us
    unnamed x45, local copies, waits for them, and re-layouts  10.3 us
  transfers between devices with their start and end apart: 9, of which 2 were waited for; matrix products, arithmetic and copies ran while one was open for 13% of the time, Pallas kernels for 0%

commit v1 on v0

v1 whole, which is shorter than its diff:
```python
import math

import jax
import jax.numpy as jnp
import numpy as np
from jax import lax
from jax.experimental import pallas as pl
from jax.experimental.pallas import tpu as pltpu
from jax.sharding import Mesh
from jax.sharding import PartitionSpec as P

HEADS = 8
HEAD_DIM = 64
EPSILON = 1e-06
F32 = jnp.float32
BF16 = jnp.bfloat16
AXES = ("yh", "z", "x", "yl", "core")
CELLS = ("yh", "z", "x")
TENSOR = ("yl", "core")
FAR = ("yh", "z", "yl")


def dot(a, b, dims=((1,), (0,))):
    return lax.dot_general(a, b, (dims, ((), ())), preferred_element_type=F32)


def split(values):
    high = values.astype(BF16)
    return high, (values - high.astype(F32)).astype(BF16)


def call(kernel, out_shapes, args, us, scalars=0, scratch=()):
    specs = [pl.BlockSpec(memory_space=pltpu.SMEM)] * scalars
    specs += [pl.BlockSpec(memory_space=pltpu.VMEM)] * (len(args) - scalars)
    return pl.pallas_call(
        kernel,
        out_shape=out_shapes,
        in_specs=specs,
        out_specs=jax.tree.map(lambda _: pl.BlockSpec(memory_space=pltpu.VMEM), out_shapes),
        scratch_shapes=list(scratch),
        cost_estimate=pl.CostEstimate(
            flops=int(us * 4e8), bytes_accessed=int(us * 1e6), transcendentals=0
        ),
    )(*args)


def shape(*dims, dtype=BF16):
    return jax.ShapeDtypeStruct(dims, dtype)


def norm_factor(values):
    return lax.rsqrt(jnp.mean(values * values, axis=-1, keepdims=True) + EPSILON)


def keys_kernel(features, gain, weight, send_rows, first, key_values, *bands):
    values = features[...].astype(F32)
    normed = (values * norm_factor(values) * gain[...]).astype(BF16)
    first[...] = normed
    width = weight.shape[2]
    for part in range(2):
        key_values[:, part * width : (part + 1) * width] = dot(normed, weight[1 + part]).astype(
            BF16
        )
    table = key_values[...]
    rows, cap = features.shape[0], send_rows.shape[1]
    row_ids = lax.broadcasted_iota(jnp.int32, (rows, cap), 0)
    for direction in range(4):
        chosen = (row_ids == send_rows[direction : direction + 1, :]).astype(F32).astype(BF16)
        bands[direction][...] = dot(chosen, table, ((0,), (0,))).astype(BF16)


def queries_kernel(
    first, weight, output_weight, cotangent, neighbours, live, queries, grad_mixed, counts
):
    queries[...] = dot(first[...], weight[0]).astype(BF16)
    grad_mixed[...] = dot(cotangent[...], output_weight[...], ((1,), (1,))).astype(BF16)
    slots = jnp.where(live[...] > 0, neighbours[...], -1)
    rows = slots.shape[0]
    columns = lax.broadcasted_iota(jnp.int32, (rows, counts.shape[1]), 1)
    total = jnp.zeros(columns.shape, F32)
    for slot in range(slots.shape[1]):
        total = total + jnp.where(slots[:, slot : slot + 1] == columns, 1.0, 0.0)
    counts[...] = total


def attention_kernel(
    queries, key_values, band0, band1, band2, band3, grad_mixed, counts, first, cotangent,
    sent, own, back0, back1, back2, back3, table, grads,
):
    rows, width = queries.shape
    cap = band0.shape[0]
    table[:rows, :] = key_values[...]
    for direction, band in enumerate((band0, band1, band2, band3)):
        start = rows + direction * cap
        table[start : start + cap, :] = band[...]
    factor = HEAD_DIM**-0.5
    count = counts[...]
    is_live = count > 0
    wide = 2 * HEAD_DIM
    side = lax.broadcasted_iota(jnp.int32, (1, wide), 1) // HEAD_DIM
    for pair in range(HEADS // 2):
        lanes = slice(pair * wide, (pair + 1) * wide)
        value_lanes = slice(width + pair * wide, width + (pair + 1) * wide)
        query, upstream = queries[:, lanes], grad_mixed[:, lanes]
        key, value = table[:, lanes], table[:, value_lanes]
        zero = jnp.zeros((), BF16)
        mixed, grad_query, grad_key, grad_value = [], [], None, None
        for half in range(2):
            mine = side == half
            query_half = jnp.where(mine, query, zero)
            upstream_half = jnp.where(mine, upstream, zero)
            scores = dot(query_half, key, ((1,), (1,))) * factor
            grad_probs = dot(upstream_half, value, ((1,), (1,)))
            scores = jnp.where(is_live, scores, -1e30)
            row_max = jnp.max(scores, axis=-1, keepdims=True)
            powers = jnp.where(is_live, jnp.exp(scores - row_max), 0.0)
            probabilities = powers / jnp.sum(count * powers, axis=-1, keepdims=True)
            weights = split(count * probabilities.astype(BF16).astype(F32))
            spread = count * probabilities
            grad_scores = spread * (
                grad_probs - jnp.sum(spread * grad_probs, axis=-1, keepdims=True)
            )
            grad_scores = split(grad_scores * factor)
            mixed.append(dot(weights[0], value) + dot(weights[1], value))
            grad_query.append(dot(grad_scores[0], key) + dot(grad_scores[1], key))
            grad_k = sum(dot(g, query_half, ((0,), (0,))) for g in grad_scores)
            grad_v = sum(dot(w, upstream_half, ((0,), (0,))) for w in weights)
            grad_key = grad_k if half == 0 else grad_key + grad_k
            grad_value = grad_v if half == 0 else grad_value + grad_v
        at = 2 * width + pair * wide
        sent[:, at : at + wide] = jnp.where(side == 0, mixed[0], mixed[1]).astype(BF16)
        at = 3 * width + pair * wide
        sent[:, at : at + wide] = jnp.where(side == 0, grad_query[0], grad_query[1]).astype(BF16)
        grads[:, lanes] = grad_key
        grads[:, value_lanes] = grad_value
    own[...] = grads[:rows, :]
    for direction, back in enumerate((back0, back1, back2, back3)):
        start = rows + direction * cap
        back[...] = grads[start : start + cap, :].astype(BF16)
    sent[:, :width] = first[...]
    sent[:, width : 2 * width] = cotangent[...]


def layer_kernel(features, sent, output_weight, layer_output):
    width = features.shape[1]
    mixed = sent[:, 2 * width : 3 * width]
    layer_output[...] = (features[...].astype(F32) + dot(mixed, output_weight[...])).astype(BF16)


def chosen_kernel(core, sent, partner, feature_of, cell_of, per_core, left, grad_output):
    rows, width = sent.shape[0], grad_output.shape[1]
    offset = core[0, 0]
    columns = lax.broadcasted_iota(jnp.int32, (feature_of.shape[0], width), 1)
    target = feature_of[...] + offset * per_core[0, 0]
    feature = jnp.bitwise_and(target, width - 1)
    chosen = (feature == columns).astype(F32).astype(BF16)
    part = jnp.right_shift(target, width.bit_length() - 1)
    for index, source in enumerate((sent, partner)):
        picked = dot(chosen, source[:, :width], ((1,), (1,)))
        for piece in range(3):
            at = (2 * piece + index) * rows
            left[:, at : at + rows] = jnp.where(part == piece, picked, 0.0).astype(BF16)
    columns = lax.broadcasted_iota(jnp.int32, (cell_of.shape[0], width), 1)
    chosen = (cell_of[...] + offset * per_core[0, 1] == columns).astype(F32).astype(BF16)
    total = None
    for source in (sent, partner):
        picked = dot(chosen, source[:, width : 2 * width], ((1,), (1,))).astype(BF16)
        product = dot(picked, source[:, 2 * width : 3 * width])
        total = product if total is None else total + product
    grad_output[...] = total


def merge_kernel(own, back0, back1, back2, back3, send_rows, grad_keys_values):
    rows, cap = own.shape[0], send_rows.shape[1]
    row_ids = lax.broadcasted_iota(jnp.int32, (rows, cap), 0)
    total = own[...]
    for direction, back in enumerate((back0, back1, back2, back3)):
        chosen = (row_ids == send_rows[direction : direction + 1, :]).astype(F32).astype(BF16)
        total = total + dot(chosen, back[...])
    grad_keys_values[...] = total.astype(BF16)


def project_kernel(left, sent, partner, own_grads, partner_grads, grad_project, right):
    rows, width = sent.shape[0], grad_project.shape[1]
    for index, (early, late) in enumerate(((sent, own_grads), (partner, partner_grads))):
        pieces = (
            early[:, 3 * width : 4 * width],
            late[:, :width],
            late[:, width : 2 * width],
        )
        for piece in range(3):
            at = (2 * piece + index) * rows
            right[at : at + rows, :] = pieces[piece]
    grad_project[...] = dot(left[...], right[...])


def features_kernel(features, cotangent, gain, sent, late, weight, grad_features):
    width = features.shape[1]
    grad_first = dot(sent[:, 3 * width : 4 * width], weight[0], ((1,), (1,)))
    for part in range(2):
        grad_first = grad_first + dot(
            late[:, part * width : (part + 1) * width], weight[1 + part], ((1,), (1,))
        )
    values = features[...].astype(F32)
    factor = norm_factor(values)
    weighted = grad_first * gain[...]
    mean = jnp.mean(values * weighted, axis=-1, keepdims=True)
    grad_features[...] = cotangent[...].astype(F32) + (
        factor * weighted - values * factor**3 * mean
    )


def near_kernel(project, output, summed):
    far = summed.shape[0]
    for source, first_row in ((project, 0), (output, summed.shape[1] - output.shape[1] // far)):
        total = source[0]
        for index in range(1, source.shape[0]):
            total = total + source[index]
        for row in range(source.shape[1] // far):
            summed[:, first_row + row, :] = total[row * far : (row + 1) * far, :]


def far_kernel(scale, parts, grad_project, grad_output):
    total = jnp.sum(parts[...], axis=0) * scale
    lanes = grad_project.shape[1]
    per_row = total.shape[1] // lanes
    project_rows = grad_project.shape[0] // per_row
    for row in range(total.shape[0]):
        for piece in range(per_row):
            values = total[row : row + 1, piece * lanes : (piece + 1) * lanes]
            if row < project_rows:
                grad_project[row * per_row + piece : row * per_row + piece + 1, :] = values
            else:
                at = (row - project_rows) * per_row + piece
                grad_output[at : at + 1, :] = values


def shifted(block, axis, distance):
    size = math.prod(lax.axis_size(name) for name in axis)
    return lax.ppermute(block, axis, [((i - distance) % size, i) for i in range(size)])


def across(block):
    return lax.ppermute(block, "core", [(0, 1), (1, 0)])


def row_order(sizes, width):
    ids = np.arange(math.prod(sizes.values())).reshape([sizes[name] for name in AXES])
    ids = ids[..., 0].transpose(2, 0, 1, 3).reshape(sizes["x"], -1)
    per_project, per_output = 3 * width // (2 * ids.size), width // (2 * ids.size)

    def rows(per):
        return (ids[:, None, :] * per + np.arange(per)[None, :, None]).reshape(-1, 1)

    per_core = np.array([[per_project, per_output]], np.int32)
    return rows(per_project).astype(np.int32), rows(per_output).astype(np.int32), per_core


def body(features, cotangent, gain, weight, output_weight, neighbours, live, send_rows):
    rows, width = features.shape
    cap = send_rows.shape[1]
    sizes = {name: lax.axis_size(name) for name in AXES}
    devices = math.prod(sizes.values())
    scale = float(rows * devices) ** -0.5
    gain = gain.reshape(1, width)
    band = shape(cap, 2 * width)
    first, key_values, *bands = call(
        keys_kernel,
        (shape(rows, width), shape(rows, 2 * width), band, band, band, band),
        (features, gain, weight, send_rows),
        3,
    )
    steps = ((TENSOR, 1), (TENSOR, -1), (CELLS, 1), (CELLS, -1))
    received = [shifted(rows_, *step) for rows_, step in zip(bands, steps)]
    queries, grad_mixed, counts = call(
        queries_kernel,
        (shape(rows, width), shape(rows, width), shape(rows, rows + 4 * cap, dtype=F32)),
        (first, weight, output_weight, cotangent, neighbours, live),
        5,
    )
    sent, own, *backs = call(
        attention_kernel,
        (shape(rows, 4 * width), shape(rows, 2 * width, dtype=F32), band, band, band, band),
        (queries, key_values, *received, grad_mixed, counts, first, cotangent),
        8,
        scratch=(
            pltpu.VMEM((rows + 4 * cap, 2 * width), BF16),
            pltpu.VMEM((rows + 4 * cap, 2 * width), F32),
        ),
    )
    returned = [shifted(rows_, axis, -step) for rows_, (axis, step) in zip(backs, steps)]
    partner = across(sent)
    layer_output = call(
        layer_kernel, shape(rows, width), (features, sent, output_weight), 3
    )
    feature_of, cell_of, per_core = row_order(sizes, width)
    core = lax.axis_index("core").astype(jnp.int32).reshape(1, 1)

    def chosen(core_, per_, *refs):
        sent_, partner_, feature_, cell_, left_, out_ = refs
        chosen_kernel(core_, sent_, partner_, feature_, cell_, per_, left_, out_)

    left, grad_output = call(
        chosen,
        (shape(3 * width // 2, 6 * rows), shape(width // 2, width, dtype=F32)),
        (core, per_core, sent, partner, feature_of, cell_of),
        4,
        scalars=2,
    )
    near = sizes["x"]
    grad_output = lax.all_to_all(
        grad_output.reshape(near, -1, width), "x", 0, 0, tiled=True
    )
    grad_keys_values = call(
        merge_kernel, shape(rows, 2 * width), (own, *returned, send_rows), 2
    )
    partner_grads = across(grad_keys_values)
    grad_project = call(
        project_kernel,
        shape(3 * width // 2, width, dtype=F32),
        (left, sent, partner, grad_keys_values, partner_grads),
        3,
        scratch=(pltpu.VMEM((6 * rows, width), BF16),),
    )
    grad_project = lax.all_to_all(
        grad_project.reshape(near, -1, width), "x", 0, 0, tiled=True
    )
    grad_features = call(
        features_kernel,
        shape(rows, width, dtype=F32),
        (features, cotangent, gain, sent, grad_keys_values, weight),
        3,
    )
    far = devices // (2 * near)
    each = 4 * width // devices
    parts = call(
        near_kernel, shape(far, each, width, dtype=F32), (grad_project, grad_output), 2
    )
    parts = lax.all_to_all(parts, FAR, 0, 0, tiled=True)
    lanes = 128

    def far_sum(*refs):
        far_kernel(scale, *refs)

    grad_project, grad_output = call(
        far_sum,
        (
            shape(3 * width * width // devices // lanes, lanes, dtype=F32),
            shape(width * width // devices // lanes, lanes, dtype=F32),
        ),
        (parts,),
        2,
    )
    return layer_output, grad_features, grad_project.reshape(-1), grad_output.reshape(-1)


def split_mesh(mesh):
    if mesh.devices.size == 512:
        sizes = (2, 8, 4, 4, 2)
    else:
        sizes = (1, 2, mesh.devices.shape[0] // 2, mesh.devices.shape[1] // 2, 2)
    return Mesh(mesh.devices.reshape(sizes), AXES)


def solution(mesh):
    mesh = split_mesh(mesh)
    by_cell = P(AXES, None)
    return jax.shard_map(
        body,
        mesh=mesh,
        in_specs=(by_cell, by_cell, P(), P(), P(), by_cell, by_cell, by_cell),
        out_specs=(by_cell, by_cell, P(AXES), P(AXES)),
        check_vma=False,
    )
```

time: 431 us -> 141 us (0.33)
  the two profiles are of different devices: /device:TPU:24 before, /device:TPU:2 now
where the time goes in v1:
time: 141 us; the launch traced here: 140 us
  starting transfers between devices  58.5 us (41%)
  Pallas kernels  31.8 us (23%)
  blocking collectives  28.3 us (20%)
  waiting for transfers between devices  15.7 us (11%)
  local copies, waits for them, and re-layouts  5.01 us (4%)
    ppermute x8, starting transfers between devices, shifted(): lax.ppermute(block, axis, [((i - distance) % size, i) for i in range(size)])  36.4 us
    pallas_call x10, Pallas kernels, call(): pl.pallas_call(kernel, out_shape=out_shapes, in_specs=specs, out_specs=ja...  31.8 us
    all_to_all x1, blocking collectives, body(): lax.all_to_all(grad_project.reshape(near, -1, width), 'x', 0, 0, tiled=True)  28.3 us
    all_to_all x1, waiting for transfers between devices, body(): parts = lax.all_to_all(parts, FAR, 0, 0, tiled=True)  14.4 us
    all_to_all x1, starting transfers between devices, body(): lax.all_to_all(grad_output.reshape(near, -1, width), 'x', 0, 0, tiled=True)  10.4 us
    all_to_all x1, starting transfers between devices, body(): parts = lax.all_to_all(parts, FAR, 0, 0, tiled=True)  6.76 us
    unnamed x30, local copies, waits for them, and re-layouts  5.01 us
    ppermute x2, starting transfers between devices, across(): return lax.ppermute(block, 'core', [(0, 1), (1, 0)])  4.97 us
  transfers between devices with their start and end apart: 12, of which 2 were waited for; matrix products, arithmetic and copies ran while one was open for 1% of the time, Pallas kernels for 13%

profile of v1, /device:TPU:2, one launch (start us, length us, event | category | flops | bytes accessed | tf_op | source)
XLA Modules:
  0.0 140.2 jit_solution(8408494918100169652)
XLA Ops:
  0.7 2.7 %shard_map.138 = (bf16[128,512]{1,0:T(8,128)(2,1)}, bf16[128,1024]{1,0:T(8,128)(2,1)}, bf16[16,1024]{1,0:T(8,128)(2,1)}, bf16[16,1024]{1,0:T(8,128)(2,1)}, bf16[...) custom-call(bf16[128,512]{1,0:T(8,128)(2,1)} %features.5, f32[1,512]{1,0:T(1,128)} %bitcast.8, bf16[3,512,512]{2,1,0:T(8,128)(2,1)} %weight.5, ...), custom_call_target="tpu_custom_call" | custom-call | flops 1200000000 | bytes 3000000 | tf_op jit(solution)/shard_map/pallas_call | solution.py:35
  3.4 1.9 %collective-permute-start = (bf16[16,1024]{1,0:T(8,128)(2,1)}, bf16[16,1024]{1,0:T(8,128)(2,1)S(1)}, u32[]{:S(2)}, u32[]{:S(2)}) collective-permute-start(bf16[16,1024]{1,0:T(8,128)(2,1)} %get-tuple-element.26), channel_id=1, source_target_pairs={{7,0},{0,1},{1,2},{2,3},{3,4},{4,5},{5,6},{6,7},{15,8},{8,9},{9,10... | collective-permute-start | bytes 98312 | tf_op jit(solution)/shard_map/ppermute | solution.py:240
  5.3 5.4 %collective-permute-start.1 = (bf16[16,1024]{1,0:T(8,128)(2,1)}, bf16[16,1024]{1,0:T(8,128)(2,1)S(1)}, u32[]{:S(2)}, u32[]{:S(2)}) collective-permute-start(bf16[16,1024]{1,0:T(8,128)(2,1)} %get-tuple-element.27), channel_id=1, source_target_pairs={{1,0},{2,1},{3,2},{4,3},{5,4},{6,5},{7,6},{0,7},{9,8},{10,9},{11,1... | collective-permute-start | bytes 98312 | tf_op jit(solution)/shard_map/ppermute | solution.py:240
  10.7 3.4 %collective-permute-start.2 = (bf16[16,1024]{1,0:T(8,128)(2,1)}, bf16[16,1024]{1,0:T(8,128)(2,1)S(1)}, u32[]{:S(2)}, u32[]{:S(2)}) collective-permute-start(bf16[16,1024]{1,0:T(8,128)(2,1)} %get-tuple-element.28), channel_id=1, source_target_pairs={{504,0},{0,8},{8,16},{16,24},{24,32},{32,40},{40,48},{48,56},{56,6... | collective-permute-start | bytes 98312 | tf_op jit(solution)/shard_map/ppermute | solution.py:240
  14.1 6.3 %collective-permute-start.3 = (bf16[16,1024]{1,0:T(8,128)(2,1)}, bf16[16,1024]{1,0:T(8,128)(2,1)S(1)}, u32[]{:S(2)}, u32[]{:S(2)}) collective-permute-start(bf16[16,1024]{1,0:T(8,128)(2,1)} %get-tuple-element.29), channel_id=1, source_target_pairs={{8,0},{16,8},{24,16},{32,24},{40,32},{48,40},{56,48},{64,56},{72,6... | collective-permute-start | bytes 98312 | tf_op jit(solution)/shard_map/ppermute | solution.py:240
  20.5 0.7 copy.15.neighbours
  21.2 0.7 copy.16.live
  21.9 3.7 %shard_map.139 = (bf16[128,512]{1,0:T(8,128)(2,1)}, bf16[128,512]{1,0:T(8,128)(2,1)}, f32[128,192]{1,0:T(8,128)}) custom-call(bf16[128,512]{1,0:T(8,128)(2,1)} %get-tuple-element.23.first, bf16[3,512,512]{2,1,0:T(8,128)(2,1)} %weight.5, bf16[512,512]{1,0:T(8,128)(2,1)} %output_weight.3, bf16[128,512]{1,0:T(8,128)(2,1)} %cotangent.5, ...), custom_call_target="tpu_custom_call" | custom-call | flops 2000000000 | bytes 5000000 | tf_op jit(solution)/shard_map/pallas_call | solution.py:35
  25.7 0.6 copy-done.6
  26.3 6.7 %shard_map.140 = (bf16[128,2048]{1,0:T(8,128)(2,1)}, f32[128,1024]{1,0:T(8,128)}, bf16[16,1024]{1,0:T(8,128)(2,1)}, bf16[16,1024]{1,0:T(8,128)(2,1)}, bf16[16,10...) custom-call(bf16[128,512]{1,0:T(8,128)(2,1)} %get-tuple-element.24.queries, bf16[128,1024]{1,0:T(8,128)(2,1)} %get-tuple-element.25.key_values, ...), custom_call_target="tpu_custom_call" | custom-call | flops 3200000000 | bytes 8000000 | tf_op jit(solution)/shard_map/pallas_call | solution.py:35
  33.0 1.9 %collective-permute-start.8 = (bf16[128,2048]{1,0:T(8,128)(2,1)}, bf16[128,2048]{1,0:T(8,128)(2,1)S(1)}, u32[]{:S(2)}, u32[]{:S(2)}) collective-permute-start(bf16[128,2048]{1,0:T(8,128)(2,1)} %get-tuple-element.32.sent.refs_0_), channel_id=1, source_target_pairs={{0,1},{1,0},{2,3},{3,2},{4,5},{5,4},{6,7},{7,6},{8,9},{9,8},{10,11... | collective-permute-start | bytes 1572872 | tf_op jit(solution)/shard_map/ppermute | solution.py:244
  34.9 1.9 %collective-permute-start.4 = (bf16[16,1024]{1,0:T(8,128)(2,1)}, bf16[16,1024]{1,0:T(8,128)(2,1)S(1)}, u32[]{:S(2)}, u32[]{:S(2)}) collective-permute-start(bf16[16,1024]{1,0:T(8,128)(2,1)} %get-tuple-element.34), channel_id=1, source_target_pairs={{1,0},{2,1},{3,2},{4,3},{5,4},{6,5},{7,6},{0,7},{9,8},{10,9},{11,1... | collective-permute-start | bytes 98312 | tf_op jit(solution)/shard_map/ppermute | solution.py:240
  36.8 2.4 %collective-permute-start.5 = (bf16[16,1024]{1,0:T(8,128)(2,1)}, bf16[16,1024]{1,0:T(8,128)(2,1)S(1)}, u32[]{:S(2)}, u32[]{:S(2)}) collective-permute-start(bf16[16,1024]{1,0:T(8,128)(2,1)} %get-tuple-element.35), channel_id=1, source_target_pairs={{7,0},{0,1},{1,2},{2,3},{3,4},{4,5},{5,6},{6,7},{15,8},{8,9},{9,10... | collective-permute-start | bytes 98312 | tf_op jit(solution)/shard_map/ppermute | solution.py:240
  39.3 13.1 %collective-permute-start.6 = (bf16[16,1024]{1,0:T(8,128)(2,1)}, bf16[16,1024]{1,0:T(8,128)(2,1)S(1)}, u32[]{:S(2)}, u32[]{:S(2)}) collective-permute-start(bf16[16,1024]{1,0:T(8,128)(2,1)} %get-tuple-element.36), channel_id=1, source_target_pairs={{8,0},{16,8},{24,16},{32,24},{40,32},{48,40},{56,48},{64,56},{72,6... | collective-permute-start | bytes 98312 | tf_op jit(solution)/shard_map/ppermute | solution.py:240
  52.3 1.9 %collective-permute-start.7 = (bf16[16,1024]{1,0:T(8,128)(2,1)}, bf16[16,1024]{1,0:T(8,128)(2,1)S(1)}, u32[]{:S(2)}, u32[]{:S(2)}) collective-permute-start(bf16[16,1024]{1,0:T(8,128)(2,1)} %get-tuple-element.37), channel_id=1, source_target_pairs={{504,0},{0,8},{8,16},{16,24},{24,32},{32,40},{40,48},{48,56},{56,6... | collective-permute-start | bytes 98312 | tf_op jit(solution)/shard_map/ppermute | solution.py:240
  54.3 0.8 copy-done.4
  55.0 3.3 %shard_map.144 = (bf16[768,768]{1,0:T(8,128)(2,1)}, f32[256,512]{1,0:T(8,128)}) custom-call(s32[1,1]{1,0:T(1,128)} %bitcast.1.core_, s32[1,2]{1,0:T(1,128)} %constant.10.clone.per_, bf16[128,2048]{1,0:T(8,128)(2,1)} %get-tuple-element.32.sent.refs_0_, bf16[128,2048]{1,0:T(8,128)(2,1)} %copy-done.4, s32[768,1]{1,0:T(8,128)} %constant.11.clone.refs_2_, ...), custom_call_target="tpu_custom_call" | custom-call | flops 1600000000 | bytes 4000000 | tf_op jit(solution)/shard_map/pallas_call | solution.py:35
  58.3 10.4 %all-to-all-start.1 = ((f32[4,64,512]{2,1,0:T(8,128)}), f32[4,64,512]{2,1,0:T(8,128)S(1)}, u32[]{:S(2)}, u32[]{:S(2)}) async-start(f32[4,64,512]{2,1,0:T(8,128)} %bitcast.7), calls=%async_computation.1 | async-start | bytes 1048576 | tf_op jit(solution)/shard_map/all_to_all | solution.py:311
  68.8 0.6 copy-done.7
  69.4 2.2 %shard_map.142.late.own_grads = bf16[128,1024]{1,0:T(8,128)(2,1)} custom-call(f32[128,1024]{1,0:T(8,128)} %get-tuple-element.33.own, bf16[16,1024]{1,0:T(8,128)(2,1)} %copy-done.7, bf16[16,1024]{1,0:T(8,128)(2,1)} %copy-done.9, bf16[16,1024]{1,0:T(8,128)(2,1)} %copy-done.11, bf16[16,1024]{1,0:T(8,128)(2,1)} %copy-done.13, s32[4,16]{1,0:T(4,128)} %send_rows.3), custom_call_target="tpu_custom_call" | custom-call | flops 800000000 | bytes 2000000 | tf_op jit(solution)/shard_map/pallas_call | solution.py:35
  71.6 3.1 %collective-permute-start.9 = (bf16[128,1024]{1,0:T(8,128)(2,1)}, bf16[128,1024]{1,0:T(8,128)(2,1)S(1)}, u32[]{:S(2)}, u32[]{:S(2)}) collective-permute-start(bf16[128,1024]{1,0:T(8,128)(2,1)} %shard_map.142.late.own_grads), channel_id=1, source_target_pairs={{0,1},{1,0},{2,3},{3,2},{4,5},{5,4},{6,7},{7,6},{8,9},{9,8},{10,11... | collective-permute-start | bytes 786440 | tf_op jit(solution)/shard_map/ppermute | solution.py:244
  74.7 1.4 collective-permute-done.9.partner_grads
  76.1 0.7 copy-done.5
  76.8 3.7 %shard_map.145 = f32[768,512]{1,0:T(8,128)} custom-call(bf16[768,768]{1,0:T(8,128)(2,1)} %get-tuple-element.38.left, bf16[128,2048]{1,0:T(8,128)(2,1)} %get-tuple-element.32.sent.refs_0_, bf16[128,2048]{1,0:T(8,128)(2,1)} %copy-done.4, bf16[128,1024]{1,0:T(8,128)(2,1)} %shard_map.142.late.own_grads, bf16[128,1024]{1,0:T(8,128)(2,1)} %copy-done.5), custom_call_target="tpu_custom_call" | custom-call | flops 1200000000 | bytes 3000000 | tf_op jit(solution)/shard_map/pallas_call | solution.py:35
  80.4 28.3 %all_to_all.15.project = f32[4,192,512]{2,1,0:T(8,128)} all-to-all(f32[4,192,512]{2,1,0:T(8,128)} %bitcast.6), channel_id=1, replica_groups=mesh['yh'=2,'z'=8,'x'=4,'yl'=4,'core'=2] {'x'}, dimensions={0} | all-to-all | bytes 3145728 | tf_op jit(solution)/shard_map/all_to_all | solution.py:325
  108.7 2.5 %shard_map.146 = f32[64,4,512]{2,1,0:T(4,128)} custom-call(f32[4,192,512]{2,1,0:T(8,128)} %all_to_all.15.project, f32[4,64,512]{2,1,0:T(8,128)} %copy-done), custom_call_target="tpu_custom_call" | custom-call | flops 800000000 | bytes 2000000 | tf_op jit(solution)/shard_map/pallas_call | solution.py:35
  111.2 6.8 %all-to-all-start.2 = ((f32[64,4,512]{2,1,0:T(4,128)}), f32[64,4,512]{2,1,0:T(4,128)S(1)}, u32[]{:S(2)}, u32[]{:S(2)}) async-start(f32[64,4,512]{2,1,0:T(4,128)} %shard_map.146), calls=%async_computation.2 | async-start | bytes 1048576 | tf_op jit(solution)/shard_map/all_to_all | solution.py:339
  118.0 2.1 %shard_map.141 = bf16[128,512]{1,0:T(8,128)(2,1)} custom-call(bf16[128,512]{1,0:T(8,128)(2,1)} %features.5, bf16[128,2048]{1,0:T(8,128)(2,1)} %get-tuple-element.32.sent.refs_0_, bf16[512,512]{1,0:T(8,128)(2,1)} %output_weight.3), custom_call_target="tpu_custom_call" | custom-call | flops 1200000000 | bytes 3000000 | tf_op jit(solution)/shard_map/pallas_call | solution.py:35
  120.1 3.2 %shard_map.143 = f32[128,512]{1,0:T(8,128)} custom-call(bf16[128,512]{1,0:T(8,128)(2,1)} %features.5, bf16[128,512]{1,0:T(8,128)(2,1)} %cotangent.5, f32[1,512]{1,0:T(1,128)} %bitcast.9, bf16[128,2048]{1,0:T(8,128)(2,1)} %get-tuple-element.32.sent.refs_0_, bf16[128,1024]{1,0:T(8,128)(2,1)} %shard_map.142.late.own_grads, bf16[3,512,512]{2,1,0:T(8,128)(2,1)} %weight.5), custom_call_target="tpu_custom_call" | custom-call | flops 1200000000 | bytes 3000000 | tf_op jit(solution)/shard_map/pallas_call | solution.py:35
  123.3 14.4 %all-to-all-done.2.refs_0_ = f32[64,4,512]{2,1,0:T(4,128)S(1)} async-done(((f32[64,4,512]{2,1,0:T(4,128)}), f32[64,4,512]{2,1,0:T(4,128)S(1)}, u32[]{:S(2)}, u32[]{:S(2)}) %all-to-all-start.2) | async-done | bytes 524320 | tf_op jit(solution)/shard_map/all_to_all | solution.py:339
  137.7 0.8 copy-done.1
  138.5 1.8 %shard_map.147 = (f32[12,128]{1,0:T(8,128)}, f32[4,128]{1,0:T(4,128)}) custom-call(f32[64,4,512]{2,1,0:T(4,128)} %copy-done.1), custom_call_target="tpu_custom_call" | custom-call | flops 800000000 | bytes 2000000 | tf_op jit(solution)/shard_map/pallas_call | solution.py:35
  (33 shorter events, 0.2 us)
Async XLA Ops:
  0.6 19.8 %copy-start.2 = (s32[128,64]{0,1:T(8,128)S(1)}, s32[128,64]{0,1:T(8,128)}, u32[]{:S(2)}) copy-start(s32[128,64]{0,1:T(8,128)} %param.16) | copy-start | bytes 98308
  0.6 20.6 %copy-start.3 = (s32[128,64]{0,1:T(8,128)S(1)}, s32[128,64]{0,1:T(8,128)}, u32[]{:S(2)}) copy-start(s32[128,64]{0,1:T(8,128)} %param.17) | copy-start | bytes 98308
  3.4 22.3 %collective-permute-start = (bf16[16,1024]{1,0:T(8,128)(2,1)}, bf16[16,1024]{1,0:T(8,128)(2,1)S(1)}, u32[]{:S(2)}, u32[]{:S(2)}) collective-permute-start(bf16[16,1024]{1,0:T(8,128)(2,1)} %get-tuple-element.26), channel_id=1, source_target_pairs={{7,0},{0,1},{1,2},{2,3},{3,4},{4,5},{5,6},{6,7},{15,8},{8,9},{9,10... | collective-permute-start | bytes 98312 | tf_op jit(solution)/shard_map/ppermute | solution.py:240
  5.3 20.4 %collective-permute-start.1 = (bf16[16,1024]{1,0:T(8,128)(2,1)}, bf16[16,1024]{1,0:T(8,128)(2,1)S(1)}, u32[]{:S(2)}, u32[]{:S(2)}) collective-permute-start(bf16[16,1024]{1,0:T(8,128)(2,1)} %get-tuple-element.27), channel_id=1, source_target_pairs={{1,0},{2,1},{3,2},{4,3},{5,4},{6,5},{7,6},{0,7},{9,8},{10,9},{11,1... | collective-permute-start | bytes 98312 | tf_op jit(solution)/shard_map/ppermute | solution.py:240
  10.7 14.9 %collective-permute-start.2 = (bf16[16,1024]{1,0:T(8,128)(2,1)}, bf16[16,1024]{1,0:T(8,128)(2,1)S(1)}, u32[]{:S(2)}, u32[]{:S(2)}) collective-permute-start(bf16[16,1024]{1,0:T(8,128)(2,1)} %get-tuple-element.28), channel_id=1, source_target_pairs={{504,0},{0,8},{8,16},{16,24},{24,32},{32,40},{40,48},{48,56},{56,6... | collective-permute-start | bytes 98312 | tf_op jit(solution)/shard_map/ppermute | solution.py:240
  14.1 11.5 %collective-permute-start.3 = (bf16[16,1024]{1,0:T(8,128)(2,1)}, bf16[16,1024]{1,0:T(8,128)(2,1)S(1)}, u32[]{:S(2)}, u32[]{:S(2)}) collective-permute-start(bf16[16,1024]{1,0:T(8,128)(2,1)} %get-tuple-element.29), channel_id=1, source_target_pairs={{8,0},{16,8},{24,16},{32,24},{40,32},{48,40},{56,48},{64,56},{72,6... | collective-permute-start | bytes 98312 | tf_op jit(solution)/shard_map/ppermute | solution.py:240
  25.6 0.6 copy-start.6
  25.6 0.6 copy-start.8
  25.7 0.6 copy-start.10
  25.7 0.6 copy-start.12
  33.0 21.3 %collective-permute-start.8 = (bf16[128,2048]{1,0:T(8,128)(2,1)}, bf16[128,2048]{1,0:T(8,128)(2,1)S(1)}, u32[]{:S(2)}, u32[]{:S(2)}) collective-permute-start(bf16[128,2048]{1,0:T(8,128)(2,1)} %get-tuple-element.32.sent.refs_0_), channel_id=1, source_target_pairs={{0,1},{1,0},{2,3},{3,2},{4,5},{5,4},{6,7},{7,6},{8,9},{9,8},{10,11... | collective-permute-start | bytes 1572872 | tf_op jit(solution)/shard_map/ppermute | solution.py:244
  34.9 33.8 %collective-permute-start.4 = (bf16[16,1024]{1,0:T(8,128)(2,1)}, bf16[16,1024]{1,0:T(8,128)(2,1)S(1)}, u32[]{:S(2)}, u32[]{:S(2)}) collective-permute-start(bf16[16,1024]{1,0:T(8,128)(2,1)} %get-tuple-element.34), channel_id=1, source_target_pairs={{1,0},{2,1},{3,2},{4,3},{5,4},{6,5},{7,6},{0,7},{9,8},{10,9},{11,1... | collective-permute-start | bytes 98312 | tf_op jit(solution)/shard_map/ppermute | solution.py:240
  36.8 31.9 %collective-permute-start.5 = (bf16[16,1024]{1,0:T(8,128)(2,1)}, bf16[16,1024]{1,0:T(8,128)(2,1)S(1)}, u32[]{:S(2)}, u32[]{:S(2)}) collective-permute-start(bf16[16,1024]{1,0:T(8,128)(2,1)} %get-tuple-element.35), channel_id=1, source_target_pairs={{7,0},{0,1},{1,2},{2,3},{3,4},{4,5},{5,6},{6,7},{15,8},{8,9},{9,10... | collective-permute-start | bytes 98312 | tf_op jit(solution)/shard_map/ppermute | solution.py:240
  39.3 29.5 %collective-permute-start.6 = (bf16[16,1024]{1,0:T(8,128)(2,1)}, bf16[16,1024]{1,0:T(8,128)(2,1)S(1)}, u32[]{:S(2)}, u32[]{:S(2)}) collective-permute-start(bf16[16,1024]{1,0:T(8,128)(2,1)} %get-tuple-element.36), channel_id=1, source_target_pairs={{8,0},{16,8},{24,16},{32,24},{40,32},{48,40},{56,48},{64,56},{72,6... | collective-permute-start | bytes 98312 | tf_op jit(solution)/shard_map/ppermute | solution.py:240
  52.3 16.5 %collective-permute-start.7 = (bf16[16,1024]{1,0:T(8,128)(2,1)}, bf16[16,1024]{1,0:T(8,128)(2,1)S(1)}, u32[]{:S(2)}, u32[]{:S(2)}) collective-permute-start(bf16[16,1024]{1,0:T(8,128)(2,1)} %get-tuple-element.37), channel_id=1, source_target_pairs={{504,0},{0,8},{8,16},{16,24},{24,32},{32,40},{40,48},{48,56},{56,6... | collective-permute-start | bytes 98312 | tf_op jit(solution)/shard_map/ppermute | solution.py:240
  54.3 0.8 copy-start.4
  58.3 22.1 %all-to-all-start.1 = ((f32[4,64,512]{2,1,0:T(8,128)}), f32[4,64,512]{2,1,0:T(8,128)S(1)}, u32[]{:S(2)}, u32[]{:S(2)}) async-start(f32[4,64,512]{2,1,0:T(8,128)} %bitcast.7), calls=%async_computation.1 | async-start | bytes 1048576 | tf_op jit(solution)/shard_map/all_to_all | solution.py:311
  68.8 0.6 copy-start.7
  68.8 0.6 copy-start.9
  68.8 0.6 copy-start.11
  68.8 0.6 copy-start.13
  71.6 4.4 %collective-permute-start.9 = (bf16[128,1024]{1,0:T(8,128)(2,1)}, bf16[128,1024]{1,0:T(8,128)(2,1)S(1)}, u32[]{:S(2)}, u32[]{:S(2)}) collective-permute-start(bf16[128,1024]{1,0:T(8,128)(2,1)} %shard_map.142.late.own_grads), channel_id=1, source_target_pairs={{0,1},{1,0},{2,3},{3,2},{4,5},{5,4},{6,7},{7,6},{8,9},{9,8},{10,11... | collective-permute-start | bytes 786440 | tf_op jit(solution)/shard_map/ppermute | solution.py:244
  76.1 0.7 copy-start.5
  80.4 28.3 %copy-start = (f32[4,64,512]{2,1,0:T(8,128)}, f32[4,64,512]{2,1,0:T(8,128)S(1)}, u32[]{:S(2)}) copy-start(f32[4,64,512]{2,1,0:T(8,128)S(1)} %all-to-all-done.1.output) | copy-start | bytes 1572868
  111.2 26.5 %all-to-all-start.2 = ((f32[64,4,512]{2,1,0:T(4,128)}), f32[64,4,512]{2,1,0:T(4,128)S(1)}, u32[]{:S(2)}, u32[]{:S(2)}) async-start(f32[64,4,512]{2,1,0:T(4,128)} %shard_map.146), calls=%async_computation.2 | async-start | bytes 1048576 | tf_op jit(solution)/shard_map/all_to_all | solution.py:339
  137.7 0.8 copy-start.1

commit v2 on v1

v2 whole, which is shorter than its diff:
```python
import math

import jax
import jax.numpy as jnp
import numpy as np
from jax import lax
from jax.experimental import pallas as pl
from jax.experimental.pallas import tpu as pltpu
from jax.sharding import Mesh
from jax.sharding import PartitionSpec as P

HEADS = 8
HEAD_DIM = 64
EPSILON = 1e-06
VMEM_BYTES = 16 * 1024 * 1024
F32 = jnp.float32
BF16 = jnp.bfloat16
AXES = ("yh", "z", "x", "yl", "core")
CELLS = ("yh", "z", "x")
TENSOR = ("yl", "core")
FAR = ("yh", "z", "yl")


def dot(a, b, dims=((1,), (0,))):
    return lax.dot_general(a, b, (dims, ((), ())), preferred_element_type=F32)


def split(values):
    high = values.astype(BF16)
    return high, (values - high.astype(F32)).astype(BF16)


def call(kernel, out_shapes, args, us, scalars=0, moved=0, scratch=()):
    held = len(args) - moved
    specs = [pl.BlockSpec(memory_space=pltpu.SMEM)] * scalars
    specs += [pl.BlockSpec(memory_space=pltpu.VMEM)] * (held - scalars)
    specs += [pl.BlockSpec(memory_space=pl.ANY)] * moved
    scratch = list(scratch)
    if moved:
        scratch += [pltpu.VMEM(arg.shape, arg.dtype) for arg in args[held:]]
        scratch.append(pltpu.SemaphoreType.DMA((moved,)))

    def moving(*refs):
        away, local, arrived = refs[held : len(args)], refs[-1 - moved : -1], refs[-1]
        copies = [
            pltpu.make_async_copy(away[index], local[index], arrived.at[index])
            for index in range(moved)
        ]
        for copy in copies:
            copy.start()
        for copy in copies:
            copy.wait()
        kernel(*refs[:held], *local, *refs[len(args) : -1 - moved])

    return pl.pallas_call(
        moving if moved else kernel,
        out_shape=out_shapes,
        in_specs=specs,
        out_specs=jax.tree.map(lambda _: pl.BlockSpec(memory_space=pltpu.VMEM), out_shapes),
        scratch_shapes=scratch,
        compiler_params=pltpu.CompilerParams(vmem_limit_bytes=VMEM_BYTES),
        cost_estimate=pl.CostEstimate(
            flops=int(us * 4e8), bytes_accessed=int(us * 1e6), transcendentals=0
        ),
    )(*args)


def shape(*dims, dtype=BF16):
    return jax.ShapeDtypeStruct(dims, dtype)


def norm_factor(values):
    return lax.rsqrt(jnp.mean(values * values, axis=-1, keepdims=True) + EPSILON)


def listed(places, send_rows, index, rows):
    first = 2 * (index // 2)
    at_even, at_odd = first + index % 2, first + 1 - index % 2
    chosen = jnp.where(
        places[0, index // 2] == 0,
        send_rows[at_even : at_even + 1, :],
        send_rows[at_odd : at_odd + 1, :],
    )
    row_ids = lax.broadcasted_iota(jnp.int32, (rows, send_rows.shape[1]), 0)
    return (row_ids == chosen).astype(F32).astype(BF16)


def keys_kernel(places, features, gain, weight, send_rows, first, key_values, *bands):
    values = features[...].astype(F32)
    normed = (values * norm_factor(values) * gain[...]).astype(BF16)
    first[...] = normed
    width = weight.shape[2]
    for part in range(2):
        key_values[:, part * width : (part + 1) * width] = dot(normed, weight[1 + part]).astype(
            BF16
        )
    table = key_values[...]
    for index in range(4):
        chosen = listed(places, send_rows, index, features.shape[0])
        bands[index][...] = dot(chosen, table, ((0,), (0,))).astype(BF16)


def queries_kernel(
    places, first, weight, output_weight, cotangent, neighbours, live, queries, grad_mixed, counts
):
    queries[...] = dot(first[...], weight[0]).astype(BF16)
    grad_mixed[...] = dot(cotangent[...], output_weight[...], ((1,), (1,))).astype(BF16)
    slots = jnp.where(live[...] > 0, neighbours[...], -1)
    rows = slots.shape[1]
    cap = (counts.shape[0] - rows) // 4
    entries = lax.broadcasted_iota(jnp.int32, counts.shape, 0)
    swapped = jnp.where(
        entries < rows,
        0,
        jnp.where(entries < rows + 2 * cap, 1 - places[0, 0], 1 - places[0, 1]),
    )
    entries = jnp.bitwise_xor(entries, swapped * cap)
    total = jnp.zeros(entries.shape, F32)
    for slot in range(slots.shape[0]):
        total = total + jnp.where(slots[slot : slot + 1, :] == entries, 1.0, 0.0)
    counts[...] = total


def attention_kernel(
    queries, key_values, grad_mixed, counts, first, cotangent, band3, band1, band2, band0,
    sent, own, back1, back2, back3, table, grads,
):
    rows, width = queries.shape
    cap = band0.shape[0]
    table[:rows, :] = key_values[...]
    for index, band in enumerate((band0, band1, band2, band3)):
        start = rows + index * cap
        table[start : start + cap, :] = band[...]
    factor = HEAD_DIM**-0.5
    count = counts[...]
    is_live = count > 0
    wide = 2 * HEAD_DIM
    side = lax.broadcasted_iota(jnp.int32, (1, wide), 1) // HEAD_DIM
    down = ((0,), (0,))
    for pair in range(HEADS // 2):
        lanes = slice(pair * wide, (pair + 1) * wide)
        value_lanes = slice(width + pair * wide, width + (pair + 1) * wide)
        query, upstream = queries[:, lanes], grad_mixed[:, lanes]
        key, value = table[:, lanes], table[:, value_lanes]
        zero = jnp.zeros((), BF16)
        mixed, grad_query, grad_key, grad_value = [], [], None, None
        for half in range(2):
            mine = side == half
            query_half = jnp.where(mine, query, zero)
            upstream_half = jnp.where(mine, upstream, zero)
            scores = dot(key, query_half, ((1,), (1,))) * factor
            grad_probs = dot(value, upstream_half, ((1,), (1,)))
            scores = jnp.where(is_live, scores, -1e30)
            row_max = jnp.max(scores, axis=0, keepdims=True)
            powers = jnp.where(is_live, jnp.exp(scores - row_max), 0.0)
            probabilities = powers / jnp.sum(count * powers, axis=0, keepdims=True)
            weights = split(count * probabilities.astype(BF16).astype(F32))
            spread = count * probabilities
            grad_scores = spread * (
                grad_probs - jnp.sum(spread * grad_probs, axis=0, keepdims=True)
            )
            grad_scores = split(grad_scores * factor)
            mixed.append(sum(dot(w, value, down) for w in weights))
            grad_query.append(sum(dot(g, key, down) for g in grad_scores))
            grad_k = sum(dot(g, query_half) for g in grad_scores)
            grad_v = sum(dot(w, upstream_half) for w in weights)
            grad_key = grad_k if half == 0 else grad_key + grad_k
            grad_value = grad_v if half == 0 else grad_value + grad_v
        sent[rows : 2 * rows, lanes] = jnp.where(side == 0, mixed[0], mixed[1]).astype(BF16)
        sent[rows : 2 * rows, value_lanes] = jnp.where(
            side == 0, grad_query[0], grad_query[1]
        ).astype(BF16)
        grads[:, lanes] = grad_key
        grads[:, value_lanes] = grad_value
    own[...] = grads[:rows, :]
    sent[2 * rows :, :] = grads[rows : rows + cap, :].astype(BF16)
    for index, back in enumerate((back1, back2, back3)):
        start = rows + (index + 1) * cap
        back[...] = grads[start : start + cap, :].astype(BF16)
    sent[:rows, :width] = first[...]
    sent[:rows, width:] = cotangent[...]


def layer_kernel(features, sent, output_weight, layer_output):
    rows, width = features.shape
    mixed = sent[rows : 2 * rows, :width]
    layer_output[...] = (features[...].astype(F32) + dot(mixed, output_weight[...])).astype(BF16)


def chosen_kernel(places, per_core, sent, feature_of, cell_of, partner, left, grad_output):
    width = grad_output.shape[1]
    rows = left.shape[1] // 6
    offset = places[0, 0]
    columns = lax.broadcasted_iota(jnp.int32, (feature_of.shape[0], width), 1)
    target = feature_of[...] + offset * per_core[0, 0]
    feature = jnp.bitwise_and(target, width - 1)
    chosen = (feature == columns).astype(F32).astype(BF16)
    part = jnp.right_shift(target, width.bit_length() - 1)
    for index, source in enumerate((sent, partner)):
        picked = dot(chosen, source[:rows, :width], ((1,), (1,)))
        for piece in range(3):
            at = (2 * piece + index) * rows
            left[:, at : at + rows] = jnp.where(part == piece, picked, 0.0).astype(BF16)
    columns = lax.broadcasted_iota(jnp.int32, (cell_of.shape[0], width), 1)
    chosen = (cell_of[...] + offset * per_core[0, 1] == columns).astype(F32).astype(BF16)
    total = None
    for source in (sent, partner):
        picked = dot(chosen, source[:rows, width:], ((1,), (1,))).astype(BF16)
        product = dot(picked, source[rows : 2 * rows, :width])
        total = product if total is None else total + product
    grad_output[...] = total


def merge_kernel(places, own, send_rows, back3, back1, back2, partner, grad_keys_values):
    rows = own.shape[0]
    total = own[...]
    for index, back in enumerate((partner[2 * rows :, :], back1, back2, back3)):
        total = total + dot(listed(places, send_rows, index, rows), back[...])
    grad_keys_values[...] = total.astype(BF16)


def project_kernel(left, sent, own_grads, partner, partner_grads, grad_project, right):
    rows, width = own_grads.shape[0], grad_project.shape[1]
    for index, (early, late) in enumerate(((sent, own_grads), (partner, partner_grads))):
        pieces = (
            early[rows : 2 * rows, width:],
            late[:, :width],
            late[:, width:],
        )
        for piece in range(3):
            at = (2 * piece + index) * rows
            right[at : at + rows, :] = pieces[piece]
    grad_project[...] = dot(left[...], right[...])


def features_kernel(features, cotangent, gain, sent, late, weight, grad_features):
    rows, width = features.shape
    grad_first = dot(sent[rows : 2 * rows, width:], weight[0], ((1,), (1,)))
    for part in range(2):
        grad_first = grad_first + dot(
            late[:, part * width : (part + 1) * width], weight[1 + part], ((1,), (1,))
        )
    values = features[...].astype(F32)
    factor = norm_factor(values)
    weighted = grad_first * gain[...]
    mean = jnp.mean(values * weighted, axis=-1, keepdims=True)
    grad_features[...] = cotangent[...].astype(F32) + (
        factor * weighted - values * factor**3 * mean
    )


def near_kernel(project, output, summed):
    far = summed.shape[0]
    for source, first_row in ((project, 0), (output, summed.shape[1] - output.shape[1] // far)):
        total = source[0]
        for index in range(1, source.shape[0]):
            total = total + source[index]
        for row in range(source.shape[1] // far):
            summed[:, first_row + row, :] = total[row * far : (row + 1) * far, :]


def far_kernel(scale, parts, grad_project, grad_output):
    total = jnp.sum(parts[...], axis=0) * scale
    lanes = grad_project.shape[1]
    per_row = total.shape[1] // lanes
    project_rows = grad_project.shape[0] // per_row
    for row in range(total.shape[0]):
        for piece in range(per_row):
            values = total[row : row + 1, piece * lanes : (piece + 1) * lanes]
            if row < project_rows:
                grad_project[row * per_row + piece : row * per_row + piece + 1, :] = values
            else:
                at = (row - project_rows) * per_row + piece
                grad_output[at : at + 1, :] = values


def exchanged(block, axis, index):
    size = math.prod(lax.axis_size(name) for name in axis)
    partners = [i ^ 1 if index == 0 else ((i - 1) ^ 1) + 1 for i in range(size)]
    return lax.ppermute(block, axis, [(i, partner % size) for i, partner in enumerate(partners)])


def row_order(sizes, width):
    ids = np.arange(math.prod(sizes.values())).reshape([sizes[name] for name in AXES])
    ids = ids[..., 0].transpose(2, 0, 1, 3).reshape(sizes["x"], -1)
    per_project, per_output = 3 * width // (2 * ids.size), width // (2 * ids.size)

    def rows(per):
        return (ids[:, None, :] * per + np.arange(per)[None, :, None]).reshape(-1, 1)

    per_core = np.array([[per_project, per_output]], np.int32)
    return rows(per_project).astype(np.int32), rows(per_output).astype(np.int32), per_core


def body(features, cotangent, gain, weight, output_weight, neighbours, live, send_rows):
    rows, width = features.shape
    cap = send_rows.shape[1]
    sizes = {name: lax.axis_size(name) for name in AXES}
    devices = math.prod(sizes.values())
    scale = float(rows * devices) ** -0.5
    gain = gain.reshape(1, width)
    core = lax.axis_index("core")
    places = jnp.stack([core, lax.axis_index("x") % 2]).astype(jnp.int32).reshape(1, 2)
    band = shape(cap, 2 * width)
    first, key_values, *bands = call(
        keys_kernel,
        (shape(rows, width), shape(rows, 2 * width), band, band, band, band),
        (places, features, gain, weight, send_rows),
        3,
        scalars=1,
    )
    steps = ((TENSOR, 0), (TENSOR, 1), (CELLS, 0), (CELLS, 1))
    received = [exchanged(bands[index], *steps[index]) for index in (3, 1, 2, 0)]
    queries, grad_mixed, counts = call(
        queries_kernel,
        (shape(rows, width), shape(rows, width), shape(rows + 4 * cap, rows, dtype=F32)),
        (places, first, weight, output_weight, cotangent, neighbours.T, live.T),
        5,
        scalars=1,
    )
    sent, own, *backs = call(
        attention_kernel,
        (
            shape(2 * rows + cap, 2 * width),
            shape(rows, 2 * width, dtype=F32),
            band,
            band,
            band,
        ),
        (queries, key_values, grad_mixed, counts, first, cotangent, *received),
        8,
        moved=4,
        scratch=(
            pltpu.VMEM((rows + 4 * cap, 2 * width), BF16),
            pltpu.VMEM((rows + 4 * cap, 2 * width), F32),
        ),
    )
    returned = [exchanged(backs[index - 1], *steps[index]) for index in (3, 1, 2)]
    partner = exchanged(sent, *steps[0])
    layer_output = call(
        layer_kernel, shape(rows, width), (features, sent, output_weight), 3
    )
    feature_of, cell_of, per_core = row_order(sizes, width)
    left, grad_output = call(
        chosen_kernel,
        (shape(3 * width // 2, 6 * rows), shape(width // 2, width, dtype=F32)),
        (places, per_core, sent, feature_of, cell_of, partner),
        4,
        scalars=2,
        moved=1,
    )
    near = sizes["x"]
    grad_output = lax.all_to_all(
        grad_output.reshape(near, -1, width), "x", 0, 0, tiled=True
    )
    grad_keys_values = call(
        merge_kernel,
        shape(rows, 2 * width),
        (places, own, send_rows, *returned, partner),
        2,
        scalars=1,
        moved=4,
    )
    partner_grads = exchanged(grad_keys_values, *steps[0])
    grad_project = call(
        project_kernel,
        shape(3 * width // 2, width, dtype=F32),
        (left, sent, grad_keys_values, partner, partner_grads),
        3,
        moved=2,
        scratch=(pltpu.VMEM((6 * rows, width), BF16),),
    )
    grad_project = lax.all_to_all(
        grad_project.reshape(near, -1, width), "x", 0, 0, tiled=True
    )
    grad_features = call(
        features_kernel,
        shape(rows, width, dtype=F32),
        (features, cotangent, gain, sent, grad_keys_values, weight),
        3,
    )
    far = devices // (2 * near)
    each = 4 * width // devices
    parts = call(
        near_kernel, shape(far, each, width, dtype=F32), (grad_project, grad_output), 2, moved=2
    )
    parts = lax.all_to_all(parts, FAR, 0, 0, tiled=True)
    lanes = 128

    def far_sum(*refs):
        far_kernel(scale, *refs)

    grad_project, grad_output = call(
        far_sum,
        (
            shape(3 * width * width // devices // lanes, lanes, dtype=F32),
            shape(width * width // devices // lanes, lanes, dtype=F32),
        ),
        (parts,),
        2,
        moved=1,
    )
    return layer_output, grad_features, grad_project.reshape(-1), grad_output.reshape(-1)


def split_mesh(mesh):
    if mesh.devices.size == 512:
        sizes = (2, 8, 4, 4, 2)
    else:
        sizes = (1, 2, mesh.devices.shape[0] // 2, mesh.devices.shape[1] // 2, 2)
    return Mesh(mesh.devices.reshape(sizes), AXES)


def solution(mesh):
    mesh = split_mesh(mesh)
    by_cell = P(AXES, None)
    return jax.shard_map(
        body,
        mesh=mesh,
        in_specs=(by_cell, by_cell, P(), P(), P(), by_cell, by_cell, by_cell),
        out_specs=(by_cell, by_cell, P(AXES), P(AXES)),
        check_vma=False,
    )
```

time: 141 us -> 118 us (0.84)
  Pallas kernels: 31.8 us -> 15.5 us
  blocking collectives: 28.3 us -> 22.4 us
  starting transfers between devices: 58.5 us -> 53 us
  waiting for transfers between devices: 15.7 us -> 20.6 us
    pallas_call x10, Pallas kernels: 31.8 us -> 15.5 us  [call(): pl.pallas_call(moving if moved else kernel, out_shape=out_shapes, in_spec...]
    all_to_all x1, starting transfers between devices: 10.4 us -> 3.85 us  [body(): lax.all_to_all(grad_output.reshape(near, -1, width), 'x', 0, 0, tiled=True)]
    all_to_all x1, blocking collectives: 28.3 us -> 22.4 us  [body(): lax.all_to_all(grad_project.reshape(near, -1, width), 'x', 0, 0, tiled=True)]
    all_to_all x1, starting transfers between devices: 6.76 us -> 9.39 us  [body(): parts = lax.all_to_all(parts, FAR, 0, 0, tiled=True)]
    all_to_all x1, waiting for transfers between devices: 0.01 us -> 2.52 us  [body(): lax.all_to_all(grad_output.reshape(near, -1, width), 'x', 0, 0, tiled=True)]
    all_to_all x1, waiting for transfers between devices: 14.4 us -> 16.5 us  [body(): parts = lax.all_to_all(parts, FAR, 0, 0, tiled=True)]
    ppermute x10 -> x9, starting transfers between devices: 41.3 us -> 39.8 us  [exchanged(): lax.ppermute(block, axis, [(i, partner % size) for i, partner in enumerat...]
    unnamed x30 -> x40, local copies, waits for them, and re-layouts: 5.01 us -> 5.31 us
  transfers between devices with their start and end apart: 12 -> 11, of which waited for: 2 -> 3; matrix products, arithmetic and copies ran while one was open for 1% -> 0% of each run, Pallas kernels for 13% -> 7%
where the time goes in v2:
time: 118 us
  starting transfers between devices  53 us (45%)
  blocking collectives  22.4 us (19%)
  waiting for transfers between devices  20.6 us (17%)
  Pallas kernels  15.5 us (13%)
  local copies, waits for them, and re-layouts  5.31 us (4%)
    ppermute x9, starting transfers between devices, exchanged(): lax.ppermute(block, axis, [(i, partner % size) for i, partner in enumerat...  39.8 us
    all_to_all x1, blocking collectives, body(): lax.all_to_all(grad_project.reshape(near, -1, width), 'x', 0, 0, tiled=True)  22.4 us
    all_to_all x1, waiting for transfers between devices, body(): parts = lax.all_to_all(parts, FAR, 0, 0, tiled=True)  16.5 us
    pallas_call x10, Pallas kernels, call(): pl.pallas_call(moving if moved else kernel, out_shape=out_shapes, in_spec...  15.5 us
    all_to_all x1, starting transfers between devices, body(): parts = lax.all_to_all(parts, FAR, 0, 0, tiled=True)  9.39 us
    unnamed x40, local copies, waits for them, and re-layouts  5.31 us
    all_to_all x1, starting transfers between devices, body(): lax.all_to_all(grad_output.reshape(near, -1, width), 'x', 0, 0, tiled=True)  3.85 us
    all_to_all x1, waiting for transfers between devices, body(): lax.all_to_all(grad_output.reshape(near, -1, width), 'x', 0, 0, tiled=True)  2.52 us
  transfers between devices with their start and end apart: 11, of which 3 were waited for; matrix products, arithmetic and copies ran while one was open for 0% of the time, Pallas kernels for 7%

profile of v2, /device:TPU:2, one launch (start us, length us, event | category | flops | bytes accessed | tf_op | source)
XLA Modules:
  0.0 117.8 jit_solution(14367371196547089523)
XLA Ops:
  0.6 0.1 add_bitcast_fusion.places.refs_0_
  0.7 1.4 %copy-done = bf16[3,512,512]{2,1,0:T(8,128)(2,1)S(1)} copy-done((bf16[3,512,512]{2,1,0:T(8,128)(2,1)S(1)}, bf16[3,512,512]{2,1,0:T(8,128)(2,1)}, u32[]{:S(2)}) %copy-start) | copy-done | bytes 1572888
  2.1 0.9 copy-done.5
  3.0 0.7 copy-done.11
  3.7 0.7 copy-done.13
  4.4 1.1 shard_map.138
  5.5 3.4 %collective-permute-start = (bf16[16,1024]{1,0:T(8,128)(2,1)S(1)}, bf16[16,1024]{1,0:T(8,128)(2,1)S(1)}, u32[]{:S(2)}, u32[]{:S(2)}) collective-permute-start(bf16[16,1024]{1,0:T(8,128)(2,1)S(1)} %get-tuple-element.27), channel_id=1, source_target_pairs={{0,504},{8,16},{16,8},{24,32},{32,24},{40,48},{48,40},{56,64},{64,... | collective-permute-start | bytes 98312 | tf_op jit(solution)/shard_map/ppermute | solution.py:280
  9.0 4.7 %collective-permute-start.1 = (bf16[16,1024]{1,0:T(8,128)(2,1)S(1)}, bf16[16,1024]{1,0:T(8,128)(2,1)S(1)}, u32[]{:S(2)}, u32[]{:S(2)}) collective-permute-start(bf16[16,1024]{1,0:T(8,128)(2,1)S(1)} %get-tuple-element.28), channel_id=1, source_target_pairs={{0,7},{1,2},{2,1},{3,4},{4,3},{5,6},{6,5},{7,0},{8,15},{9,10},{10,... | collective-permute-start | bytes 98312 | tf_op jit(solution)/shard_map/ppermute | solution.py:280
  13.6 14.8 %collective-permute-start.2 = (bf16[16,1024]{1,0:T(8,128)(2,1)S(1)}, bf16[16,1024]{1,0:T(8,128)(2,1)S(1)}, u32[]{:S(2)}, u32[]{:S(2)}) collective-permute-start(bf16[16,1024]{1,0:T(8,128)(2,1)S(1)} %get-tuple-element.29), channel_id=1, source_target_pairs={{0,8},{8,0},{16,24},{24,16},{32,40},{40,32},{48,56},{56,48},{64,72... | collective-permute-start | bytes 98312 | tf_op jit(solution)/shard_map/ppermute | solution.py:280
  28.4 2.4 %collective-permute-start.3 = (bf16[16,1024]{1,0:T(8,128)(2,1)S(1)}, bf16[16,1024]{1,0:T(8,128)(2,1)S(1)}, u32[]{:S(2)}, u32[]{:S(2)}) collective-permute-start(bf16[16,1024]{1,0:T(8,128)(2,1)S(1)} %get-tuple-element.30), channel_id=1, source_target_pairs={{0,1},{1,0},{2,3},{3,2},{4,5},{5,4},{6,7},{7,6},{8,9},{9,8},{10,11... | collective-permute-start | bytes 98312 | tf_op jit(solution)/shard_map/ppermute | solution.py:280
  30.8 1.7 %shard_map.139 = (bf16[128,512]{1,0:T(8,128)(2,1)S(1)}, bf16[128,512]{1,0:T(8,128)(2,1)S(1)}, f32[192,128]{1,0:T(8,128)S(1)}) custom-call(s32[1,2]{1,0:T(1,128)S(1)} %add_bitcast_fusion.places.refs_0_, bf16[128,512]{1,0:T(8,128)(2,1)S(1)} %get-tuple-element.22.first.refs_4_, bf16[3,512,512]{2,1,0:T(8,128)(2,1)S(1)} %copy-done.1, ...), custom_call_target="tpu_custom_call" | custom-call | flops 2000000000 | bytes 5000000 | tf_op jit(solution)/shard_map/pallas_call | solution.py:55
  32.6 3.9 %shard_map.140 = (bf16[272,1024]{1,0:T(8,128)(2,1)S(1)}, f32[128,1024]{1,0:T(8,128)S(1)}, bf16[16,1024]{1,0:T(8,128)(2,1)S(1)}, bf16[16,1024]{1,0:T(8,128)(2,1)S(1)}, bf16[16,1024]{1,0:T(8,128)(2,1)S(1)}) custom-call(bf16[128,512]{1,0:T(8,128)(2,1)S(1)} %get-tuple-element.23.refs_0_, bf16[128,1024]{1,0:T(8,128)(2,1)S(1)} %get-tuple-element.24.refs_1_, ...), custom_call_target="tpu_custom_call" | custom-call | flops 3200000000 | bytes 8000000 | tf_op jit(solution)/shard_map/pallas_call | solution.py:55
  36.5 2.0 %collective-permute-start.7 = (bf16[272,1024]{1,0:T(8,128)(2,1)S(1)}, bf16[272,1024]{1,0:T(8,128)(2,1)S(1)}, u32[]{:S(2)}, u32[]{:S(2)}) collective-permute-start(bf16[272,1024]{1,0:T(8,128)(2,1)S(1)} %get-tuple-element.31.sent.refs_2_.refs_1_), channel_id=1, source_target_pairs={{0,1},{1,0},{2,3},{3,2},{4,5},{5,4},{6,7},{7,6},{8,9},{9,8},{10,11... | collective-permute-start | bytes 1671176 | tf_op jit(solution)/shard_map/ppermute | solution.py:280
  38.4 1.9 %collective-permute-start.4 = (bf16[16,1024]{1,0:T(8,128)(2,1)S(1)}, bf16[16,1024]{1,0:T(8,128)(2,1)S(1)}, u32[]{:S(2)}, u32[]{:S(2)}) collective-permute-start(bf16[16,1024]{1,0:T(8,128)(2,1)S(1)} %get-tuple-element.33), channel_id=1, source_target_pairs={{0,504},{8,16},{16,8},{24,32},{32,24},{40,48},{48,40},{56,64},{64,... | collective-permute-start | bytes 98312 | tf_op jit(solution)/shard_map/ppermute | solution.py:280
  40.4 5.1 %collective-permute-start.5 = (bf16[16,1024]{1,0:T(8,128)(2,1)S(1)}, bf16[16,1024]{1,0:T(8,128)(2,1)S(1)}, u32[]{:S(2)}, u32[]{:S(2)}) collective-permute-start(bf16[16,1024]{1,0:T(8,128)(2,1)S(1)} %get-tuple-element.34), channel_id=1, source_target_pairs={{0,7},{1,2},{2,1},{3,4},{4,3},{5,6},{6,5},{7,0},{8,15},{9,10},{10,... | collective-permute-start | bytes 98312 | tf_op jit(solution)/shard_map/ppermute | solution.py:280
  45.5 3.7 %collective-permute-start.6 = (bf16[16,1024]{1,0:T(8,128)(2,1)S(1)}, bf16[16,1024]{1,0:T(8,128)(2,1)S(1)}, u32[]{:S(2)}, u32[]{:S(2)}) collective-permute-start(bf16[16,1024]{1,0:T(8,128)(2,1)S(1)} %get-tuple-element.35), channel_id=1, source_target_pairs={{0,8},{8,0},{16,24},{24,16},{32,40},{40,32},{48,56},{56,48},{64,72... | collective-permute-start | bytes 98312 | tf_op jit(solution)/shard_map/ppermute | solution.py:280
  49.2 2.5 %shard_map.144 = (bf16[768,768]{1,0:T(8,128)(2,1)S(1)}, f32[256,512]{1,0:T(8,128)}) custom-call(s32[1,2]{1,0:T(1,128)S(1)} %add_bitcast_fusion.places.refs_0_, s32[1,2]{1,0:T(1,128)S(1)} %copy-done.19, bf16[272,1024]{1,0:T(8,128)(2,1)S(1)} %get-tuple-element.31.sent.refs_2_.refs_1_, s32[768,1]{1,0:T(8,128)S(1)} %copy-done.15, s32[256,1]{1,0:T(8,128)S(1)} %copy-done.16, ...), custom_call_target="tpu_custom_call" | custom-call | flops 1600000000 | bytes 4000000 | tf_op jit(solution)/shard_map/pallas_call | solution.py:55
  51.7 1.0 copy-done.17
  52.8 3.8 %all-to-all-start.1 = ((f32[4,64,512]{2,1,0:T(8,128)}), f32[4,64,512]{2,1,0:T(8,128)S(1)}, u32[]{:S(2)}, u32[]{:S(2)}) async-start(f32[4,64,512]{2,1,0:T(8,128)} %bitcast.7), calls=%async_computation.1 | async-start | bytes 1048576 | tf_op jit(solution)/shard_map/all_to_all | solution.py:353
  56.6 1.2 %shard_map.142.late.refs_2_ = bf16[128,1024]{1,0:T(8,128)(2,1)S(1)} custom-call(s32[1,2]{1,0:T(1,128)S(1)} %add_bitcast_fusion.places.refs_0_, f32[128,1024]{1,0:T(8,128)S(1)} %get-tuple-element.32.refs_1_, s32[4,16]{1,0:T(4,128)S(1)} %copy-done.12, bf16[16,1024]{1,0:T(8,128)(2,1)S(1)} %collective-permute-done.4.refs_3_, ...), custom_call_target="tpu_custom_call" | custom-call | flops 800000000 | bytes 2000000 | tf_op jit(solution)/shard_map/pallas_call | solution.py:55
  57.8 1.9 %collective-permute-start.8 = (bf16[128,1024]{1,0:T(8,128)(2,1)S(1)}, bf16[128,1024]{1,0:T(8,128)(2,1)S(1)}, u32[]{:S(2)}, u32[]{:S(2)}) collective-permute-start(bf16[128,1024]{1,0:T(8,128)(2,1)S(1)} %shard_map.142.late.refs_2_), channel_id=1, source_target_pairs={{0,1},{1,0},{2,3},{3,2},{4,5},{5,4},{6,7},{7,6},{8,9},{9,8},{10,11... | collective-permute-start | bytes 786440 | tf_op jit(solution)/shard_map/ppermute | solution.py:280
  59.8 1.5 %collective-permute-done.8.refs_4_ = bf16[128,1024]{1,0:T(8,128)(2,1)S(1)} collective-permute-done((bf16[128,1024]{1,0:T(8,128)(2,1)S(1)}, bf16[128,1024]{1,0:T(8,128)(2,1)S(1)}, u32[]{:S(2)}, u32[]{:S(2)}) %collective-permute-start.8) | collective-permute-done | bytes 262176 | tf_op jit(solution)/shard_map/ppermute | solution.py:280
  61.3 0.9 shard_map.145
  62.2 2.5 %all-to-all-done.1.refs_1_ = f32[4,64,512]{2,1,0:T(8,128)S(1)} async-done(((f32[4,64,512]{2,1,0:T(8,128)}), f32[4,64,512]{2,1,0:T(8,128)S(1)}, u32[]{:S(2)}, u32[]{:S(2)}) %all-to-all-start.1) | async-done | bytes 524320 | tf_op jit(solution)/shard_map/all_to_all | solution.py:353
  64.7 22.4 %all_to_all.15.refs_0_ = f32[4,192,512]{2,1,0:T(8,128)S(1)} all-to-all(f32[4,192,512]{2,1,0:T(8,128)S(1)} %bitcast.11), channel_id=1, replica_groups=mesh['yh'=2,'z'=8,'x'=4,'yl'=4,'core'=2] {'x'}, dimensions={0} | all-to-all | bytes 3145728 | tf_op jit(solution)/shard_map/all_to_all | solution.py:373
  87.1 1.1 shard_map.146
  88.2 9.4 %all-to-all-start.2 = ((f32[64,4,512]{2,1,0:T(4,128)}), f32[64,4,512]{2,1,0:T(4,128)S(1)}, u32[]{:S(2)}, u32[]{:S(2)}) async-start(f32[64,4,512]{2,1,0:T(4,128)} %shard_map.146), calls=%async_computation.2 | async-start | bytes 1048576 | tf_op jit(solution)/shard_map/all_to_all | solution.py:387
  97.6 0.9 shard_map.141
  98.5 0.5 copy-done.2
  99.1 1.4 %shard_map.143 = f32[128,512]{1,0:T(8,128)} custom-call(bf16[128,512]{1,0:T(8,128)(2,1)S(1)} %copy-done.6, bf16[128,512]{1,0:T(8,128)(2,1)S(1)} %copy-done.8, f32[1,512]{1,0:T(1,128)S(1)} %bitcast.15, bf16[272,1024]{1,0:T(8,128)(2,1)S(1)} %get-tuple-element.31.sent.refs_2_.refs_1_, bf16[128,1024]{1,0:T(8,128)(2,1)S(1)} %shard_map.142.late.refs_2_, ...), custom_call_target="tpu_custom_call" | custom-call | flops 1200000000 | bytes 3000000 | tf_op jit(solution)/shard_map/pallas_call | solution.py:55
  100.5 16.5 %all-to-all-done.2.refs_0_ = f32[64,4,512]{2,1,0:T(4,128)S(1)} async-done(((f32[64,4,512]{2,1,0:T(4,128)}), f32[64,4,512]{2,1,0:T(4,128)S(1)}, u32[]{:S(2)}, u32[]{:S(2)}) %all-to-all-start.2) | async-done | bytes 524320 | tf_op jit(solution)/shard_map/all_to_all | solution.py:387
  117.1 0.8 shard_map.147
  (42 shorter events, 0.1 us)
Async XLA Ops:
  0.7 1.4 %copy-start = (bf16[3,512,512]{2,1,0:T(8,128)(2,1)S(1)}, bf16[3,512,512]{2,1,0:T(8,128)(2,1)}, u32[]{:S(2)}) copy-start(bf16[3,512,512]{2,1,0:T(8,128)(2,1)} %weight.5) | copy-start | bytes 4718596
  2.1 0.9 copy-start.5
  3.0 0.7 copy-start.11
  3.7 0.7 copy-start.13
  4.4 26.4 %copy-start.1 = (bf16[3,512,512]{2,1,0:T(8,128)(2,1)S(1)}, bf16[3,512,512]{2,1,0:T(8,128)(2,1)}, u32[]{:S(2)}) copy-start(bf16[3,512,512]{2,1,0:T(8,128)(2,1)} %weight.5) | copy-start | bytes 4718596
  4.4 26.4 %copy-start.3 = (bf16[512,512]{1,0:T(8,128)(2,1)S(1)}, bf16[512,512]{1,0:T(8,128)(2,1)}, u32[]{:S(2)}) copy-start(bf16[512,512]{1,0:T(8,128)(2,1)} %output_weight.3) | copy-start | bytes 1572868
  4.4 26.4 %copy-start.7 = (bf16[128,512]{1,0:T(8,128)(2,1)S(1)}, bf16[128,512]{1,0:T(8,128)(2,1)}, u32[]{:S(2)}) copy-start(bf16[128,512]{1,0:T(8,128)(2,1)} %cotangent.3) | copy-start | bytes 393220
  4.4 26.4 %copy-start.9 = (s32[128,64]{0,1:T(8,128)S(1)}, s32[128,64]{0,1:T(8,128)}, u32[]{:S(2)}) copy-start(s32[128,64]{0,1:T(8,128)} %param.16) | copy-start | bytes 98308
  4.4 26.4 %copy-start.10 = (s32[128,64]{0,1:T(8,128)S(1)}, s32[128,64]{0,1:T(8,128)}, u32[]{:S(2)}) copy-start(s32[128,64]{0,1:T(8,128)} %param.17) | copy-start | bytes 98308
  5.5 27.0 %collective-permute-start = (bf16[16,1024]{1,0:T(8,128)(2,1)S(1)}, bf16[16,1024]{1,0:T(8,128)(2,1)S(1)}, u32[]{:S(2)}, u32[]{:S(2)}) collective-permute-start(bf16[16,1024]{1,0:T(8,128)(2,1)S(1)} %get-tuple-element.27), channel_id=1, source_target_pairs={{0,504},{8,16},{16,8},{24,32},{32,24},{40,48},{48,40},{56,64},{64,... | collective-permute-start | bytes 98312 | tf_op jit(solution)/shard_map/ppermute | solution.py:280
  9.0 23.6 %collective-permute-start.1 = (bf16[16,1024]{1,0:T(8,128)(2,1)S(1)}, bf16[16,1024]{1,0:T(8,128)(2,1)S(1)}, u32[]{:S(2)}, u32[]{:S(2)}) collective-permute-start(bf16[16,1024]{1,0:T(8,128)(2,1)S(1)} %get-tuple-element.28), channel_id=1, source_target_pairs={{0,7},{1,2},{2,1},{3,4},{4,3},{5,6},{6,5},{7,0},{8,15},{9,10},{10,... | collective-permute-start | bytes 98312 | tf_op jit(solution)/shard_map/ppermute | solution.py:280
  13.6 18.9 %collective-permute-start.2 = (bf16[16,1024]{1,0:T(8,128)(2,1)S(1)}, bf16[16,1024]{1,0:T(8,128)(2,1)S(1)}, u32[]{:S(2)}, u32[]{:S(2)}) collective-permute-start(bf16[16,1024]{1,0:T(8,128)(2,1)S(1)} %get-tuple-element.29), channel_id=1, source_target_pairs={{0,8},{8,0},{16,24},{24,16},{32,40},{40,32},{48,56},{56,48},{64,72... | collective-permute-start | bytes 98312 | tf_op jit(solution)/shard_map/ppermute | solution.py:280
  28.4 4.2 %collective-permute-start.3 = (bf16[16,1024]{1,0:T(8,128)(2,1)S(1)}, bf16[16,1024]{1,0:T(8,128)(2,1)S(1)}, u32[]{:S(2)}, u32[]{:S(2)}) collective-permute-start(bf16[16,1024]{1,0:T(8,128)(2,1)S(1)} %get-tuple-element.30), channel_id=1, source_target_pairs={{0,1},{1,0},{2,3},{3,2},{4,5},{5,4},{6,7},{7,6},{8,9},{9,8},{10,11... | collective-permute-start | bytes 98312 | tf_op jit(solution)/shard_map/ppermute | solution.py:280
  32.6 16.6 %copy-start.15 = (s32[768,1]{1,0:T(8,128)S(1)}, s32[768,1]{1,0:T(8,128)}, u32[]{:S(2)}) copy-start(s32[768,1]{1,0:T(8,128)} %constant.29.clone.refs_3_) | copy-start | bytes 9220
  32.6 16.6 %copy-start.16 = (s32[256,1]{1,0:T(8,128)S(1)}, s32[256,1]{1,0:T(8,128)}, u32[]{:S(2)}) copy-start(s32[256,1]{1,0:T(8,128)} %constant.30.clone.refs_4_) | copy-start | bytes 3076
  32.6 16.6 %copy-start.19 = (s32[1,2]{1,0:T(1,128)S(1)}, s32[1,2]{1,0:T(1,128)}, u32[]{:S(2)}) copy-start(s32[1,2]{1,0:T(1,128)} %constant.28.clone.refs_1_) | copy-start | bytes 28
  36.5 12.7 %collective-permute-start.7 = (bf16[272,1024]{1,0:T(8,128)(2,1)S(1)}, bf16[272,1024]{1,0:T(8,128)(2,1)S(1)}, u32[]{:S(2)}, u32[]{:S(2)}) collective-permute-start(bf16[272,1024]{1,0:T(8,128)(2,1)S(1)} %get-tuple-element.31.sent.refs_2_.refs_1_), channel_id=1, source_target_pairs={{0,1},{1,0},{2,3},{3,2},{4,5},{5,4},{6,7},{7,6},{8,9},{9,8},{10,11... | collective-permute-start | bytes 1671176 | tf_op jit(solution)/shard_map/ppermute | solution.py:280
  38.4 18.2 %collective-permute-start.4 = (bf16[16,1024]{1,0:T(8,128)(2,1)S(1)}, bf16[16,1024]{1,0:T(8,128)(2,1)S(1)}, u32[]{:S(2)}, u32[]{:S(2)}) collective-permute-start(bf16[16,1024]{1,0:T(8,128)(2,1)S(1)} %get-tuple-element.33), channel_id=1, source_target_pairs={{0,504},{8,16},{16,8},{24,32},{32,24},{40,48},{48,40},{56,64},{64,... | collective-permute-start | bytes 98312 | tf_op jit(solution)/shard_map/ppermute | solution.py:280
  40.4 16.2 %collective-permute-start.5 = (bf16[16,1024]{1,0:T(8,128)(2,1)S(1)}, bf16[16,1024]{1,0:T(8,128)(2,1)S(1)}, u32[]{:S(2)}, u32[]{:S(2)}) collective-permute-start(bf16[16,1024]{1,0:T(8,128)(2,1)S(1)} %get-tuple-element.34), channel_id=1, source_target_pairs={{0,7},{1,2},{2,1},{3,4},{4,3},{5,6},{6,5},{7,0},{8,15},{9,10},{10,... | collective-permute-start | bytes 98312 | tf_op jit(solution)/shard_map/ppermute | solution.py:280
  45.5 11.1 %copy-start.12 = (s32[4,16]{1,0:T(4,128)S(1)}, s32[4,16]{1,0:T(4,128)}, u32[]{:S(2)}) copy-start(s32[4,16]{1,0:T(4,128)} %refs_2_.1) | copy-start | bytes 772
  45.5 11.1 %collective-permute-start.6 = (bf16[16,1024]{1,0:T(8,128)(2,1)S(1)}, bf16[16,1024]{1,0:T(8,128)(2,1)S(1)}, u32[]{:S(2)}, u32[]{:S(2)}) collective-permute-start(bf16[16,1024]{1,0:T(8,128)(2,1)S(1)} %get-tuple-element.35), channel_id=1, source_target_pairs={{0,8},{8,0},{16,24},{24,16},{32,40},{40,32},{48,56},{56,48},{64,72... | collective-permute-start | bytes 98312 | tf_op jit(solution)/shard_map/ppermute | solution.py:280
  51.7 1.0 copy-start.17
  52.8 11.9 %all-to-all-start.1 = ((f32[4,64,512]{2,1,0:T(8,128)}), f32[4,64,512]{2,1,0:T(8,128)S(1)}, u32[]{:S(2)}, u32[]{:S(2)}) async-start(f32[4,64,512]{2,1,0:T(8,128)} %bitcast.7), calls=%async_computation.1 | async-start | bytes 1048576 | tf_op jit(solution)/shard_map/all_to_all | solution.py:353
  56.6 4.7 %copy-start.18 = (bf16[768,768]{1,0:T(8,128)(2,1)S(1)}, bf16[768,768]{1,0:T(8,128)(2,1)}, u32[]{:S(2)}) copy-start(bf16[768,768]{1,0:T(8,128)(2,1)} %copy-done.17) | copy-start | bytes 3538948
  57.8 3.4 %collective-permute-start.8 = (bf16[128,1024]{1,0:T(8,128)(2,1)S(1)}, bf16[128,1024]{1,0:T(8,128)(2,1)S(1)}, u32[]{:S(2)}, u32[]{:S(2)}) collective-permute-start(bf16[128,1024]{1,0:T(8,128)(2,1)S(1)} %shard_map.142.late.refs_2_), channel_id=1, source_target_pairs={{0,1},{1,0},{2,3},{3,2},{4,5},{5,4},{6,7},{7,6},{8,9},{9,8},{10,11... | collective-permute-start | bytes 786440 | tf_op jit(solution)/shard_map/ppermute | solution.py:280
  87.1 10.5 %copy-start.4 = (bf16[512,512]{1,0:T(8,128)(2,1)S(1)}, bf16[512,512]{1,0:T(8,128)(2,1)}, u32[]{:S(2)}) copy-start(bf16[512,512]{1,0:T(8,128)(2,1)} %output_weight.3) | copy-start | bytes 1572868
  87.1 10.5 %copy-start.6 = (bf16[128,512]{1,0:T(8,128)(2,1)S(1)}, bf16[128,512]{1,0:T(8,128)(2,1)}, u32[]{:S(2)}) copy-start(bf16[128,512]{1,0:T(8,128)(2,1)} %features.5) | copy-start | bytes 393220
  88.2 28.9 %all-to-all-start.2 = ((f32[64,4,512]{2,1,0:T(4,128)}), f32[64,4,512]{2,1,0:T(4,128)S(1)}, u32[]{:S(2)}, u32[]{:S(2)}) async-start(f32[64,4,512]{2,1,0:T(4,128)} %shard_map.146), calls=%async_computation.2 | async-start | bytes 1048576 | tf_op jit(solution)/shard_map/all_to_all | solution.py:387
  97.6 1.5 %copy-start.2 = (bf16[3,512,512]{2,1,0:T(8,128)(2,1)S(1)}, bf16[3,512,512]{2,1,0:T(8,128)(2,1)}, u32[]{:S(2)}) copy-start(bf16[3,512,512]{2,1,0:T(8,128)(2,1)} %weight.5) | copy-start | bytes 4718596
  97.6 1.4 %copy-start.8 = (bf16[128,512]{1,0:T(8,128)(2,1)S(1)}, bf16[128,512]{1,0:T(8,128)(2,1)}, u32[]{:S(2)}) copy-start(bf16[128,512]{1,0:T(8,128)(2,1)} %cotangent.3) | copy-start | bytes 393220
  97.6 1.4 %copy-start.14 = (f32[512]{0:T(512)S(1)}, f32[512]{0:T(512)}, u32[]{:S(2)}) copy-start(f32[512]{0:T(512)} %param.13) | copy-start | bytes 6148

commit v3 on v2

--- a/solution.py
+++ b/solution.py
@@ -1,3 +1,4 @@
+import functools
 import math
 
 import jax
@@ -85,19 +86,62 @@
     return (row_ids == chosen).astype(F32).astype(BF16)
 
 
-def keys_kernel(places, features, gain, weight, send_rows, first, key_values, *bands):
+def keys_kernel(
+    places, features_hbm, gain_hbm, weight_hbm, send_rows_hbm,
+    first, key_values, band0, band1, band2, band3,
+    features, gain, weight, send_rows, arrived,
+):
+    copies = [
+        pltpu.make_async_copy(source, local, arrived.at[index])
+        for index, (source, local) in enumerate(
+            (
+                (features_hbm, features),
+                (gain_hbm, gain),
+                (weight_hbm.at[1], weight.at[0]),
+                (weight_hbm.at[2], weight.at[1]),
+                (send_rows_hbm, send_rows),
+            )
+        )
+    ]
+    for copy in copies:
+        copy.start()
+    copies[0].wait()
+    copies[1].wait()
     values = features[...].astype(F32)
     normed = (values * norm_factor(values) * gain[...]).astype(BF16)
     first[...] = normed
     width = weight.shape[2]
     for part in range(2):
-        key_values[:, part * width : (part + 1) * width] = dot(normed, weight[1 + part]).astype(
-            BF16
-        )
+        copies[2 + part].wait()
+        key_values[:, part * width : (part + 1) * width] = dot(normed, weight[part]).astype(BF16)
+    copies[4].wait()
     table = key_values[...]
-    for index in range(4):
+    for index, band in enumerate((band0, band1, band2, band3)):
         chosen = listed(places, send_rows, index, features.shape[0])
-        bands[index][...] = dot(chosen, table, ((0,), (0,))).astype(BF16)
+        band[...] = dot(chosen, table, ((0,), (0,))).astype(BF16)
+
+
+def keys_call(places, features, gain, weight, send_rows):
+    rows, width = features.shape
+    band = shape(send_rows.shape[1], 2 * width)
+    vmem = pl.BlockSpec(memory_space=pltpu.VMEM)
+    return pl.pallas_call(
+        keys_kernel,
+        out_shape=(shape(rows, width), shape(rows, 2 * width), band, band, band, band),
+        in_specs=[pl.BlockSpec(memory_space=pltpu.SMEM)]
+        + [pl.BlockSpec(memory_space=pltpu.HBM)] * 4,
+        out_specs=(vmem,) * 6,
+        scratch_shapes=[
+            pltpu.VMEM(features.shape, BF16),
+            pltpu.VMEM(gain.shape, F32),
+            pltpu.VMEM((2, width, width), BF16),
+            pltpu.VMEM(send_rows.shape, jnp.int32),
+            pltpu.SemaphoreType.DMA((5,)),
+        ],
+        cost_estimate=pl.CostEstimate(
+            flops=1200000000, bytes_accessed=3000000, transcendentals=0
+        ),
+    )(places, features, gain, weight, send_rows)
 
 
 def queries_kernel(
@@ -188,11 +232,9 @@
 
 
 def chosen_kernel(places, per_core, sent, feature_of, cell_of, partner, left, grad_output):
-    width = grad_output.shape[1]
-    rows = left.shape[1] // 6
-    offset = places[0, 0]
+    width, rows = sent.shape[1] // 2, left.shape[1] // 6
     columns = lax.broadcasted_iota(jnp.int32, (feature_of.shape[0], width), 1)
-    target = feature_of[...] + offset * per_core[0, 0]
+    target = feature_of[...] + places[0, 0] * per_core[0, 0]
     feature = jnp.bitwise_and(target, width - 1)
     chosen = (feature == columns).astype(F32).astype(BF16)
     part = jnp.right_shift(target, width.bit_length() - 1)
@@ -202,7 +244,8 @@
             at = (2 * piece + index) * rows
             left[:, at : at + rows] = jnp.where(part == piece, picked, 0.0).astype(BF16)
     columns = lax.broadcasted_iota(jnp.int32, (cell_of.shape[0], width), 1)
-    chosen = (cell_of[...] + offset * per_core[0, 1] == columns).astype(F32).astype(BF16)
+    target = cell_of[...] + places[0, 0] * per_core[0, 1]
+    chosen = (target == columns).astype(F32).astype(BF16)
     total = None
     for source in (sent, partner):
         picked = dot(chosen, source[:rows, width:], ((1,), (1,))).astype(BF16)
@@ -219,8 +262,10 @@
     grad_keys_values[...] = total.astype(BF16)
 
 
-def project_kernel(left, sent, own_grads, partner, partner_grads, grad_project, right):
-    rows, width = own_grads.shape[0], grad_project.shape[1]
+def project_kernel(
+    left, sent, own_grads, grad_output, partner, partner_grads, both, right
+):
+    rows, width = own_grads.shape[0], both.shape[2]
     for index, (early, late) in enumerate(((sent, own_grads), (partner, partner_grads))):
         pieces = (
             early[rows : 2 * rows, width:],
@@ -230,7 +275,13 @@
         for piece in range(3):
             at = (2 * piece + index) * rows
             right[at : at + rows, :] = pieces[piece]
-    grad_project[...] = dot(left[...], right[...])
+    near = both.shape[0]
+    count = left.shape[0] // near
+    for index in range(near):
+        both[index, :count, :] = dot(left[index * count : (index + 1) * count, :], right[...])
+    count = grad_output.shape[0] // near
+    for index in range(near):
+        both[index, -count:, :] = grad_output[index * count : (index + 1) * count, :]
 
 
 def features_kernel(features, cotangent, gain, sent, late, weight, grad_features):
@@ -249,14 +300,13 @@
     )
 
 
-def near_kernel(project, output, summed):
+def near_kernel(both, summed):
     far = summed.shape[0]
-    for source, first_row in ((project, 0), (output, summed.shape[1] - output.shape[1] // far)):
-        total = source[0]
-        for index in range(1, source.shape[0]):
-            total = total + source[index]
-        for row in range(source.shape[1] // far):
-            summed[:, first_row + row, :] = total[row * far : (row + 1) * far, :]
+    total = both[0]
+    for index in range(1, both.shape[0]):
+        total = total + both[index]
+    for row in range(summed.shape[1]):
+        summed[:, row, :] = total[row * far : (row + 1) * far, :]
 
 
 def far_kernel(scale, parts, grad_project, grad_output):
@@ -268,7 +318,8 @@
         for piece in range(per_row):
             values = total[row : row + 1, piece * lanes : (piece + 1) * lanes]
             if row < project_rows:
-                grad_project[row * per_row + piece : row * per_row + piece + 1, :] = values
+                at = row * per_row + piece
+                grad_project[at : at + 1, :] = values
             else:
                 at = (row - project_rows) * per_row + piece
                 grad_output[at : at + 1, :] = values
@@ -302,13 +353,7 @@
     core = lax.axis_index("core")
     places = jnp.stack([core, lax.axis_index("x") % 2]).astype(jnp.int32).reshape(1, 2)
     band = shape(cap, 2 * width)
-    first, key_values, *bands = call(
-        keys_kernel,
-        (shape(rows, width), shape(rows, 2 * width), band, band, band, band),
-        (places, features, gain, weight, send_rows),
-        3,
-        scalars=1,
-    )
+    first, key_values, *bands = keys_call(places, features, gain, weight, send_rows)
     steps = ((TENSOR, 0), (TENSOR, 1), (CELLS, 0), (CELLS, 1))
     received = [exchanged(bands[index], *steps[index]) for index in (3, 1, 2, 0)]
     queries, grad_mixed, counts = call(
@@ -341,17 +386,15 @@
         layer_kernel, shape(rows, width), (features, sent, output_weight), 3
     )
     feature_of, cell_of, per_core = row_order(sizes, width)
+    near = sizes["x"]
+    far = devices // (2 * near)
     left, grad_output = call(
         chosen_kernel,
         (shape(3 * width // 2, 6 * rows), shape(width // 2, width, dtype=F32)),
         (places, per_core, sent, feature_of, cell_of, partner),
-        4,
+        3,
         scalars=2,
         moved=1,
-    )
-    near = sizes["x"]
-    grad_output = lax.all_to_all(
-        grad_output.reshape(near, -1, width), "x", 0, 0, tiled=True
     )
     grad_keys_values = call(
         merge_kernel,
@@ -362,40 +405,28 @@
         moved=4,
     )
     partner_grads = exchanged(grad_keys_values, *steps[0])
-    grad_project = call(
+    both = call(
         project_kernel,
-        shape(3 * width // 2, width, dtype=F32),
-        (left, sent, grad_keys_values, partner, partner_grads),
+        shape(near, 2 * width // near, width, dtype=F32),
+        (left, sent, grad_keys_values, grad_output, partner, partner_grads),
         3,
         moved=2,
         scratch=(pltpu.VMEM((6 * rows, width), BF16),),
     )
-    grad_project = lax.all_to_all(
-        grad_project.reshape(near, -1, width), "x", 0, 0, tiled=True
-    )
+    both = lax.all_to_all(both, "x", 0, 0, tiled=True)
     grad_features = call(
         features_kernel,
         shape(rows, width, dtype=F32),
         (features, cotangent, gain, sent, grad_keys_values, weight),
         3,
     )
-    far = devices // (2 * near)
-    each = 4 * width // devices
     parts = call(
-        near_kernel, shape(far, each, width, dtype=F32), (grad_project, grad_output), 2, moved=2
+        near_kernel, shape(far, 4 * width // devices, width, dtype=F32), (both,), 2, moved=1
     )
     parts = lax.all_to_all(parts, FAR, 0, 0, tiled=True)
-    lanes = 128
-
-    def far_sum(*refs):
-        far_kernel(scale, *refs)
-
     grad_project, grad_output = call(
-        far_sum,
-        (
-            shape(3 * width * width // devices // lanes, lanes, dtype=F32),
-            shape(width * width // devices // lanes, lanes, dtype=F32),
-        ),
+        functools.partial(far_kernel, scale),
+        tuple(shape(count * width * width // devices // 128, 128, dtype=F32) for count in (3, 1)),
         (parts,),
         2,
         moved=1,

time: 118 us -> 119 us (level)
  blocking collectives: 22.4 us -> 30.4 us
  starting transfers between devices: 53 us -> 48.4 us
  local copies, waits for them, and re-layouts: 5.31 us -> 1.87 us
  Pallas kernels: 15.5 us -> 17 us
  waiting for transfers between devices: 20.6 us -> 19.3 us
    all_to_all x1, blocking collectives: 22.4 us -> 30.4 us  [body(): both = lax.all_to_all(both, 'x', 0, 0, tiled=True)]
    all_to_all x1 -> x0, starting transfers between devices: 3.85 us -> none  [body(): lax.all_to_all(grad_output.reshape(near, -1, width), 'x', 0, 0, tiled=True)]
    unnamed x40 -> x30, local copies, waits for them, and re-layouts: 5.31 us -> 1.87 us
    pallas_call x0 -> x1, Pallas kernels: none -> 3.36 us  [keys_call(): pl.pallas_call(keys_kernel, out_shape=(shape(rows, width), shape(rows, 2...]
    all_to_all x1 -> x0, waiting for transfers between devices: 2.52 us -> none  [body(): lax.all_to_all(grad_output.reshape(near, -1, width), 'x', 0, 0, tiled=True)]
    pallas_call x10 -> x9, Pallas kernels: 15.5 us -> 13.6 us  [call(): pl.pallas_call(moving if moved else kernel, out_shape=out_shapes, in_spec...]
    ppermute x9, waiting for transfers between devices: 1.52 us -> 2.82 us  [exchanged(): lax.ppermute(block, axis, [(i, partner % size) for i, partner in enumerat...]
  transfers between devices with their start and end apart: 11 -> 10, of which waited for: 3 -> 2; matrix products, arithmetic and copies ran while one was open for 0% -> 0% of each run, Pallas kernels for 7% -> 5%
where the time goes in v3:
time: 119 us
  starting transfers between devices  48.4 us (41%)
  blocking collectives  30.4 us (26%)
  waiting for transfers between devices  19.3 us (16%)
  Pallas kernels  17 us (14%)
  local copies, waits for them, and re-layouts  1.87 us (2%)
    ppermute x9, starting transfers between devices, exchanged(): lax.ppermute(block, axis, [(i, partner % size) for i, partner in enumerat...  39.2 us
    all_to_all x1, blocking collectives, body(): both = lax.all_to_all(both, 'x', 0, 0, tiled=True)  30.4 us
    all_to_all x1, waiting for transfers between devices, body(): parts = lax.all_to_all(parts, FAR, 0, 0, tiled=True)  16.5 us
    pallas_call x9, Pallas kernels, call(): pl.pallas_call(moving if moved else kernel, out_shape=out_shapes, in_spec...  13.6 us
    all_to_all x1, starting transfers between devices, body(): parts = lax.all_to_all(parts, FAR, 0, 0, tiled=True)  9.21 us
    pallas_call x1, Pallas kernels, keys_call(): pl.pallas_call(keys_kernel, out_shape=(shape(rows, width), shape(rows, 2...  3.36 us
    ppermute x9, waiting for transfers between devices, exchanged(): lax.ppermute(block, axis, [(i, partner % size) for i, partner in enumerat...  2.82 us
  transfers between devices with their start and end apart: 10, of which 2 were waited for; matrix products, arithmetic and copies ran while one was open for 0% of the time, Pallas kernels for 5%

profile of v3, /device:TPU:2, one launch (start us, length us, event | category | flops | bytes accessed | tf_op | source)
XLA Modules:
  0.0 118.5 jit_solution(15231047434277065655)
XLA Ops:
  0.6 0.6 add_bitcast_fusion.places.refs_0_
  1.2 0.0 copy-start.6
  1.3 3.4 %shard_map.138 = (bf16[128,512]{1,0:T(8,128)(2,1)}, bf16[128,1024]{1,0:T(8,128)(2,1)}, bf16[16,1024]{1,0:T(8,128)(2,1)}, bf16[16,1024]{1,0:T(8,128)(2,1)}, bf16[...) custom-call(s32[1,2]{1,0:T(1,128)} %add_bitcast_fusion.places.refs_0_, bf16[128,512]{1,0:T(8,128)(2,1)} %features.3, ...), custom_call_target="tpu_custom_call" | custom-call | flops 1200000000 | bytes 3000000 | tf_op jit(solution)/shard_map/pallas_call | solution.py:128
  4.6 3.4 %collective-permute-start = (bf16[16,1024]{1,0:T(8,128)(2,1)}, bf16[16,1024]{1,0:T(8,128)(2,1)S(1)}, u32[]{:S(2)}, u32[]{:S(2)}) collective-permute-start(bf16[16,1024]{1,0:T(8,128)(2,1)} %get-tuple-element.27), channel_id=1, source_target_pairs={{0,504},{8,16},{16,8},{24,32},{32,24},{40,48},{48,40},{56,64},{64,... | collective-permute-start | bytes 98312 | tf_op jit(solution)/shard_map/ppermute | solution.py:331
  8.0 4.7 %collective-permute-start.1 = (bf16[16,1024]{1,0:T(8,128)(2,1)}, bf16[16,1024]{1,0:T(8,128)(2,1)S(1)}, u32[]{:S(2)}, u32[]{:S(2)}) collective-permute-start(bf16[16,1024]{1,0:T(8,128)(2,1)} %get-tuple-element.28), channel_id=1, source_target_pairs={{0,7},{1,2},{2,1},{3,4},{4,3},{5,6},{6,5},{7,0},{8,15},{9,10},{10,... | collective-permute-start | bytes 98312 | tf_op jit(solution)/shard_map/ppermute | solution.py:331
  12.7 14.8 %collective-permute-start.2 = (bf16[16,1024]{1,0:T(8,128)(2,1)}, bf16[16,1024]{1,0:T(8,128)(2,1)S(1)}, u32[]{:S(2)}, u32[]{:S(2)}) collective-permute-start(bf16[16,1024]{1,0:T(8,128)(2,1)} %get-tuple-element.29), channel_id=1, source_target_pairs={{0,8},{8,0},{16,24},{24,16},{32,40},{40,32},{48,56},{56,48},{64,72... | collective-permute-start | bytes 98312 | tf_op jit(solution)/shard_map/ppermute | solution.py:331
  27.5 2.4 %collective-permute-start.3 = (bf16[16,1024]{1,0:T(8,128)(2,1)}, bf16[16,1024]{1,0:T(8,128)(2,1)S(1)}, u32[]{:S(2)}, u32[]{:S(2)}) collective-permute-start(bf16[16,1024]{1,0:T(8,128)(2,1)} %get-tuple-element.30), channel_id=1, source_target_pairs={{0,1},{1,0},{2,3},{3,2},{4,5},{5,4},{6,7},{7,6},{8,9},{9,8},{10,11... | collective-permute-start | bytes 98312 | tf_op jit(solution)/shard_map/ppermute | solution.py:331
  29.9 0.9 copy-done.14
  30.8 1.7 %shard_map.139 = (bf16[128,512]{1,0:T(8,128)(2,1)S(1)}, bf16[128,512]{1,0:T(8,128)(2,1)S(1)}, f32[192,128]{1,0:T(8,128)S(1)}) custom-call(s32[1,2]{1,0:T(1,128)S(1)} %copy-done.11, bf16[128,512]{1,0:T(8,128)(2,1)S(1)} %copy-done.14, bf16[3,512,512]{2,1,0:T(8,128)(2,1)S(1)} %copy-done, bf16[512,512]{1,0:T(8,128)(2,1)S(1)} %copy-done.1, ...), custom_call_target="tpu_custom_call" | custom-call | flops 2000000000 | bytes 5000000 | tf_op jit(solution)/shard_map/pallas_call | solution.py:56
  32.6 0.0 copy-start.7
  32.6 3.9 %shard_map.140 = (bf16[272,1024]{1,0:T(8,128)(2,1)S(1)}, f32[128,1024]{1,0:T(8,128)S(1)}, bf16[16,1024]{1,0:T(8,128)(2,1)S(1)}, bf16[16,1024]{1,0:T(8,128)(2,1)S(1)}, bf16[16,1024]{1,0:T(8,128)(2,1)S(1)}) custom-call(bf16[128,512]{1,0:T(8,128)(2,1)S(1)} %get-tuple-element.23.refs_0_, bf16[128,1024]{1,0:T(8,128)(2,1)S(1)} %copy-done.13, ...), custom_call_target="tpu_custom_call" | custom-call | flops 3200000000 | bytes 8000000 | tf_op jit(solution)/shard_map/pallas_call | solution.py:56
  36.4 0.0 copy-start.9
  36.4 0.0 copy-start.10
  36.5 0.0 copy-start.12
  36.5 2.1 %collective-permute-start.7 = (bf16[272,1024]{1,0:T(8,128)(2,1)S(1)}, bf16[272,1024]{1,0:T(8,128)(2,1)S(1)}, u32[]{:S(2)}, u32[]{:S(2)}) collective-permute-start(bf16[272,1024]{1,0:T(8,128)(2,1)S(1)} %get-tuple-element.31.sent.refs_2_.refs_1_), channel_id=1, source_target_pairs={{0,1},{1,0},{2,3},{3,2},{4,5},{5,4},{6,7},{7,6},{8,9},{9,8},{10,11... | collective-permute-start | bytes 1671176 | tf_op jit(solution)/shard_map/ppermute | solution.py:331
  38.6 1.9 %collective-permute-start.4 = (bf16[16,1024]{1,0:T(8,128)(2,1)S(1)}, bf16[16,1024]{1,0:T(8,128)(2,1)S(1)}, u32[]{:S(2)}, u32[]{:S(2)}) collective-permute-start(bf16[16,1024]{1,0:T(8,128)(2,1)S(1)} %get-tuple-element.33), channel_id=1, source_target_pairs={{0,504},{8,16},{16,8},{24,32},{32,24},{40,48},{48,40},{56,64},{64,... | collective-permute-start | bytes 98312 | tf_op jit(solution)/shard_map/ppermute | solution.py:331
  40.5 5.1 %collective-permute-start.5 = (bf16[16,1024]{1,0:T(8,128)(2,1)S(1)}, bf16[16,1024]{1,0:T(8,128)(2,1)S(1)}, u32[]{:S(2)}, u32[]{:S(2)}) collective-permute-start(bf16[16,1024]{1,0:T(8,128)(2,1)S(1)} %get-tuple-element.34), channel_id=1, source_target_pairs={{0,7},{1,2},{2,1},{3,4},{4,3},{5,6},{6,5},{7,0},{8,15},{9,10},{10,... | collective-permute-start | bytes 98312 | tf_op jit(solution)/shard_map/ppermute | solution.py:331
  45.6 3.0 %collective-permute-start.6 = (bf16[16,1024]{1,0:T(8,128)(2,1)S(1)}, bf16[16,1024]{1,0:T(8,128)(2,1)S(1)}, u32[]{:S(2)}, u32[]{:S(2)}) collective-permute-start(bf16[16,1024]{1,0:T(8,128)(2,1)S(1)} %get-tuple-element.35), channel_id=1, source_target_pairs={{0,8},{8,0},{16,24},{24,16},{32,40},{40,32},{48,56},{56,48},{64,72... | collective-permute-start | bytes 98312 | tf_op jit(solution)/shard_map/ppermute | solution.py:331
  48.6 2.8 %collective-permute-done.6.refs_5_ = bf16[16,1024]{1,0:T(8,128)(2,1)S(1)} collective-permute-done((bf16[16,1024]{1,0:T(8,128)(2,1)S(1)}, bf16[16,1024]{1,0:T(8,128)(2,1)S(1)}, u32[]{:S(2)}, u32[]{:S(2)}) %collective-permute-start.6) | collective-permute-done | bytes 32800 | tf_op jit(solution)/shard_map/ppermute | solution.py:331
  51.4 1.2 %shard_map.142.late.refs_2_ = bf16[128,1024]{1,0:T(8,128)(2,1)S(1)} custom-call(s32[1,2]{1,0:T(1,128)S(1)} %copy-done.11, f32[128,1024]{1,0:T(8,128)S(1)} %get-tuple-element.32.refs_1_, s32[4,16]{1,0:T(4,128)S(1)} %copy-done.7, bf16[16,1024]{1,0:T(8,128)(2,1)S(1)} %collective-permute-done.4.refs_3_, bf16[16,1024]{1,0:T(8,128)(2,1)S(1)} %collective-permute-done.5.refs_4_, ...), custom_call_target="tpu_custom_call" | custom-call | flops 800000000 | bytes 2000000 | tf_op jit(solution)/shard_map/pallas_call | solution.py:56
  52.6 1.9 %collective-permute-start.8 = (bf16[128,1024]{1,0:T(8,128)(2,1)S(1)}, bf16[128,1024]{1,0:T(8,128)(2,1)S(1)}, u32[]{:S(2)}, u32[]{:S(2)}) collective-permute-start(bf16[128,1024]{1,0:T(8,128)(2,1)S(1)} %shard_map.142.late.refs_2_), channel_id=1, source_target_pairs={{0,1},{1,0},{2,3},{3,2},{4,5},{5,4},{6,7},{7,6},{8,9},{9,8},{10,11... | collective-permute-start | bytes 786440 | tf_op jit(solution)/shard_map/ppermute | solution.py:331
  54.6 1.7 %shard_map.144 = (bf16[768,768]{1,0:T(8,128)(2,1)S(1)}, f32[256,512]{1,0:T(8,128)S(1)}) custom-call(s32[1,2]{1,0:T(1,128)S(1)} %copy-done.11, s32[1,2]{1,0:T(1,128)S(1)} %copy-done.12, bf16[272,1024]{1,0:T(8,128)(2,1)S(1)} %get-tuple-element.31.sent.refs_2_.refs_1_, s32[768,1]{1,0:T(8,128)S(1)} %copy-done.9, s32[256,1]{1,0:T(8,128)S(1)} %copy-done.10, ...), custom_call_target="tpu_custom_call" | custom-call | flops 1200000000 | bytes 3000000 | tf_op jit(solution)/shard_map/pallas_call | solution.py:56
  56.3 0.9 shard_map.145
  57.3 30.4 %all_to_all.10.refs_0_ = f32[4,256,512]{2,1,0:T(8,128)S(1)} all-to-all(f32[4,256,512]{2,1,0:T(8,128)S(1)} %shard_map.145), channel_id=1, replica_groups=mesh['yh'=2,'z'=8,'x'=4,'yl'=4,'core'=2] {'x'}, dimensions={0} | all-to-all | bytes 4194304 | tf_op jit(solution)/shard_map/all_to_all | solution.py:416
  87.6 1.1 shard_map.146
  88.8 9.2 %all-to-all-start.1 = ((f32[64,4,512]{2,1,0:T(4,128)}), f32[64,4,512]{2,1,0:T(4,128)S(1)}, u32[]{:S(2)}, u32[]{:S(2)}) async-start(f32[64,4,512]{2,1,0:T(4,128)} %shard_map.146), calls=%async_computation.1 | async-start | bytes 1048576 | tf_op jit(solution)/shard_map/all_to_all | solution.py:426
  98.0 0.9 copy-done.2
  98.9 0.9 shard_map.141
  99.8 0.0 copy-done.4
  99.8 1.4 %shard_map.143 = f32[128,512]{1,0:T(8,128)} custom-call(bf16[128,512]{1,0:T(8,128)(2,1)S(1)} %copy-done.2, bf16[128,512]{1,0:T(8,128)(2,1)S(1)} %copy-done.4, f32[1,512]{1,0:T(1,128)S(1)} %bitcast.12, bf16[272,1024]{1,0:T(8,128)(2,1)S(1)} %get-tuple-element.31.sent.refs_2_.refs_1_, bf16[128,1024]{1,0:T(8,128)(2,1)S(1)} %shard_map.142.late.refs_2_, ...), custom_call_target="tpu_custom_call" | custom-call | flops 1200000000 | bytes 3000000 | tf_op jit(solution)/shard_map/pallas_call | solution.py:56
  101.3 16.5 %all-to-all-done.1.refs_0_ = f32[64,4,512]{2,1,0:T(4,128)S(1)} async-done(((f32[64,4,512]{2,1,0:T(4,128)}), f32[64,4,512]{2,1,0:T(4,128)S(1)}, u32[]{:S(2)}, u32[]{:S(2)}) %all-to-all-start.1) | async-done | bytes 524320 | tf_op jit(solution)/shard_map/all_to_all | solution.py:426
  117.7 0.8 shard_map.147
  (30 shorter events, 0.1 us)
Async XLA Ops:
  1.2 28.6 %copy-start = (bf16[3,512,512]{2,1,0:T(8,128)(2,1)S(1)}, bf16[3,512,512]{2,1,0:T(8,128)(2,1)}, u32[]{:S(2)}) copy-start(bf16[3,512,512]{2,1,0:T(8,128)(2,1)} %weight.3) | copy-start | bytes 4718596
  1.2 28.6 %copy-start.1 = (bf16[512,512]{1,0:T(8,128)(2,1)S(1)}, bf16[512,512]{1,0:T(8,128)(2,1)}, u32[]{:S(2)}) copy-start(bf16[512,512]{1,0:T(8,128)(2,1)} %output_weight.3) | copy-start | bytes 1572868
  1.2 28.6 %copy-start.3 = (bf16[128,512]{1,0:T(8,128)(2,1)S(1)}, bf16[128,512]{1,0:T(8,128)(2,1)}, u32[]{:S(2)}) copy-start(bf16[128,512]{1,0:T(8,128)(2,1)} %cotangent.3) | copy-start | bytes 393220
  1.2 28.6 %copy-start.5 = (s32[128,64]{0,1:T(8,128)S(1)}, s32[128,64]{0,1:T(8,128)}, u32[]{:S(2)}) copy-start(s32[128,64]{0,1:T(8,128)} %param.16) | copy-start | bytes 98308
  1.2 28.6 %copy-start.6 = (s32[128,64]{0,1:T(8,128)S(1)}, s32[128,64]{0,1:T(8,128)}, u32[]{:S(2)}) copy-start(s32[128,64]{0,1:T(8,128)} %param.17) | copy-start | bytes 98308
  1.2 28.6 %copy-start.11 = (s32[1,2]{1,0:T(1,128)S(1)}, s32[1,2]{1,0:T(1,128)}, u32[]{:S(2)}) copy-start(s32[1,2]{1,0:T(1,128)} %add_bitcast_fusion.places.refs_0_) | copy-start | bytes 28
  4.6 27.9 %collective-permute-start = (bf16[16,1024]{1,0:T(8,128)(2,1)}, bf16[16,1024]{1,0:T(8,128)(2,1)S(1)}, u32[]{:S(2)}, u32[]{:S(2)}) collective-permute-start(bf16[16,1024]{1,0:T(8,128)(2,1)} %get-tuple-element.27), channel_id=1, source_target_pairs={{0,504},{8,16},{16,8},{24,32},{32,24},{40,48},{48,40},{56,64},{64,... | collective-permute-start | bytes 98312 | tf_op jit(solution)/shard_map/ppermute | solution.py:331
  8.0 24.5 %collective-permute-start.1 = (bf16[16,1024]{1,0:T(8,128)(2,1)}, bf16[16,1024]{1,0:T(8,128)(2,1)S(1)}, u32[]{:S(2)}, u32[]{:S(2)}) collective-permute-start(bf16[16,1024]{1,0:T(8,128)(2,1)} %get-tuple-element.28), channel_id=1, source_target_pairs={{0,7},{1,2},{2,1},{3,4},{4,3},{5,6},{6,5},{7,0},{8,15},{9,10},{10,... | collective-permute-start | bytes 98312 | tf_op jit(solution)/shard_map/ppermute | solution.py:331
  12.7 19.8 %collective-permute-start.2 = (bf16[16,1024]{1,0:T(8,128)(2,1)}, bf16[16,1024]{1,0:T(8,128)(2,1)S(1)}, u32[]{:S(2)}, u32[]{:S(2)}) collective-permute-start(bf16[16,1024]{1,0:T(8,128)(2,1)} %get-tuple-element.29), channel_id=1, source_target_pairs={{0,8},{8,0},{16,24},{24,16},{32,40},{40,32},{48,56},{56,48},{64,72... | collective-permute-start | bytes 98312 | tf_op jit(solution)/shard_map/ppermute | solution.py:331
  27.5 5.1 %collective-permute-start.3 = (bf16[16,1024]{1,0:T(8,128)(2,1)}, bf16[16,1024]{1,0:T(8,128)(2,1)S(1)}, u32[]{:S(2)}, u32[]{:S(2)}) collective-permute-start(bf16[16,1024]{1,0:T(8,128)(2,1)} %get-tuple-element.30), channel_id=1, source_target_pairs={{0,1},{1,0},{2,3},{3,2},{4,5},{5,4},{6,7},{7,6},{8,9},{9,8},{10,11... | collective-permute-start | bytes 98312 | tf_op jit(solution)/shard_map/ppermute | solution.py:331
  29.9 0.9 copy-start.14
  30.8 1.8 %copy-start.13 = (bf16[128,1024]{1,0:T(8,128)(2,1)S(1)}, bf16[128,1024]{1,0:T(8,128)(2,1)}, u32[]{:S(2)}) copy-start(bf16[128,1024]{1,0:T(8,128)(2,1)} %get-tuple-element.24.refs_1_) | copy-start | bytes 786436
  32.6 18.9 %copy-start.7 = (s32[4,16]{1,0:T(4,128)S(1)}, s32[4,16]{1,0:T(4,128)}, u32[]{:S(2)}) copy-start(s32[4,16]{1,0:T(4,128)} %refs_2_.1) | copy-start | bytes 772
  36.4 18.1 %copy-start.9 = (s32[768,1]{1,0:T(8,128)S(1)}, s32[768,1]{1,0:T(8,128)}, u32[]{:S(2)}) copy-start(s32[768,1]{1,0:T(8,128)} %constant.29.clone.refs_3_) | copy-start | bytes 9220
  36.4 18.1 %copy-start.10 = (s32[256,1]{1,0:T(8,128)S(1)}, s32[256,1]{1,0:T(8,128)}, u32[]{:S(2)}) copy-start(s32[256,1]{1,0:T(8,128)} %constant.30.clone.refs_4_) | copy-start | bytes 3076
  36.5 18.1 %copy-start.12 = (s32[1,2]{1,0:T(1,128)S(1)}, s32[1,2]{1,0:T(1,128)}, u32[]{:S(2)}) copy-start(s32[1,2]{1,0:T(1,128)} %constant.28.clone.refs_1_) | copy-start | bytes 28
  36.5 15.0 %collective-permute-start.7 = (bf16[272,1024]{1,0:T(8,128)(2,1)S(1)}, bf16[272,1024]{1,0:T(8,128)(2,1)S(1)}, u32[]{:S(2)}, u32[]{:S(2)}) collective-permute-start(bf16[272,1024]{1,0:T(8,128)(2,1)S(1)} %get-tuple-element.31.sent.refs_2_.refs_1_), channel_id=1, source_target_pairs={{0,1},{1,0},{2,3},{3,2},{4,5},{5,4},{6,7},{7,6},{8,9},{9,8},{10,11... | collective-permute-start | bytes 1671176 | tf_op jit(solution)/shard_map/ppermute | solution.py:331
  38.6 10.0 %collective-permute-start.4 = (bf16[16,1024]{1,0:T(8,128)(2,1)S(1)}, bf16[16,1024]{1,0:T(8,128)(2,1)S(1)}, u32[]{:S(2)}, u32[]{:S(2)}) collective-permute-start(bf16[16,1024]{1,0:T(8,128)(2,1)S(1)} %get-tuple-element.33), channel_id=1, source_target_pairs={{0,504},{8,16},{16,8},{24,32},{32,24},{40,48},{48,40},{56,64},{64,... | collective-permute-start | bytes 98312 | tf_op jit(solution)/shard_map/ppermute | solution.py:331
  40.5 8.1 %collective-permute-start.5 = (bf16[16,1024]{1,0:T(8,128)(2,1)S(1)}, bf16[16,1024]{1,0:T(8,128)(2,1)S(1)}, u32[]{:S(2)}, u32[]{:S(2)}) collective-permute-start(bf16[16,1024]{1,0:T(8,128)(2,1)S(1)} %get-tuple-element.34), channel_id=1, source_target_pairs={{0,7},{1,2},{2,1},{3,4},{4,3},{5,6},{6,5},{7,0},{8,15},{9,10},{10,... | collective-permute-start | bytes 98312 | tf_op jit(solution)/shard_map/ppermute | solution.py:331
  45.6 5.8 %collective-permute-start.6 = (bf16[16,1024]{1,0:T(8,128)(2,1)S(1)}, bf16[16,1024]{1,0:T(8,128)(2,1)S(1)}, u32[]{:S(2)}, u32[]{:S(2)}) collective-permute-start(bf16[16,1024]{1,0:T(8,128)(2,1)S(1)} %get-tuple-element.35), channel_id=1, source_target_pairs={{0,8},{8,0},{16,24},{24,16},{32,40},{40,32},{48,56},{56,48},{64,72... | collective-permute-start | bytes 98312 | tf_op jit(solution)/shard_map/ppermute | solution.py:331
  52.6 3.6 %collective-permute-start.8 = (bf16[128,1024]{1,0:T(8,128)(2,1)S(1)}, bf16[128,1024]{1,0:T(8,128)(2,1)S(1)}, u32[]{:S(2)}, u32[]{:S(2)}) collective-permute-start(bf16[128,1024]{1,0:T(8,128)(2,1)S(1)} %shard_map.142.late.refs_2_), channel_id=1, source_target_pairs={{0,1},{1,0},{2,3},{3,2},{4,5},{5,4},{6,7},{7,6},{8,9},{9,8},{10,11... | collective-permute-start | bytes 786440 | tf_op jit(solution)/shard_map/ppermute | solution.py:331
  88.8 29.0 %all-to-all-start.1 = ((f32[64,4,512]{2,1,0:T(4,128)}), f32[64,4,512]{2,1,0:T(4,128)S(1)}, u32[]{:S(2)}, u32[]{:S(2)}) async-start(f32[64,4,512]{2,1,0:T(4,128)} %shard_map.146), calls=%async_computation.1 | async-start | bytes 1048576 | tf_op jit(solution)/shard_map/all_to_all | solution.py:426
  98.0 0.9 copy-start.2
  98.9 0.9 copy-start.4
  98.9 0.9 copy-start.8

commit v4 on v3

--- a/solution.py
+++ b/solution.py
@@ -13,6 +13,8 @@
 HEADS = 8
 HEAD_DIM = 64
 EPSILON = 1e-06
+HEADER = 16
+HEADROOM = 13.0
 VMEM_BYTES = 16 * 1024 * 1024
 F32 = jnp.float32
 BF16 = jnp.bfloat16
@@ -262,9 +264,12 @@
     grad_keys_values[...] = total.astype(BF16)
 
 
-def project_kernel(
-    left, sent, own_grads, grad_output, partner, partner_grads, both, right
-):
+def exponent(values):
+    largest = jnp.max(jnp.max(jnp.abs(values), axis=0, keepdims=True), axis=1, keepdims=True)
+    return jnp.floor(jnp.log2(jnp.maximum(largest, 1e-30)))
+
+
+def project_kernel(left, sent, own_grads, grad_output, partner, partner_grads, both, right):
     rows, width = own_grads.shape[0], both.shape[2]
     for index, (early, late) in enumerate(((sent, own_grads), (partner, partner_grads))):
         pieces = (
@@ -276,12 +281,18 @@
             at = (2 * piece + index) * rows
             right[at : at + rows, :] = pieces[piece]
     near = both.shape[0]
-    count = left.shape[0] // near
-    for index in range(near):
-        both[index, :count, :] = dot(left[index * count : (index + 1) * count, :], right[...])
-    count = grad_output.shape[0] // near
-    for index in range(near):
-        both[index, -count:, :] = grad_output[index * count : (index + 1) * count, :]
+    first_row = 0
+    for part, values in enumerate((dot(left[...], right[...]), grad_output[...])):
+        power = exponent(values)
+        scaled = values * jnp.exp2(HEADROOM - power)
+        count = values.shape[0] // near
+        at = both.shape[1] - HEADER + part * (HEADER // 2)
+        for index in range(near):
+            both[index, first_row : first_row + count, :] = scaled[
+                index * count : (index + 1) * count, :
+            ]
+            both[index, at : at + HEADER // 2, :] = jnp.broadcast_to(power, (HEADER // 2, width))
+        first_row += count
 
 
 def features_kernel(features, cotangent, gain, sent, late, weight, grad_features):
@@ -301,12 +312,18 @@
 
 
 def near_kernel(both, summed):
-    far = summed.shape[0]
-    total = both[0]
-    for index in range(1, both.shape[0]):
-        total = total + both[index]
-    for row in range(summed.shape[1]):
-        summed[:, row, :] = total[row * far : (row + 1) * far, :]
+    far, each = summed.shape[:2]
+    first_row = 0
+    for part, per in enumerate((each - each // 4, each // 4)):
+        at = both.shape[1] - HEADER + part * (HEADER // 2)
+        total = None
+        for index in range(both.shape[0]):
+            scale = jnp.exp2(both[index, at : at + 1, :] - HEADROOM)
+            values = both[index, first_row * far : (first_row + per) * far, :] * scale
+            total = values if total is None else total + values
+        for row in range(per):
+            summed[:, first_row + row, :] = total[row * far : (row + 1) * far, :]
+        first_row += per
 
 
 def far_kernel(scale, parts, grad_project, grad_output):
@@ -407,13 +424,13 @@
     partner_grads = exchanged(grad_keys_values, *steps[0])
     both = call(
         project_kernel,
-        shape(near, 2 * width // near, width, dtype=F32),
+        shape(near, 2 * width // near + HEADER, width, dtype=F32),
         (left, sent, grad_keys_values, grad_output, partner, partner_grads),
         3,
         moved=2,
         scratch=(pltpu.VMEM((6 * rows, width), BF16),),
     )
-    both = lax.all_to_all(both, "x", 0, 0, tiled=True)
+    both = lax.all_to_all(both.astype(jnp.float16), "x", 0, 0, tiled=True).astype(F32)
     grad_features = call(
         features_kernel,
         shape(rows, width, dtype=F32),

time: 119 us -> 109 us (0.916)
  blocking collectives: 30.4 us -> 19.9 us
    all_to_all x1, blocking collectives: 30.4 us -> 19.9 us  [body(): lax.all_to_all(both.astype(jnp.float16), 'x', 0, 0, tiled=True).astype(F32)]
where the time goes in v4:
time: 109 us
  starting transfers between devices  48.4 us (44%)
  blocking collectives  19.9 us (18%)
  waiting for transfers between devices  19 us (17%)
  Pallas kernels  17.4 us (16%)
  local copies, waits for them, and re-layouts  1.87 us (2%)
  other arithmetic  1.14 us (1%)
    ppermute x9, starting transfers between devices, exchanged(): lax.ppermute(block, axis, [(i, partner % size) for i, partner in enumerat...  39.2 us
    all_to_all x1, blocking collectives, body(): lax.all_to_all(both.astype(jnp.float16), 'x', 0, 0, tiled=True).astype(F32)  19.9 us
    all_to_all x1, waiting for transfers between devices, body(): parts = lax.all_to_all(parts, FAR, 0, 0, tiled=True)  16.2 us
    pallas_call x9, Pallas kernels, call(): pl.pallas_call(moving if moved else kernel, out_shape=out_shapes, in_spec...  14.1 us
    all_to_all x1, starting transfers between devices, body(): parts = lax.all_to_all(parts, FAR, 0, 0, tiled=True)  9.21 us
    pallas_call x1, Pallas kernels, keys_call(): pl.pallas_call(keys_kernel, out_shape=(shape(rows, width), shape(rows, 2...  3.36 us
    ppermute x9, waiting for transfers between devices, exchanged(): lax.ppermute(block, axis, [(i, partner % size) for i, partner in enumerat...  2.82 us
  transfers between devices with their start and end apart: 10, of which 2 were waited for; matrix products, arithmetic and copies ran while one was open for 0% of the time, Pallas kernels for 5%

profile of v4, /device:TPU:2, one launch (start us, length us, event | category | flops | bytes accessed | tf_op | source)
XLA Modules:
  0.0 108.8 jit_solution(11834125216291149074)
XLA Ops:
  0.6 0.6 add_bitcast_fusion.places.refs_0_
  1.3 3.4 %shard_map.138 = (bf16[128,512]{1,0:T(8,128)(2,1)}, bf16[128,1024]{1,0:T(8,128)(2,1)}, bf16[16,1024]{1,0:T(8,128)(2,1)}, bf16[16,1024]{1,0:T(8,128)(2,1)}, bf16[...) custom-call(s32[1,2]{1,0:T(1,128)} %add_bitcast_fusion.places.refs_0_, bf16[128,512]{1,0:T(8,128)(2,1)} %features.3, ...), custom_call_target="tpu_custom_call" | custom-call | flops 1200000000 | bytes 3000000 | tf_op jit(solution)/shard_map/pallas_call | solution.py:130
  4.6 3.4 %collective-permute-start = (bf16[16,1024]{1,0:T(8,128)(2,1)}, bf16[16,1024]{1,0:T(8,128)(2,1)S(1)}, u32[]{:S(2)}, u32[]{:S(2)}) collective-permute-start(bf16[16,1024]{1,0:T(8,128)(2,1)} %get-tuple-element.27), channel_id=1, source_target_pairs={{0,504},{8,16},{16,8},{24,32},{32,24},{40,48},{48,40},{56,64},{64,... | collective-permute-start | bytes 98312 | tf_op jit(solution)/shard_map/ppermute | solution.py:348
  8.0 4.7 %collective-permute-start.1 = (bf16[16,1024]{1,0:T(8,128)(2,1)}, bf16[16,1024]{1,0:T(8,128)(2,1)S(1)}, u32[]{:S(2)}, u32[]{:S(2)}) collective-permute-start(bf16[16,1024]{1,0:T(8,128)(2,1)} %get-tuple-element.28), channel_id=1, source_target_pairs={{0,7},{1,2},{2,1},{3,4},{4,3},{5,6},{6,5},{7,0},{8,15},{9,10},{10,... | collective-permute-start | bytes 98312 | tf_op jit(solution)/shard_map/ppermute | solution.py:348
  12.7 14.8 %collective-permute-start.2 = (bf16[16,1024]{1,0:T(8,128)(2,1)}, bf16[16,1024]{1,0:T(8,128)(2,1)S(1)}, u32[]{:S(2)}, u32[]{:S(2)}) collective-permute-start(bf16[16,1024]{1,0:T(8,128)(2,1)} %get-tuple-element.29), channel_id=1, source_target_pairs={{0,8},{8,0},{16,24},{24,16},{32,40},{40,32},{48,56},{56,48},{64,72... | collective-permute-start | bytes 98312 | tf_op jit(solution)/shard_map/ppermute | solution.py:348
  27.5 2.4 %collective-permute-start.3 = (bf16[16,1024]{1,0:T(8,128)(2,1)}, bf16[16,1024]{1,0:T(8,128)(2,1)S(1)}, u32[]{:S(2)}, u32[]{:S(2)}) collective-permute-start(bf16[16,1024]{1,0:T(8,128)(2,1)} %get-tuple-element.30), channel_id=1, source_target_pairs={{0,1},{1,0},{2,3},{3,2},{4,5},{5,4},{6,7},{7,6},{8,9},{9,8},{10,11... | collective-permute-start | bytes 98312 | tf_op jit(solution)/shard_map/ppermute | solution.py:348
  29.9 0.9 copy-done.14
  30.8 1.7 %shard_map.139 = (bf16[128,512]{1,0:T(8,128)(2,1)S(1)}, bf16[128,512]{1,0:T(8,128)(2,1)S(1)}, f32[192,128]{1,0:T(8,128)S(1)}) custom-call(s32[1,2]{1,0:T(1,128)S(1)} %copy-done.11, bf16[128,512]{1,0:T(8,128)(2,1)S(1)} %copy-done.14, bf16[3,512,512]{2,1,0:T(8,128)(2,1)S(1)} %copy-done, bf16[512,512]{1,0:T(8,128)(2,1)S(1)} %copy-done.1, ...), custom_call_target="tpu_custom_call" | custom-call | flops 2000000000 | bytes 5000000 | tf_op jit(solution)/shard_map/pallas_call | solution.py:58
  32.6 3.9 %shard_map.140 = (bf16[272,1024]{1,0:T(8,128)(2,1)S(1)}, f32[128,1024]{1,0:T(8,128)S(1)}, bf16[16,1024]{1,0:T(8,128)(2,1)S(1)}, bf16[16,1024]{1,0:T(8,128)(2,1)S(1)}, bf16[16,1024]{1,0:T(8,128)(2,1)S(1)}) custom-call(bf16[128,512]{1,0:T(8,128)(2,1)S(1)} %get-tuple-element.23.refs_0_, bf16[128,1024]{1,0:T(8,128)(2,1)S(1)} %copy-done.13, ...), custom_call_target="tpu_custom_call" | custom-call | flops 3200000000 | bytes 8000000 | tf_op jit(solution)/shard_map/pallas_call | solution.py:58
  36.4 0.0 copy-start.9
  36.4 0.0 copy-start.10
  36.5 0.0 copy-start.12
  36.5 2.1 %collective-permute-start.7 = (bf16[272,1024]{1,0:T(8,128)(2,1)S(1)}, bf16[272,1024]{1,0:T(8,128)(2,1)S(1)}, u32[]{:S(2)}, u32[]{:S(2)}) collective-permute-start(bf16[272,1024]{1,0:T(8,128)(2,1)S(1)} %get-tuple-element.31.sent.refs_2_.refs_1_), channel_id=1, source_target_pairs={{0,1},{1,0},{2,3},{3,2},{4,5},{5,4},{6,7},{7,6},{8,9},{9,8},{10,11... | collective-permute-start | bytes 1671176 | tf_op jit(solution)/shard_map/ppermute | solution.py:348
  38.6 1.9 %collective-permute-start.4 = (bf16[16,1024]{1,0:T(8,128)(2,1)S(1)}, bf16[16,1024]{1,0:T(8,128)(2,1)S(1)}, u32[]{:S(2)}, u32[]{:S(2)}) collective-permute-start(bf16[16,1024]{1,0:T(8,128)(2,1)S(1)} %get-tuple-element.33), channel_id=1, source_target_pairs={{0,504},{8,16},{16,8},{24,32},{32,24},{40,48},{48,40},{56,64},{64,... | collective-permute-start | bytes 98312 | tf_op jit(solution)/shard_map/ppermute | solution.py:348
  40.5 5.1 %collective-permute-start.5 = (bf16[16,1024]{1,0:T(8,128)(2,1)S(1)}, bf16[16,1024]{1,0:T(8,128)(2,1)S(1)}, u32[]{:S(2)}, u32[]{:S(2)}) collective-permute-start(bf16[16,1024]{1,0:T(8,128)(2,1)S(1)} %get-tuple-element.34), channel_id=1, source_target_pairs={{0,7},{1,2},{2,1},{3,4},{4,3},{5,6},{6,5},{7,0},{8,15},{9,10},{10,... | collective-permute-start | bytes 98312 | tf_op jit(solution)/shard_map/ppermute | solution.py:348
  45.6 3.0 %collective-permute-start.6 = (bf16[16,1024]{1,0:T(8,128)(2,1)S(1)}, bf16[16,1024]{1,0:T(8,128)(2,1)S(1)}, u32[]{:S(2)}, u32[]{:S(2)}) collective-permute-start(bf16[16,1024]{1,0:T(8,128)(2,1)S(1)} %get-tuple-element.35), channel_id=1, source_target_pairs={{0,8},{8,0},{16,24},{24,16},{32,40},{40,32},{48,56},{56,48},{64,72... | collective-permute-start | bytes 98312 | tf_op jit(solution)/shard_map/ppermute | solution.py:348
  48.6 2.8 %collective-permute-done.6.refs_5_ = bf16[16,1024]{1,0:T(8,128)(2,1)S(1)} collective-permute-done((bf16[16,1024]{1,0:T(8,128)(2,1)S(1)}, bf16[16,1024]{1,0:T(8,128)(2,1)S(1)}, u32[]{:S(2)}, u32[]{:S(2)}) %collective-permute-start.6) | collective-permute-done | bytes 32800 | tf_op jit(solution)/shard_map/ppermute | solution.py:348
  51.4 1.2 %shard_map.142.late.refs_2_ = bf16[128,1024]{1,0:T(8,128)(2,1)S(1)} custom-call(s32[1,2]{1,0:T(1,128)S(1)} %copy-done.11, f32[128,1024]{1,0:T(8,128)S(1)} %get-tuple-element.32.refs_1_, s32[4,16]{1,0:T(4,128)S(1)} %copy-done.7, bf16[16,1024]{1,0:T(8,128)(2,1)S(1)} %collective-permute-done.4.refs_3_, bf16[16,1024]{1,0:T(8,128)(2,1)S(1)} %collective-permute-done.5.refs_4_, ...), custom_call_target="tpu_custom_call" | custom-call | flops 800000000 | bytes 2000000 | tf_op jit(solution)/shard_map/pallas_call | solution.py:58
  52.6 1.9 %collective-permute-start.8 = (bf16[128,1024]{1,0:T(8,128)(2,1)S(1)}, bf16[128,1024]{1,0:T(8,128)(2,1)S(1)}, u32[]{:S(2)}, u32[]{:S(2)}) collective-permute-start(bf16[128,1024]{1,0:T(8,128)(2,1)S(1)} %shard_map.142.late.refs_2_), channel_id=1, source_target_pairs={{0,1},{1,0},{2,3},{3,2},{4,5},{5,4},{6,7},{7,6},{8,9},{9,8},{10,11... | collective-permute-start | bytes 786440 | tf_op jit(solution)/shard_map/ppermute | solution.py:348
  54.6 1.7 %shard_map.144 = (bf16[768,768]{1,0:T(8,128)(2,1)S(1)}, f32[256,512]{1,0:T(8,128)S(1)}) custom-call(s32[1,2]{1,0:T(1,128)S(1)} %copy-done.11, s32[1,2]{1,0:T(1,128)S(1)} %copy-done.12, bf16[272,1024]{1,0:T(8,128)(2,1)S(1)} %get-tuple-element.31.sent.refs_2_.refs_1_, s32[768,1]{1,0:T(8,128)S(1)} %copy-done.9, s32[256,1]{1,0:T(8,128)S(1)} %copy-done.10, ...), custom_call_target="tpu_custom_call" | custom-call | flops 1200000000 | bytes 3000000 | tf_op jit(solution)/shard_map/pallas_call | solution.py:58
  56.3 1.1 %shard_map.145 = f32[4,272,512]{2,1,0:T(8,128)S(1)} custom-call(bf16[768,768]{1,0:T(8,128)(2,1)S(1)} %get-tuple-element.36.refs_0_, bf16[272,1024]{1,0:T(8,128)(2,1)S(1)} %get-tuple-element.31.sent.refs_2_.refs_1_, bf16[128,1024]{1,0:T(8,128)(2,1)S(1)} %shard_map.142.late.refs_2_, f32[256,512]{1,0:T(8,128)S(1)} %get-tuple-element.37.refs_3_, ...), custom_call_target="tpu_custom_call" | custom-call | flops 1200000000 | bytes 3000000 | tf_op jit(solution)/shard_map/pallas_call | solution.py:58
  57.4 0.3 convert_element_type.6
  57.7 19.9 %all_to_all.10 = f16[4,272,512]{2,1,0:T(8,128)(2,1)S(1)} all-to-all(f16[4,272,512]{2,1,0:T(8,128)(2,1)S(1)} %convert_element_type.6), channel_id=1, replica_groups=mesh['yh'=2,'z'=8,'x'=4,'yl'=4,'core'=2] {'x'}, dimensions={0} | all-to-all | bytes 2228224 | tf_op jit(solution)/shard_map/all_to_all | solution.py:433
  77.6 0.3 convert_element_type.7.refs_0_
  77.9 1.4 %shard_map.146 = f32[64,4,512]{2,1,0:T(4,128)} custom-call(f32[4,272,512]{2,1,0:T(8,128)S(1)} %convert_element_type.7.refs_0_), custom_call_target="tpu_custom_call" | custom-call | flops 800000000 | bytes 2000000 | tf_op jit(solution)/shard_map/pallas_call | solution.py:58
  79.3 9.2 %all-to-all-start.1 = ((f32[64,4,512]{2,1,0:T(4,128)}), f32[64,4,512]{2,1,0:T(4,128)S(1)}, u32[]{:S(2)}, u32[]{:S(2)}) async-start(f32[64,4,512]{2,1,0:T(4,128)} %shard_map.146), calls=%async_computation.1 | async-start | bytes 1048576 | tf_op jit(solution)/shard_map/all_to_all | solution.py:443
  88.5 0.9 copy-done.2
  89.4 0.9 shard_map.141
  90.3 0.0 copy-done.4
  90.3 1.4 %shard_map.143 = f32[128,512]{1,0:T(8,128)} custom-call(bf16[128,512]{1,0:T(8,128)(2,1)S(1)} %copy-done.2, bf16[128,512]{1,0:T(8,128)(2,1)S(1)} %copy-done.4, f32[1,512]{1,0:T(1,128)S(1)} %bitcast.12, bf16[272,1024]{1,0:T(8,128)(2,1)S(1)} %get-tuple-element.31.sent.refs_2_.refs_1_, bf16[128,1024]{1,0:T(8,128)(2,1)S(1)} %shard_map.142.late.refs_2_, ...), custom_call_target="tpu_custom_call" | custom-call | flops 1200000000 | bytes 3000000 | tf_op jit(solution)/shard_map/pallas_call | solution.py:58
  91.8 16.2 %all-to-all-done.1.refs_0_ = f32[64,4,512]{2,1,0:T(4,128)S(1)} async-done(((f32[64,4,512]{2,1,0:T(4,128)}), f32[64,4,512]{2,1,0:T(4,128)S(1)}, u32[]{:S(2)}, u32[]{:S(2)}) %all-to-all-start.1) | async-done | bytes 524320 | tf_op jit(solution)/shard_map/all_to_all | solution.py:443
  108.0 0.8 shard_map.147
  (32 shorter events, 0.1 us)
Async XLA Ops:
  1.2 28.6 %copy-start = (bf16[3,512,512]{2,1,0:T(8,128)(2,1)S(1)}, bf16[3,512,512]{2,1,0:T(8,128)(2,1)}, u32[]{:S(2)}) copy-start(bf16[3,512,512]{2,1,0:T(8,128)(2,1)} %weight.3) | copy-start | bytes 4718596
  1.2 28.6 %copy-start.1 = (bf16[512,512]{1,0:T(8,128)(2,1)S(1)}, bf16[512,512]{1,0:T(8,128)(2,1)}, u32[]{:S(2)}) copy-start(bf16[512,512]{1,0:T(8,128)(2,1)} %output_weight.3) | copy-start | bytes 1572868
  1.2 28.6 %copy-start.3 = (bf16[128,512]{1,0:T(8,128)(2,1)S(1)}, bf16[128,512]{1,0:T(8,128)(2,1)}, u32[]{:S(2)}) copy-start(bf16[128,512]{1,0:T(8,128)(2,1)} %cotangent.3) | copy-start | bytes 393220
  1.2 28.6 %copy-start.5 = (s32[128,64]{0,1:T(8,128)S(1)}, s32[128,64]{0,1:T(8,128)}, u32[]{:S(2)}) copy-start(s32[128,64]{0,1:T(8,128)} %param.16) | copy-start | bytes 98308
  1.2 28.6 %copy-start.6 = (s32[128,64]{0,1:T(8,128)S(1)}, s32[128,64]{0,1:T(8,128)}, u32[]{:S(2)}) copy-start(s32[128,64]{0,1:T(8,128)} %param.17) | copy-start | bytes 98308
  1.2 28.6 %copy-start.11 = (s32[1,2]{1,0:T(1,128)S(1)}, s32[1,2]{1,0:T(1,128)}, u32[]{:S(2)}) copy-start(s32[1,2]{1,0:T(1,128)} %add_bitcast_fusion.places.refs_0_) | copy-start | bytes 28
  4.6 27.9 %collective-permute-start = (bf16[16,1024]{1,0:T(8,128)(2,1)}, bf16[16,1024]{1,0:T(8,128)(2,1)S(1)}, u32[]{:S(2)}, u32[]{:S(2)}) collective-permute-start(bf16[16,1024]{1,0:T(8,128)(2,1)} %get-tuple-element.27), channel_id=1, source_target_pairs={{0,504},{8,16},{16,8},{24,32},{32,24},{40,48},{48,40},{56,64},{64,... | collective-permute-start | bytes 98312 | tf_op jit(solution)/shard_map/ppermute | solution.py:348
  8.0 24.5 %collective-permute-start.1 = (bf16[16,1024]{1,0:T(8,128)(2,1)}, bf16[16,1024]{1,0:T(8,128)(2,1)S(1)}, u32[]{:S(2)}, u32[]{:S(2)}) collective-permute-start(bf16[16,1024]{1,0:T(8,128)(2,1)} %get-tuple-element.28), channel_id=1, source_target_pairs={{0,7},{1,2},{2,1},{3,4},{4,3},{5,6},{6,5},{7,0},{8,15},{9,10},{10,... | collective-permute-start | bytes 98312 | tf_op jit(solution)/shard_map/ppermute | solution.py:348
  12.7 19.8 %collective-permute-start.2 = (bf16[16,1024]{1,0:T(8,128)(2,1)}, bf16[16,1024]{1,0:T(8,128)(2,1)S(1)}, u32[]{:S(2)}, u32[]{:S(2)}) collective-permute-start(bf16[16,1024]{1,0:T(8,128)(2,1)} %get-tuple-element.29), channel_id=1, source_target_pairs={{0,8},{8,0},{16,24},{24,16},{32,40},{40,32},{48,56},{56,48},{64,72... | collective-permute-start | bytes 98312 | tf_op jit(solution)/shard_map/ppermute | solution.py:348
  27.5 5.1 %collective-permute-start.3 = (bf16[16,1024]{1,0:T(8,128)(2,1)}, bf16[16,1024]{1,0:T(8,128)(2,1)S(1)}, u32[]{:S(2)}, u32[]{:S(2)}) collective-permute-start(bf16[16,1024]{1,0:T(8,128)(2,1)} %get-tuple-element.30), channel_id=1, source_target_pairs={{0,1},{1,0},{2,3},{3,2},{4,5},{5,4},{6,7},{7,6},{8,9},{9,8},{10,11... | collective-permute-start | bytes 98312 | tf_op jit(solution)/shard_map/ppermute | solution.py:348
  29.9 0.9 copy-start.14
  30.8 1.8 %copy-start.13 = (bf16[128,1024]{1,0:T(8,128)(2,1)S(1)}, bf16[128,1024]{1,0:T(8,128)(2,1)}, u32[]{:S(2)}) copy-start(bf16[128,1024]{1,0:T(8,128)(2,1)} %get-tuple-element.24.refs_1_) | copy-start | bytes 786436
  32.6 18.9 %copy-start.7 = (s32[4,16]{1,0:T(4,128)S(1)}, s32[4,16]{1,0:T(4,128)}, u32[]{:S(2)}) copy-start(s32[4,16]{1,0:T(4,128)} %refs_2_.1) | copy-start | bytes 772
  36.4 18.1 %copy-start.9 = (s32[768,1]{1,0:T(8,128)S(1)}, s32[768,1]{1,0:T(8,128)}, u32[]{:S(2)}) copy-start(s32[768,1]{1,0:T(8,128)} %constant.29.clone.refs_3_) | copy-start | bytes 9220
  36.4 18.1 %copy-start.10 = (s32[256,1]{1,0:T(8,128)S(1)}, s32[256,1]{1,0:T(8,128)}, u32[]{:S(2)}) copy-start(s32[256,1]{1,0:T(8,128)} %constant.30.clone.refs_4_) | copy-start | bytes 3076
  36.5 18.1 %copy-start.12 = (s32[1,2]{1,0:T(1,128)S(1)}, s32[1,2]{1,0:T(1,128)}, u32[]{:S(2)}) copy-start(s32[1,2]{1,0:T(1,128)} %constant.28.clone.refs_1_) | copy-start | bytes 28
  36.5 15.0 %collective-permute-start.7 = (bf16[272,1024]{1,0:T(8,128)(2,1)S(1)}, bf16[272,1024]{1,0:T(8,128)(2,1)S(1)}, u32[]{:S(2)}, u32[]{:S(2)}) collective-permute-start(bf16[272,1024]{1,0:T(8,128)(2,1)S(1)} %get-tuple-element.31.sent.refs_2_.refs_1_), channel_id=1, source_target_pairs={{0,1},{1,0},{2,3},{3,2},{4,5},{5,4},{6,7},{7,6},{8,9},{9,8},{10,11... | collective-permute-start | bytes 1671176 | tf_op jit(solution)/shard_map/ppermute | solution.py:348
  38.6 10.0 %collective-permute-start.4 = (bf16[16,1024]{1,0:T(8,128)(2,1)S(1)}, bf16[16,1024]{1,0:T(8,128)(2,1)S(1)}, u32[]{:S(2)}, u32[]{:S(2)}) collective-permute-start(bf16[16,1024]{1,0:T(8,128)(2,1)S(1)} %get-tuple-element.33), channel_id=1, source_target_pairs={{0,504},{8,16},{16,8},{24,32},{32,24},{40,48},{48,40},{56,64},{64,... | collective-permute-start | bytes 98312 | tf_op jit(solution)/shard_map/ppermute | solution.py:348
  40.5 8.1 %collective-permute-start.5 = (bf16[16,1024]{1,0:T(8,128)(2,1)S(1)}, bf16[16,1024]{1,0:T(8,128)(2,1)S(1)}, u32[]{:S(2)}, u32[]{:S(2)}) collective-permute-start(bf16[16,1024]{1,0:T(8,128)(2,1)S(1)} %get-tuple-element.34), channel_id=1, source_target_pairs={{0,7},{1,2},{2,1},{3,4},{4,3},{5,6},{6,5},{7,0},{8,15},{9,10},{10,... | collective-permute-start | bytes 98312 | tf_op jit(solution)/shard_map/ppermute | solution.py:348
  45.6 5.8 %collective-permute-start.6 = (bf16[16,1024]{1,0:T(8,128)(2,1)S(1)}, bf16[16,1024]{1,0:T(8,128)(2,1)S(1)}, u32[]{:S(2)}, u32[]{:S(2)}) collective-permute-start(bf16[16,1024]{1,0:T(8,128)(2,1)S(1)} %get-tuple-element.35), channel_id=1, source_target_pairs={{0,8},{8,0},{16,24},{24,16},{32,40},{40,32},{48,56},{56,48},{64,72... | collective-permute-start | bytes 98312 | tf_op jit(solution)/shard_map/ppermute | solution.py:348
  52.6 3.6 %collective-permute-start.8 = (bf16[128,1024]{1,0:T(8,128)(2,1)S(1)}, bf16[128,1024]{1,0:T(8,128)(2,1)S(1)}, u32[]{:S(2)}, u32[]{:S(2)}) collective-permute-start(bf16[128,1024]{1,0:T(8,128)(2,1)S(1)} %shard_map.142.late.refs_2_), channel_id=1, source_target_pairs={{0,1},{1,0},{2,3},{3,2},{4,5},{5,4},{6,7},{7,6},{8,9},{9,8},{10,11... | collective-permute-start | bytes 786440 | tf_op jit(solution)/shard_map/ppermute | solution.py:348
  79.3 28.7 %all-to-all-start.1 = ((f32[64,4,512]{2,1,0:T(4,128)}), f32[64,4,512]{2,1,0:T(4,128)S(1)}, u32[]{:S(2)}, u32[]{:S(2)}) async-start(f32[64,4,512]{2,1,0:T(4,128)} %shard_map.146), calls=%async_computation.1 | async-start | bytes 1048576 | tf_op jit(solution)/shard_map/all_to_all | solution.py:443
  88.5 0.9 copy-start.2
  89.4 0.9 copy-start.4
  89.4 0.9 copy-start.8

commit v5 on v4

--- a/solution.py
+++ b/solution.py
@@ -33,10 +33,9 @@
     return high, (values - high.astype(F32)).astype(BF16)
 
 
-def call(kernel, out_shapes, args, us, scalars=0, moved=0, scratch=()):
+def call(kernel, out_shapes, args, us, moved=0, scratch=()):
     held = len(args) - moved
-    specs = [pl.BlockSpec(memory_space=pltpu.SMEM)] * scalars
-    specs += [pl.BlockSpec(memory_space=pltpu.VMEM)] * (held - scalars)
+    specs = [pl.BlockSpec(memory_space=pltpu.VMEM)] * held
     specs += [pl.BlockSpec(memory_space=pl.ANY)] * moved
     scratch = list(scratch)
     if moved:
@@ -76,11 +75,15 @@
     return lax.rsqrt(jnp.mean(values * values, axis=-1, keepdims=True) + EPSILON)
 
 
+def here():
+    return lax.axis_index("core"), lax.rem(lax.axis_index("x"), 2)
+
+
 def listed(places, send_rows, index, rows):
     first = 2 * (index // 2)
     at_even, at_odd = first + index % 2, first + 1 - index % 2
     chosen = jnp.where(
-        places[0, index // 2] == 0,
+        places[index // 2] == 0,
         send_rows[at_even : at_even + 1, :],
         send_rows[at_odd : at_odd + 1, :],
     )
@@ -89,7 +92,7 @@
 
 
 def keys_kernel(
-    places, features_hbm, gain_hbm, weight_hbm, send_rows_hbm,
+    features_hbm, gain_hbm, weight_hbm, send_rows_hbm,
     first, key_values, band0, band1, band2, band3,
     features, gain, weight, send_rows, arrived,
 ):
@@ -118,20 +121,20 @@
         key_values[:, part * width : (part + 1) * width] = dot(normed, weight[part]).astype(BF16)
     copies[4].wait()
     table = key_values[...]
+    places = here()
     for index, band in enumerate((band0, band1, band2, band3)):
         chosen = listed(places, send_rows, index, features.shape[0])
         band[...] = dot(chosen, table, ((0,), (0,))).astype(BF16)
 
 
-def keys_call(places, features, gain, weight, send_rows):
+def keys_call(features, gain, weight, send_rows):
     rows, width = features.shape
     band = shape(send_rows.shape[1], 2 * width)
     vmem = pl.BlockSpec(memory_space=pltpu.VMEM)
     return pl.pallas_call(
         keys_kernel,
         out_shape=(shape(rows, width), shape(rows, 2 * width), band, band, band, band),
-        in_specs=[pl.BlockSpec(memory_space=pltpu.SMEM)]
-        + [pl.BlockSpec(memory_space=pltpu.HBM)] * 4,
+        in_specs=[pl.BlockSpec(memory_space=pltpu.HBM)] * 4,
         out_specs=(vmem,) * 6,
         scratch_shapes=[
             pltpu.VMEM(features.shape, BF16),
@@ -140,15 +143,22 @@
             pltpu.VMEM(send_rows.shape, jnp.int32),
             pltpu.SemaphoreType.DMA((5,)),
         ],
+        compiler_params=pltpu.CompilerParams(vmem_limit_bytes=VMEM_BYTES),
         cost_estimate=pl.CostEstimate(
             flops=1200000000, bytes_accessed=3000000, transcendentals=0
         ),
-    )(places, features, gain, weight, send_rows)
+    )(
+        *(
+            pltpu.with_memory_space_constraint(array, pltpu.HBM)
+            for array in (features, gain, weight, send_rows)
+        )
+    )
 
 
 def queries_kernel(
-    places, first, weight, output_weight, cotangent, neighbours, live, queries, grad_mixed, counts
+    first, weight, output_weight, cotangent, neighbours, live, queries, grad_mixed, counts
 ):
+    places = here()
     queries[...] = dot(first[...], weight[0]).astype(BF16)
     grad_mixed[...] = dot(cotangent[...], output_weight[...], ((1,), (1,))).astype(BF16)
     slots = jnp.where(live[...] > 0, neighbours[...], -1)
@@ -158,7 +168,7 @@
     swapped = jnp.where(
         entries < rows,
         0,
-        jnp.where(entries < rows + 2 * cap, 1 - places[0, 0], 1 - places[0, 1]),
+        jnp.where(entries < rows + 2 * cap, 1 - places[0], 1 - places[1]),
     )
     entries = jnp.bitwise_xor(entries, swapped * cap)
     total = jnp.zeros(entries.shape, F32)
@@ -233,10 +243,11 @@
     layer_output[...] = (features[...].astype(F32) + dot(mixed, output_weight[...])).astype(BF16)
 
 
-def chosen_kernel(places, per_core, sent, feature_of, cell_of, partner, left, grad_output):
+def chosen_kernel(per_core, sent, feature_of, cell_of, partner, left, grad_output):
     width, rows = sent.shape[1] // 2, left.shape[1] // 6
+    core = lax.axis_index("core")
     columns = lax.broadcasted_iota(jnp.int32, (feature_of.shape[0], width), 1)
-    target = feature_of[...] + places[0, 0] * per_core[0, 0]
+    target = feature_of[...] + core * per_core[0]
     feature = jnp.bitwise_and(target, width - 1)
     chosen = (feature == columns).astype(F32).astype(BF16)
     part = jnp.right_shift(target, width.bit_length() - 1)
@@ -246,7 +257,7 @@
             at = (2 * piece + index) * rows
             left[:, at : at + rows] = jnp.where(part == piece, picked, 0.0).astype(BF16)
     columns = lax.broadcasted_iota(jnp.int32, (cell_of.shape[0], width), 1)
-    target = cell_of[...] + places[0, 0] * per_core[0, 1]
+    target = cell_of[...] + core * per_core[1]
     chosen = (target == columns).astype(F32).astype(BF16)
     total = None
     for source in (sent, partner):
@@ -256,8 +267,9 @@
     grad_output[...] = total
 
 
-def merge_kernel(places, own, send_rows, back3, back1, back2, partner, grad_keys_values):
+def merge_kernel(own, send_rows, back3, back1, back2, partner, grad_keys_values):
     rows = own.shape[0]
+    places = here()
     total = own[...]
     for index, back in enumerate((partner[2 * rows :, :], back1, back2, back3)):
         total = total + dot(listed(places, send_rows, index, rows), back[...])
@@ -313,6 +325,7 @@
 
 def near_kernel(both, summed):
     far, each = summed.shape[:2]
+    width = both.shape[2]
     first_row = 0
     for part, per in enumerate((each - each // 4, each // 4)):
         at = both.shape[1] - HEADER + part * (HEADER // 2)
@@ -321,25 +334,32 @@
             scale = jnp.exp2(both[index, at : at + 1, :] - HEADROOM)
             values = both[index, first_row * far : (first_row + per) * far, :] * scale
             total = values if total is None else total + values
+        power = exponent(total)
+        total = total * jnp.exp2(HEADROOM - power)
         for row in range(per):
-            summed[:, first_row + row, :] = total[row * far : (row + 1) * far, :]
+            summed[:, first_row + row, :width] = total[row * far : (row + 1) * far, :]
+            summed[:, first_row + row, width:] = jnp.broadcast_to(
+                power, (far, summed.shape[2] - width)
+            )
         first_row += per
 
 
 def far_kernel(scale, parts, grad_project, grad_output):
-    total = jnp.sum(parts[...], axis=0) * scale
     lanes = grad_project.shape[1]
-    per_row = total.shape[1] // lanes
+    per_row = (parts.shape[2] - lanes) // lanes
+    width = per_row * lanes
+    factors = jnp.exp2(parts[:, :, width:] - HEADROOM) * scale
     project_rows = grad_project.shape[0] // per_row
-    for row in range(total.shape[0]):
-        for piece in range(per_row):
-            values = total[row : row + 1, piece * lanes : (piece + 1) * lanes]
+    for piece in range(per_row):
+        values = parts[:, :, piece * lanes : (piece + 1) * lanes]
+        total = jnp.sum(values * factors, axis=0)
+        for row in range(total.shape[0]):
             if row < project_rows:
                 at = row * per_row + piece
-                grad_project[at : at + 1, :] = values
+                grad_project[at : at + 1, :] = total[row : row + 1, :]
             else:
                 at = (row - project_rows) * per_row + piece
-                grad_output[at : at + 1, :] = values
+                grad_output[at : at + 1, :] = total[row : row + 1, :]
 
 
 def exchanged(block, axis, index):
@@ -356,7 +376,7 @@
     def rows(per):
         return (ids[:, None, :] * per + np.arange(per)[None, :, None]).reshape(-1, 1)
 
-    per_core = np.array([[per_project, per_output]], np.int32)
+    per_core = (per_project, per_output)
     return rows(per_project).astype(np.int32), rows(per_output).astype(np.int32), per_core
 
 
@@ -367,18 +387,15 @@
     devices = math.prod(sizes.values())
     scale = float(rows * devices) ** -0.5
     gain = gain.reshape(1, width)
-    core = lax.axis_index("core")
-    places = jnp.stack([core, lax.axis_index("x") % 2]).astype(jnp.int32).reshape(1, 2)
     band = shape(cap, 2 * width)
-    first, key_values, *bands = keys_call(places, features, gain, weight, send_rows)
+    first, key_values, *bands = keys_call(features, gain, weight, send_rows)
     steps = ((TENSOR, 0), (TENSOR, 1), (CELLS, 0), (CELLS, 1))
     received = [exchanged(bands[index], *steps[index]) for index in (3, 1, 2, 0)]
     queries, grad_mixed, counts = call(
         queries_kernel,
         (shape(rows, width), shape(rows, width), shape(rows + 4 * cap, rows, dtype=F32)),
-        (places, first, weight, output_weight, cotangent, neighbours.T, live.T),
+        (first, weight, output_weight, cotangent, neighbours.T, live.T),
         5,
-        scalars=1,
     )
     sent, own, *backs = call(
         attention_kernel,
@@ -406,19 +423,17 @@
     near = sizes["x"]
     far = devices // (2 * near)
     left, grad_output = call(
-        chosen_kernel,
+        functools.partial(chosen_kernel, per_core),
         (shape(3 * width // 2, 6 * rows), shape(width // 2, width, dtype=F32)),
-        (places, per_core, sent, feature_of, cell_of, partner),
+        (sent, feature_of, cell_of, partner),
         3,
-        scalars=2,
         moved=1,
     )
     grad_keys_values = call(
         merge_kernel,
         shape(rows, 2 * width),
-        (places, own, send_rows, *returned, partner),
+        (own, send_rows, *returned, partner),
         2,
-        scalars=1,
         moved=4,
     )
     partner_grads = exchanged(grad_keys_values, *steps[0])
@@ -438,9 +453,9 @@
         3,
     )
     parts = call(
-        near_kernel, shape(far, 4 * width // devices, width, dtype=F32), (both,), 2, moved=1
-    )
-    parts = lax.all_to_all(parts, FAR, 0, 0, tiled=True)
+        near_kernel, shape(far, 4 * width // devices, width + 128, dtype=F32), (both,), 2, moved=1
+    )
+    parts = lax.all_to_all(parts.astype(jnp.float16), FAR, 0, 0, tiled=True).astype(F32)
     grad_project, grad_output = call(
         functools.partial(far_kernel, scale),
         tuple(shape(count * width * width // devices // 128, 128, dtype=F32) for count in (3, 1)),

time: 109 us -> 102 us (0.936)
  the two profiles are of different devices: /device:TPU:2 before, /device:TPU:8 now
where the time goes in v5:
time: 102 us; the launch traced here: 101 us
  starting transfers between devices  48.6 us (48%)
  blocking collectives  18.8 us (18%)
  waiting for transfers between devices  17.5 us (17%)
  Pallas kernels  14.1 us (14%)
  other arithmetic  1.5 us (1%)
    ppermute x9, starting transfers between devices, exchanged(): lax.ppermute(block, axis, [(i, partner % size) for i, partner in enumerat...  39 us
    all_to_all x1, blocking collectives, body(): lax.all_to_all(both.astype(jnp.float16), 'x', 0, 0, tiled=True).astype(F32)  18.8 us
    all_to_all x1, waiting for transfers between devices, body(): lax.all_to_all(parts.astype(jnp.float16), FAR, 0, 0, tiled=True).astype(F32)  12.8 us
    pallas_call x9, Pallas kernels, call(): pl.pallas_call(moving if moved else kernel, out_shape=out_shapes, in_spec...  12 us
    all_to_all x1, starting transfers between devices, body(): lax.all_to_all(parts.astype(jnp.float16), FAR, 0, 0, tiled=True).astype(F32)  9.59 us
    ppermute x9, waiting for transfers between devices, exchanged(): lax.ppermute(block, axis, [(i, partner % size) for i, partner in enumerat...  4.66 us
    pallas_call x1, Pallas kernels, keys_call(): pl.pallas_call(keys_kernel, out_shape=(shape(rows, width), shape(rows, 2...  2.09 us
  transfers between devices with their start and end apart: 10, of which 5 were waited for; matrix products, arithmetic and copies ran while one was open for 0% of the time, Pallas kernels for 5%

profile of v5, /device:TPU:8, one launch (start us, length us, event | category | flops | bytes accessed | tf_op | source)
XLA Modules:
  0.0 101.5 jit_solution(4339389342835002399)
XLA Ops:
  0.7 2.1 %shard_map.129 = (bf16[128,512]{1,0:T(8,128)(2,1)S(1)}, bf16[128,1024]{1,0:T(8,128)(2,1)S(1)}, bf16[16,1024]{1,0:T(8,128)(2,1)S(1)}, bf16[16,1024]{1,0:T(8,128)(...) custom-call(bf16[128,512]{1,0:T(8,128)(2,1)} %features.3, f32[1,512]{1,0:T(1,128)} %bitcast.7, ...), custom_call_target="tpu_custom_call" | custom-call | flops 1200000000 | bytes 3000000 | tf_op jit(solution)/shard_map/pallas_call | solution.py:134
  2.8 17.5 %collective-permute-start = (bf16[16,1024]{1,0:T(8,128)(2,1)S(1)}, bf16[16,1024]{1,0:T(8,128)(2,1)S(1)}, u32[]{:S(2)}, u32[]{:S(2)}) collective-permute-start(bf16[16,1024]{1,0:T(8,128)(2,1)S(1)} %get-tuple-element.27), channel_id=1, source_target_pairs={{0,504},{8,16},{16,8},{24,32},{32,24},{40,48},{48,40},{56,64},{64,... | collective-permute-start | bytes 98312 | tf_op jit(solution)/shard_map/ppermute | solution.py:368
  20.3 2.4 %collective-permute-start.1 = (bf16[16,1024]{1,0:T(8,128)(2,1)S(1)}, bf16[16,1024]{1,0:T(8,128)(2,1)S(1)}, u32[]{:S(2)}, u32[]{:S(2)}) collective-permute-start(bf16[16,1024]{1,0:T(8,128)(2,1)S(1)} %get-tuple-element.28), channel_id=1, source_target_pairs={{0,7},{1,2},{2,1},{3,4},{4,3},{5,6},{6,5},{7,0},{8,15},{9,10},{10,... | collective-permute-start | bytes 98312 | tf_op jit(solution)/shard_map/ppermute | solution.py:368
  22.7 1.9 %collective-permute-start.2 = (bf16[16,1024]{1,0:T(8,128)(2,1)S(1)}, bf16[16,1024]{1,0:T(8,128)(2,1)S(1)}, u32[]{:S(2)}, u32[]{:S(2)}) collective-permute-start(bf16[16,1024]{1,0:T(8,128)(2,1)S(1)} %get-tuple-element.29), channel_id=1, source_target_pairs={{0,8},{8,0},{16,24},{24,16},{32,40},{40,32},{48,56},{56,48},{64,72... | collective-permute-start | bytes 98312 | tf_op jit(solution)/shard_map/ppermute | solution.py:368
  24.6 2.2 %collective-permute-start.3 = (bf16[16,1024]{1,0:T(8,128)(2,1)S(1)}, bf16[16,1024]{1,0:T(8,128)(2,1)S(1)}, u32[]{:S(2)}, u32[]{:S(2)}) collective-permute-start(bf16[16,1024]{1,0:T(8,128)(2,1)S(1)} %get-tuple-element.30), channel_id=1, source_target_pairs={{0,1},{1,0},{2,3},{3,2},{4,5},{5,4},{6,7},{7,6},{8,9},{9,8},{10,11... | collective-permute-start | bytes 98312 | tf_op jit(solution)/shard_map/ppermute | solution.py:368
  26.9 1.2 %shard_map.130 = (bf16[128,512]{1,0:T(8,128)(2,1)S(1)}, bf16[128,512]{1,0:T(8,128)(2,1)S(1)}, f32[192,128]{1,0:T(8,128)S(1)}) custom-call(bf16[128,512]{1,0:T(8,128)(2,1)S(1)} %get-tuple-element.22.first.refs_4_, bf16[3,512,512]{2,1,0:T(8,128)(2,1)S(1)} %copy-done, bf16[512,512]{1,0:T(8,128)(2,1)S(1)} %copy-done.1, bf16[128,512]{1,0:T(8,128)(2,1)S(1)} %copy-done.3, ...), custom_call_target="tpu_custom_call" | custom-call | flops 2000000000 | bytes 5000000 | tf_op jit(solution)/shard_map/pallas_call | solution.py:57
  28.1 0.4 collective-permute-done.2.refs_8_
  28.5 3.8 %shard_map.131 = (bf16[272,1024]{1,0:T(8,128)(2,1)S(1)}, f32[128,1024]{1,0:T(8,128)S(1)}, bf16[16,1024]{1,0:T(8,128)(2,1)S(1)}, bf16[16,1024]{1,0:T(8,128)(2,1)S(1)}, bf16[16,1024]{1,0:T(8,128)(2,1)S(1)}) custom-call(bf16[128,512]{1,0:T(8,128)(2,1)S(1)} %get-tuple-element.23.refs_0_, bf16[128,1024]{1,0:T(8,128)(2,1)S(1)} %get-tuple-element.24.refs_1_, ...), custom_call_target="tpu_custom_call" | custom-call | flops 3200000000 | bytes 8000000 | tf_op jit(solution)/shard_map/pallas_call | solution.py:57
  32.4 0.0 copy-start.8
  32.4 0.0 copy-start.9
  32.4 2.1 %collective-permute-start.7 = (bf16[272,1024]{1,0:T(8,128)(2,1)S(1)}, bf16[272,1024]{1,0:T(8,128)(2,1)S(1)}, u32[]{:S(2)}, u32[]{:S(2)}) collective-permute-start(bf16[272,1024]{1,0:T(8,128)(2,1)S(1)} %get-tuple-element.31.sent.refs_0_.refs_1_), channel_id=1, source_target_pairs={{0,1},{1,0},{2,3},{3,2},{4,5},{5,4},{6,7},{7,6},{8,9},{9,8},{10,11... | collective-permute-start | bytes 1671176 | tf_op jit(solution)/shard_map/ppermute | solution.py:368
  34.5 6.0 %collective-permute-start.4 = (bf16[16,1024]{1,0:T(8,128)(2,1)S(1)}, bf16[16,1024]{1,0:T(8,128)(2,1)S(1)}, u32[]{:S(2)}, u32[]{:S(2)}) collective-permute-start(bf16[16,1024]{1,0:T(8,128)(2,1)S(1)} %get-tuple-element.33), channel_id=1, source_target_pairs={{0,504},{8,16},{16,8},{24,32},{32,24},{40,48},{48,40},{56,64},{64,... | collective-permute-start | bytes 98312 | tf_op jit(solution)/shard_map/ppermute | solution.py:368
  40.5 3.0 %collective-permute-start.5 = (bf16[16,1024]{1,0:T(8,128)(2,1)S(1)}, bf16[16,1024]{1,0:T(8,128)(2,1)S(1)}, u32[]{:S(2)}, u32[]{:S(2)}) collective-permute-start(bf16[16,1024]{1,0:T(8,128)(2,1)S(1)} %get-tuple-element.34), channel_id=1, source_target_pairs={{0,7},{1,2},{2,1},{3,4},{4,3},{5,6},{6,5},{7,0},{8,15},{9,10},{10,... | collective-permute-start | bytes 98312 | tf_op jit(solution)/shard_map/ppermute | solution.py:368
  43.5 1.9 %collective-permute-start.6 = (bf16[16,1024]{1,0:T(8,128)(2,1)S(1)}, bf16[16,1024]{1,0:T(8,128)(2,1)S(1)}, u32[]{:S(2)}, u32[]{:S(2)}) collective-permute-start(bf16[16,1024]{1,0:T(8,128)(2,1)S(1)} %get-tuple-element.35), channel_id=1, source_target_pairs={{0,8},{8,0},{16,24},{24,16},{32,40},{40,32},{48,56},{56,48},{64,72... | collective-permute-start | bytes 98312 | tf_op jit(solution)/shard_map/ppermute | solution.py:368
  45.5 2.9 %collective-permute-done.4.refs_2_ = bf16[16,1024]{1,0:T(8,128)(2,1)S(1)} collective-permute-done((bf16[16,1024]{1,0:T(8,128)(2,1)S(1)}, bf16[16,1024]{1,0:T(8,128)(2,1)S(1)}, u32[]{:S(2)}, u32[]{:S(2)}) %collective-permute-start.4) | collective-permute-done | bytes 32800 | tf_op jit(solution)/shard_map/ppermute | solution.py:368
  48.4 0.9 collective-permute-done.6.refs_4_
  49.4 0.7 shard_map.133.late.refs_2_
  50.0 1.9 %collective-permute-start.8 = (bf16[128,1024]{1,0:T(8,128)(2,1)S(1)}, bf16[128,1024]{1,0:T(8,128)(2,1)S(1)}, u32[]{:S(2)}, u32[]{:S(2)}) collective-permute-start(bf16[128,1024]{1,0:T(8,128)(2,1)S(1)} %shard_map.133.late.refs_2_), channel_id=1, source_target_pairs={{0,1},{1,0},{2,3},{3,2},{4,5},{5,4},{6,7},{7,6},{8,9},{9,8},{10,11... | collective-permute-start | bytes 786440 | tf_op jit(solution)/shard_map/ppermute | solution.py:368
  52.0 1.1 %shard_map.135 = (bf16[768,768]{1,0:T(8,128)(2,1)S(1)}, f32[256,512]{1,0:T(8,128)S(1)}) custom-call(bf16[272,1024]{1,0:T(8,128)(2,1)S(1)} %get-tuple-element.31.sent.refs_0_.refs_1_, s32[768,1]{1,0:T(8,128)S(1)} %copy-done.8, s32[256,1]{1,0:T(8,128)S(1)} %copy-done.9, bf16[272,1024]{1,0:T(8,128)(2,1)S(1)} %collective-permute-done.7.refs_5_.refs_3_.refs_4_), custom_call_target="tpu_custom_call" | custom-call | flops 1200000000 | bytes 3000000 | tf_op jit(solution)/shard_map/pallas_call | solution.py:57
  53.1 0.3 collective-permute-done.8.refs_5_
  53.4 1.1 %shard_map.136 = f32[4,272,512]{2,1,0:T(8,128)S(1)} custom-call(bf16[768,768]{1,0:T(8,128)(2,1)S(1)} %get-tuple-element.36.refs_0_, bf16[272,1024]{1,0:T(8,128)(2,1)S(1)} %get-tuple-element.31.sent.refs_0_.refs_1_, bf16[128,1024]{1,0:T(8,128)(2,1)S(1)} %shard_map.133.late.refs_2_, f32[256,512]{1,0:T(8,128)S(1)} %get-tuple-element.37.refs_3_, ...), custom_call_target="tpu_custom_call" | custom-call | flops 1200000000 | bytes 3000000 | tf_op jit(solution)/shard_map/pallas_call | solution.py:57
  54.6 0.3 convert_element_type.12
  54.9 18.8 %all_to_all.10 = f16[4,272,512]{2,1,0:T(8,128)(2,1)S(1)} all-to-all(f16[4,272,512]{2,1,0:T(8,128)(2,1)S(1)} %convert_element_type.12), channel_id=1, replica_groups=mesh['yh'=2,'z'=8,'x'=4,'yl'=4,'core'=2] {'x'}, dimensions={0} | all-to-all | bytes 2228224 | tf_op jit(solution)/shard_map/all_to_all | solution.py:448
  73.7 0.3 convert_element_type.13.refs_0_
  74.0 0.8 shard_map.137
  74.8 0.8 convert_element_type.14
  75.6 9.6 %all-to-all-start.1 = ((f16[64,4,640]{2,1,0:T(4,128)(2,1)}), f16[64,4,640]{2,1,0:T(4,128)(2,1)S(1)}, u32[]{:S(2)}, u32[]{:S(2)}) async-start(f16[64,4,640]{2,1,0:T(4,128)(2,1)} %convert_element_type.14), calls=%async_computation.1 | async-start | bytes 655360 | tf_op jit(solution)/shard_map/all_to_all | solution.py:458
  85.2 0.9 shard_map.132
  86.1 1.4 %shard_map.134 = f32[128,512]{1,0:T(8,128)} custom-call(bf16[128,512]{1,0:T(8,128)(2,1)S(1)} %copy-done.2, bf16[128,512]{1,0:T(8,128)(2,1)S(1)} %copy-done.3, f32[1,512]{1,0:T(1,128)S(1)} %bitcast.8, bf16[272,1024]{1,0:T(8,128)(2,1)S(1)} %get-tuple-element.31.sent.refs_0_.refs_1_, bf16[128,1024]{1,0:T(8,128)(2,1)S(1)} %shard_map.133.late.refs_2_, ...), custom_call_target="tpu_custom_call" | custom-call | flops 1200000000 | bytes 3000000 | tf_op jit(solution)/shard_map/pallas_call | solution.py:57
  87.6 12.8 %all-to-all-done.1 = f16[64,4,640]{2,1,0:T(4,128)(2,1)S(1)} async-done(((f16[64,4,640]{2,1,0:T(4,128)(2,1)}), f16[64,4,640]{2,1,0:T(4,128)(2,1)S(1)}, u32[]{:S(2)}, u32[]{:S(2)}) %all-to-all-start.1) | async-done | bytes 327712 | tf_op jit(solution)/shard_map/all_to_all | solution.py:458
  100.4 0.1 convert_element_type.15.refs_0_
  100.5 1.0 shard_map.138
  (23 shorter events, 0.1 us)
Async XLA Ops:
  0.6 26.2 %copy-start = (bf16[3,512,512]{2,1,0:T(8,128)(2,1)S(1)}, bf16[3,512,512]{2,1,0:T(8,128)(2,1)}, u32[]{:S(2)}) copy-start(bf16[3,512,512]{2,1,0:T(8,128)(2,1)} %weight.3) | copy-start | bytes 4718596
  0.6 26.2 %copy-start.1 = (bf16[512,512]{1,0:T(8,128)(2,1)S(1)}, bf16[512,512]{1,0:T(8,128)(2,1)}, u32[]{:S(2)}) copy-start(bf16[512,512]{1,0:T(8,128)(2,1)} %output_weight.3) | copy-start | bytes 1572868
  0.7 26.2 %copy-start.3 = (bf16[128,512]{1,0:T(8,128)(2,1)S(1)}, bf16[128,512]{1,0:T(8,128)(2,1)}, u32[]{:S(2)}) copy-start(bf16[128,512]{1,0:T(8,128)(2,1)} %cotangent.3) | copy-start | bytes 393220
  0.7 26.2 %copy-start.4 = (s32[128,64]{0,1:T(8,128)S(1)}, s32[128,64]{0,1:T(8,128)}, u32[]{:S(2)}) copy-start(s32[128,64]{0,1:T(8,128)} %param.15) | copy-start | bytes 98308
  0.7 26.2 %copy-start.5 = (s32[128,64]{0,1:T(8,128)S(1)}, s32[128,64]{0,1:T(8,128)}, u32[]{:S(2)}) copy-start(s32[128,64]{0,1:T(8,128)} %param.16) | copy-start | bytes 98308
  2.8 25.3 %collective-permute-start = (bf16[16,1024]{1,0:T(8,128)(2,1)S(1)}, bf16[16,1024]{1,0:T(8,128)(2,1)S(1)}, u32[]{:S(2)}, u32[]{:S(2)}) collective-permute-start(bf16[16,1024]{1,0:T(8,128)(2,1)S(1)} %get-tuple-element.27), channel_id=1, source_target_pairs={{0,504},{8,16},{16,8},{24,32},{32,24},{40,48},{48,40},{56,64},{64,... | collective-permute-start | bytes 98312 | tf_op jit(solution)/shard_map/ppermute | solution.py:368
  20.3 7.8 %collective-permute-start.1 = (bf16[16,1024]{1,0:T(8,128)(2,1)S(1)}, bf16[16,1024]{1,0:T(8,128)(2,1)S(1)}, u32[]{:S(2)}, u32[]{:S(2)}) collective-permute-start(bf16[16,1024]{1,0:T(8,128)(2,1)S(1)} %get-tuple-element.28), channel_id=1, source_target_pairs={{0,7},{1,2},{2,1},{3,4},{4,3},{5,6},{6,5},{7,0},{8,15},{9,10},{10,... | collective-permute-start | bytes 98312 | tf_op jit(solution)/shard_map/ppermute | solution.py:368
  22.7 5.8 %collective-permute-start.2 = (bf16[16,1024]{1,0:T(8,128)(2,1)S(1)}, bf16[16,1024]{1,0:T(8,128)(2,1)S(1)}, u32[]{:S(2)}, u32[]{:S(2)}) collective-permute-start(bf16[16,1024]{1,0:T(8,128)(2,1)S(1)} %get-tuple-element.29), channel_id=1, source_target_pairs={{0,8},{8,0},{16,24},{24,16},{32,40},{40,32},{48,56},{56,48},{64,72... | collective-permute-start | bytes 98312 | tf_op jit(solution)/shard_map/ppermute | solution.py:368
  24.6 3.9 %collective-permute-start.3 = (bf16[16,1024]{1,0:T(8,128)(2,1)S(1)}, bf16[16,1024]{1,0:T(8,128)(2,1)S(1)}, u32[]{:S(2)}, u32[]{:S(2)}) collective-permute-start(bf16[16,1024]{1,0:T(8,128)(2,1)S(1)} %get-tuple-element.30), channel_id=1, source_target_pairs={{0,1},{1,0},{2,3},{3,2},{4,5},{5,4},{6,7},{7,6},{8,9},{9,8},{10,11... | collective-permute-start | bytes 98312 | tf_op jit(solution)/shard_map/ppermute | solution.py:368
  28.5 20.8 %copy-start.6 = (s32[4,16]{1,0:T(4,128)S(1)}, s32[4,16]{1,0:T(4,128)}, u32[]{:S(2)}) copy-start(s32[4,16]{1,0:T(4,128)} %refs_1_.2) | copy-start | bytes 772
  32.4 19.6 %copy-start.8 = (s32[768,1]{1,0:T(8,128)S(1)}, s32[768,1]{1,0:T(8,128)}, u32[]{:S(2)}) copy-start(s32[768,1]{1,0:T(8,128)} %constant.4.clone.refs_1_) | copy-start | bytes 9220
  32.4 19.6 %copy-start.9 = (s32[256,1]{1,0:T(8,128)S(1)}, s32[256,1]{1,0:T(8,128)}, u32[]{:S(2)}) copy-start(s32[256,1]{1,0:T(8,128)} %constant.5.clone.refs_2_) | copy-start | bytes 3076
  32.4 17.0 %collective-permute-start.7 = (bf16[272,1024]{1,0:T(8,128)(2,1)S(1)}, bf16[272,1024]{1,0:T(8,128)(2,1)S(1)}, u32[]{:S(2)}, u32[]{:S(2)}) collective-permute-start(bf16[272,1024]{1,0:T(8,128)(2,1)S(1)} %get-tuple-element.31.sent.refs_0_.refs_1_), channel_id=1, source_target_pairs={{0,1},{1,0},{2,3},{3,2},{4,5},{5,4},{6,7},{7,6},{8,9},{9,8},{10,11... | collective-permute-start | bytes 1671176 | tf_op jit(solution)/shard_map/ppermute | solution.py:368
  34.5 13.9 %collective-permute-start.4 = (bf16[16,1024]{1,0:T(8,128)(2,1)S(1)}, bf16[16,1024]{1,0:T(8,128)(2,1)S(1)}, u32[]{:S(2)}, u32[]{:S(2)}) collective-permute-start(bf16[16,1024]{1,0:T(8,128)(2,1)S(1)} %get-tuple-element.33), channel_id=1, source_target_pairs={{0,504},{8,16},{16,8},{24,32},{32,24},{40,48},{48,40},{56,64},{64,... | collective-permute-start | bytes 98312 | tf_op jit(solution)/shard_map/ppermute | solution.py:368
  40.5 7.9 %collective-permute-start.5 = (bf16[16,1024]{1,0:T(8,128)(2,1)S(1)}, bf16[16,1024]{1,0:T(8,128)(2,1)S(1)}, u32[]{:S(2)}, u32[]{:S(2)}) collective-permute-start(bf16[16,1024]{1,0:T(8,128)(2,1)S(1)} %get-tuple-element.34), channel_id=1, source_target_pairs={{0,7},{1,2},{2,1},{3,4},{4,3},{5,6},{6,5},{7,0},{8,15},{9,10},{10,... | collective-permute-start | bytes 98312 | tf_op jit(solution)/shard_map/ppermute | solution.py:368
  43.5 5.8 %collective-permute-start.6 = (bf16[16,1024]{1,0:T(8,128)(2,1)S(1)}, bf16[16,1024]{1,0:T(8,128)(2,1)S(1)}, u32[]{:S(2)}, u32[]{:S(2)}) collective-permute-start(bf16[16,1024]{1,0:T(8,128)(2,1)S(1)} %get-tuple-element.35), channel_id=1, source_target_pairs={{0,8},{8,0},{16,24},{24,16},{32,40},{40,32},{48,56},{56,48},{64,72... | collective-permute-start | bytes 98312 | tf_op jit(solution)/shard_map/ppermute | solution.py:368
  50.0 3.4 %collective-permute-start.8 = (bf16[128,1024]{1,0:T(8,128)(2,1)S(1)}, bf16[128,1024]{1,0:T(8,128)(2,1)S(1)}, u32[]{:S(2)}, u32[]{:S(2)}) collective-permute-start(bf16[128,1024]{1,0:T(8,128)(2,1)S(1)} %shard_map.133.late.refs_2_), channel_id=1, source_target_pairs={{0,1},{1,0},{2,3},{3,2},{4,5},{5,4},{6,7},{7,6},{8,9},{9,8},{10,11... | collective-permute-start | bytes 786440 | tf_op jit(solution)/shard_map/ppermute | solution.py:368
  74.0 11.2 %copy-start.2 = (bf16[128,512]{1,0:T(8,128)(2,1)S(1)}, bf16[128,512]{1,0:T(8,128)(2,1)}, u32[]{:S(2)}) copy-start(bf16[128,512]{1,0:T(8,128)(2,1)} %features.3) | copy-start | bytes 393220
  75.6 24.8 %all-to-all-start.1 = ((f16[64,4,640]{2,1,0:T(4,128)(2,1)}), f16[64,4,640]{2,1,0:T(4,128)(2,1)S(1)}, u32[]{:S(2)}, u32[]{:S(2)}) async-start(f16[64,4,640]{2,1,0:T(4,128)(2,1)} %convert_element_type.14), calls=%async_computation.1 | async-start | bytes 655360 | tf_op jit(solution)/shard_map/all_to_all | solution.py:458
  85.2 0.9 copy-start.7

commit v6 on v5

--- a/solution.py
+++ b/solution.py
@@ -9,6 +9,7 @@
 from jax.experimental.pallas import tpu as pltpu
 from jax.sharding import Mesh
 from jax.sharding import PartitionSpec as P
+
 
 HEADS = 8
 HEAD_DIM = 64
@@ -188,46 +189,40 @@
         start = rows + index * cap
         table[start : start + cap, :] = band[...]
     factor = HEAD_DIM**-0.5
-    count = counts[...]
+    count = jnp.concatenate([counts[...], counts[...]], axis=1)
     is_live = count > 0
     wide = 2 * HEAD_DIM
     side = lax.broadcasted_iota(jnp.int32, (1, wide), 1) // HEAD_DIM
     down = ((0,), (0,))
+    zero = jnp.zeros((), BF16)
+
+    def halves(block):
+        return jnp.concatenate([jnp.where(side == half, block, zero) for half in range(2)], axis=0)
+
+    def joined(block):
+        return jnp.where(side == 0, block[:rows, :], block[rows:, :]).astype(BF16)
+
     for pair in range(HEADS // 2):
         lanes = slice(pair * wide, (pair + 1) * wide)
         value_lanes = slice(width + pair * wide, width + (pair + 1) * wide)
-        query, upstream = queries[:, lanes], grad_mixed[:, lanes]
+        query, upstream = halves(queries[:, lanes]), halves(grad_mixed[:, lanes])
         key, value = table[:, lanes], table[:, value_lanes]
-        zero = jnp.zeros((), BF16)
-        mixed, grad_query, grad_key, grad_value = [], [], None, None
-        for half in range(2):
-            mine = side == half
-            query_half = jnp.where(mine, query, zero)
-            upstream_half = jnp.where(mine, upstream, zero)
-            scores = dot(key, query_half, ((1,), (1,))) * factor
-            grad_probs = dot(value, upstream_half, ((1,), (1,)))
-            scores = jnp.where(is_live, scores, -1e30)
-            row_max = jnp.max(scores, axis=0, keepdims=True)
-            powers = jnp.where(is_live, jnp.exp(scores - row_max), 0.0)
-            probabilities = powers / jnp.sum(count * powers, axis=0, keepdims=True)
-            weights = split(count * probabilities.astype(BF16).astype(F32))
-            spread = count * probabilities
-            grad_scores = spread * (
-                grad_probs - jnp.sum(spread * grad_probs, axis=0, keepdims=True)
-            )
-            grad_scores = split(grad_scores * factor)
-            mixed.append(sum(dot(w, value, down) for w in weights))
-            grad_query.append(sum(dot(g, key, down) for g in grad_scores))
-            grad_k = sum(dot(g, query_half) for g in grad_scores)
-            grad_v = sum(dot(w, upstream_half) for w in weights)
-            grad_key = grad_k if half == 0 else grad_key + grad_k
-            grad_value = grad_v if half == 0 else grad_value + grad_v
-        sent[rows : 2 * rows, lanes] = jnp.where(side == 0, mixed[0], mixed[1]).astype(BF16)
-        sent[rows : 2 * rows, value_lanes] = jnp.where(
-            side == 0, grad_query[0], grad_query[1]
-        ).astype(BF16)
-        grads[:, lanes] = grad_key
-        grads[:, value_lanes] = grad_value
+        scores = dot(key, query, ((1,), (1,))) * factor
+        grad_probs = dot(value, upstream, ((1,), (1,)))
+        scores = jnp.where(is_live, scores, -1e30)
+        row_max = jnp.max(scores, axis=0, keepdims=True)
+        powers = jnp.where(is_live, jnp.exp(scores - row_max), 0.0)
+        probabilities = powers / jnp.sum(count * powers, axis=0, keepdims=True)
+        weights = split(count * probabilities.astype(BF16).astype(F32))
+        spread = count * probabilities
+        grad_scores = spread * (
+            grad_probs - jnp.sum(spread * grad_probs, axis=0, keepdims=True)
+        )
+        grad_scores = split(grad_scores * factor)
+        sent[rows : 2 * rows, lanes] = joined(sum(dot(w, value, down) for w in weights))
+        sent[rows : 2 * rows, value_lanes] = joined(sum(dot(g, key, down) for g in grad_scores))
+        grads[:, lanes] = sum(dot(g, query) for g in grad_scores)
+        grads[:, value_lanes] = sum(dot(w, upstream) for w in weights)
     own[...] = grads[:rows, :]
     sent[2 * rows :, :] = grads[rows : rows + cap, :].astype(BF16)
     for index, back in enumerate((back1, back2, back3)):
@@ -414,7 +409,9 @@
             pltpu.VMEM((rows + 4 * cap, 2 * width), F32),
         ),
     )
-    returned = [exchanged(backs[index - 1], *steps[index]) for index in (3, 1, 2)]
+    returned = []
+    for index in (3, 1, 2):
+        returned.append(exchanged(backs[index - 1], *steps[index]))
     partner = exchanged(sent, *steps[0])
     layer_output = call(
         layer_kernel, shape(rows, width), (features, sent, output_weight), 3

time: 102 us -> 101 us (level)
  Pallas kernels: 14.1 us -> 13 us
    pallas_call x9, Pallas kernels: 12 us -> 10.9 us  [call(): pl.pallas_call(moving if moved else kernel, out_shape=out_shapes, in_spec...]
where the time goes in v6:
time: 101 us; the launch traced here: 100 us
  starting transfers between devices  48.6 us (48%)
  blocking collectives  18.8 us (19%)
  waiting for transfers between devices  17.5 us (17%)
  Pallas kernels  13 us (13%)
  other arithmetic  1.5 us (1%)
    ppermute x9, starting transfers between devices, exchanged(): lax.ppermute(block, axis, [(i, partner % size) for i, partner in enumerat...  39 us
    all_to_all x1, blocking collectives, body(): lax.all_to_all(both.astype(jnp.float16), 'x', 0, 0, tiled=True).astype(F32)  18.8 us
    all_to_all x1, waiting for transfers between devices, body(): lax.all_to_all(parts.astype(jnp.float16), FAR, 0, 0, tiled=True).astype(F32)  12.8 us
    pallas_call x9, Pallas kernels, call(): pl.pallas_call(moving if moved else kernel, out_shape=out_shapes, in_spec...  10.9 us
    all_to_all x1, starting transfers between devices, body(): lax.all_to_all(parts.astype(jnp.float16), FAR, 0, 0, tiled=True).astype(F32)  9.62 us
    ppermute x9, waiting for transfers between devices, exchanged(): lax.ppermute(block, axis, [(i, partner % size) for i, partner in enumerat...  4.66 us
    pallas_call x1, Pallas kernels, keys_call(): pl.pallas_call(keys_kernel, out_shape=(shape(rows, width), shape(rows, 2...  2.09 us
  transfers between devices with their start and end apart: 10, of which 5 were waited for; matrix products, arithmetic and copies ran while one was open for 0% of the time, Pallas kernels for 5%

profile of v6, /device:TPU:8, one launch (start us, length us, event | category | flops | bytes accessed | tf_op | source)
XLA Modules:
  0.0 100.4 jit_solution(11385617054851105036)
XLA Ops:
  0.7 2.1 %shard_map.129 = (bf16[128,512]{1,0:T(8,128)(2,1)S(1)}, bf16[128,1024]{1,0:T(8,128)(2,1)S(1)}, bf16[16,1024]{1,0:T(8,128)(2,1)S(1)}, bf16[16,1024]{1,0:T(8,128)(...) custom-call(bf16[128,512]{1,0:T(8,128)(2,1)} %features.3, f32[1,512]{1,0:T(1,128)} %bitcast.7, ...), custom_call_target="tpu_custom_call" | custom-call | flops 1200000000 | bytes 3000000 | tf_op jit(solution)/shard_map/pallas_call | solution.py:135
  2.8 17.5 %collective-permute-start = (bf16[16,1024]{1,0:T(8,128)(2,1)S(1)}, bf16[16,1024]{1,0:T(8,128)(2,1)S(1)}, u32[]{:S(2)}, u32[]{:S(2)}) collective-permute-start(bf16[16,1024]{1,0:T(8,128)(2,1)S(1)} %get-tuple-element.27), channel_id=1, source_target_pairs={{0,504},{8,16},{16,8},{24,32},{32,24},{40,48},{48,40},{56,64},{64,... | collective-permute-start | bytes 98312 | tf_op jit(solution)/shard_map/ppermute | solution.py:363
  20.3 2.4 %collective-permute-start.1 = (bf16[16,1024]{1,0:T(8,128)(2,1)S(1)}, bf16[16,1024]{1,0:T(8,128)(2,1)S(1)}, u32[]{:S(2)}, u32[]{:S(2)}) collective-permute-start(bf16[16,1024]{1,0:T(8,128)(2,1)S(1)} %get-tuple-element.28), channel_id=1, source_target_pairs={{0,7},{1,2},{2,1},{3,4},{4,3},{5,6},{6,5},{7,0},{8,15},{9,10},{10,... | collective-permute-start | bytes 98312 | tf_op jit(solution)/shard_map/ppermute | solution.py:363
  22.7 1.9 %collective-permute-start.2 = (bf16[16,1024]{1,0:T(8,128)(2,1)S(1)}, bf16[16,1024]{1,0:T(8,128)(2,1)S(1)}, u32[]{:S(2)}, u32[]{:S(2)}) collective-permute-start(bf16[16,1024]{1,0:T(8,128)(2,1)S(1)} %get-tuple-element.29), channel_id=1, source_target_pairs={{0,8},{8,0},{16,24},{24,16},{32,40},{40,32},{48,56},{56,48},{64,72... | collective-permute-start | bytes 98312 | tf_op jit(solution)/shard_map/ppermute | solution.py:363
  24.6 2.2 %collective-permute-start.3 = (bf16[16,1024]{1,0:T(8,128)(2,1)S(1)}, bf16[16,1024]{1,0:T(8,128)(2,1)S(1)}, u32[]{:S(2)}, u32[]{:S(2)}) collective-permute-start(bf16[16,1024]{1,0:T(8,128)(2,1)S(1)} %get-tuple-element.30), channel_id=1, source_target_pairs={{0,1},{1,0},{2,3},{3,2},{4,5},{5,4},{6,7},{7,6},{8,9},{9,8},{10,11... | collective-permute-start | bytes 98312 | tf_op jit(solution)/shard_map/ppermute | solution.py:363
  26.9 1.2 %shard_map.130 = (bf16[128,512]{1,0:T(8,128)(2,1)S(1)}, bf16[128,512]{1,0:T(8,128)(2,1)S(1)}, f32[192,128]{1,0:T(8,128)S(1)}) custom-call(bf16[128,512]{1,0:T(8,128)(2,1)S(1)} %get-tuple-element.22.first.refs_4_, bf16[3,512,512]{2,1,0:T(8,128)(2,1)S(1)} %copy-done, bf16[512,512]{1,0:T(8,128)(2,1)S(1)} %copy-done.1, bf16[128,512]{1,0:T(8,128)(2,1)S(1)} %copy-done.3, ...), custom_call_target="tpu_custom_call" | custom-call | flops 2000000000 | bytes 5000000 | tf_op jit(solution)/shard_map/pallas_call | solution.py:58
  28.1 0.4 collective-permute-done.2.refs_8_
  28.5 2.8 %shard_map.131 = (bf16[272,1024]{1,0:T(8,128)(2,1)S(1)}, f32[128,1024]{1,0:T(8,128)S(1)}, bf16[16,1024]{1,0:T(8,128)(2,1)S(1)}, bf16[16,1024]{1,0:T(8,128)(2,1)S(1)}, bf16[16,1024]{1,0:T(8,128)(2,1)S(1)}) custom-call(bf16[128,512]{1,0:T(8,128)(2,1)S(1)} %get-tuple-element.23.refs_0_, bf16[128,1024]{1,0:T(8,128)(2,1)S(1)} %get-tuple-element.24.refs_1_, ...), custom_call_target="tpu_custom_call" | custom-call | flops 3200000000 | bytes 8000000 | tf_op jit(solution)/shard_map/pallas_call | solution.py:58
  31.3 0.0 copy-start.8
  31.3 0.0 copy-start.9
  31.3 2.1 %collective-permute-start.7 = (bf16[272,1024]{1,0:T(8,128)(2,1)S(1)}, bf16[272,1024]{1,0:T(8,128)(2,1)S(1)}, u32[]{:S(2)}, u32[]{:S(2)}) collective-permute-start(bf16[272,1024]{1,0:T(8,128)(2,1)S(1)} %get-tuple-element.31.sent.refs_0_.refs_1_), channel_id=1, source_target_pairs={{0,1},{1,0},{2,3},{3,2},{4,5},{5,4},{6,7},{7,6},{8,9},{9,8},{10,11... | collective-permute-start | bytes 1671176 | tf_op jit(solution)/shard_map/ppermute | solution.py:363
  33.4 6.0 %collective-permute-start.4 = (bf16[16,1024]{1,0:T(8,128)(2,1)S(1)}, bf16[16,1024]{1,0:T(8,128)(2,1)S(1)}, u32[]{:S(2)}, u32[]{:S(2)}) collective-permute-start(bf16[16,1024]{1,0:T(8,128)(2,1)S(1)} %get-tuple-element.33), channel_id=1, source_target_pairs={{0,504},{8,16},{16,8},{24,32},{32,24},{40,48},{48,40},{56,64},{64,... | collective-permute-start | bytes 98312 | tf_op jit(solution)/shard_map/ppermute | solution.py:363
  39.4 3.0 %collective-permute-start.5 = (bf16[16,1024]{1,0:T(8,128)(2,1)S(1)}, bf16[16,1024]{1,0:T(8,128)(2,1)S(1)}, u32[]{:S(2)}, u32[]{:S(2)}) collective-permute-start(bf16[16,1024]{1,0:T(8,128)(2,1)S(1)} %get-tuple-element.34), channel_id=1, source_target_pairs={{0,7},{1,2},{2,1},{3,4},{4,3},{5,6},{6,5},{7,0},{8,15},{9,10},{10,... | collective-permute-start | bytes 98312 | tf_op jit(solution)/shard_map/ppermute | solution.py:363
  42.5 1.9 %collective-permute-start.6 = (bf16[16,1024]{1,0:T(8,128)(2,1)S(1)}, bf16[16,1024]{1,0:T(8,128)(2,1)S(1)}, u32[]{:S(2)}, u32[]{:S(2)}) collective-permute-start(bf16[16,1024]{1,0:T(8,128)(2,1)S(1)} %get-tuple-element.35), channel_id=1, source_target_pairs={{0,8},{8,0},{16,24},{24,16},{32,40},{40,32},{48,56},{56,48},{64,72... | collective-permute-start | bytes 98312 | tf_op jit(solution)/shard_map/ppermute | solution.py:363
  44.4 2.9 %collective-permute-done.4.refs_2_ = bf16[16,1024]{1,0:T(8,128)(2,1)S(1)} collective-permute-done((bf16[16,1024]{1,0:T(8,128)(2,1)S(1)}, bf16[16,1024]{1,0:T(8,128)(2,1)S(1)}, u32[]{:S(2)}, u32[]{:S(2)}) %collective-permute-start.4) | collective-permute-done | bytes 32800 | tf_op jit(solution)/shard_map/ppermute | solution.py:363
  47.3 0.9 collective-permute-done.6.refs_4_
  48.3 0.6 shard_map.133.late.refs_2_
  48.9 1.9 %collective-permute-start.8 = (bf16[128,1024]{1,0:T(8,128)(2,1)S(1)}, bf16[128,1024]{1,0:T(8,128)(2,1)S(1)}, u32[]{:S(2)}, u32[]{:S(2)}) collective-permute-start(bf16[128,1024]{1,0:T(8,128)(2,1)S(1)} %shard_map.133.late.refs_2_), channel_id=1, source_target_pairs={{0,1},{1,0},{2,3},{3,2},{4,5},{5,4},{6,7},{7,6},{8,9},{9,8},{10,11... | collective-permute-start | bytes 786440 | tf_op jit(solution)/shard_map/ppermute | solution.py:363
  50.9 1.1 %shard_map.135 = (bf16[768,768]{1,0:T(8,128)(2,1)S(1)}, f32[256,512]{1,0:T(8,128)S(1)}) custom-call(bf16[272,1024]{1,0:T(8,128)(2,1)S(1)} %get-tuple-element.31.sent.refs_0_.refs_1_, s32[768,1]{1,0:T(8,128)S(1)} %copy-done.8, s32[256,1]{1,0:T(8,128)S(1)} %copy-done.9, bf16[272,1024]{1,0:T(8,128)(2,1)S(1)} %collective-permute-done.7.refs_5_.refs_3_.refs_4_), custom_call_target="tpu_custom_call" | custom-call | flops 1200000000 | bytes 3000000 | tf_op jit(solution)/shard_map/pallas_call | solution.py:58
  52.0 0.3 collective-permute-done.8.refs_5_
  52.4 1.1 %shard_map.136 = f32[4,272,512]{2,1,0:T(8,128)S(1)} custom-call(bf16[768,768]{1,0:T(8,128)(2,1)S(1)} %get-tuple-element.36.refs_0_, bf16[272,1024]{1,0:T(8,128)(2,1)S(1)} %get-tuple-element.31.sent.refs_0_.refs_1_, bf16[128,1024]{1,0:T(8,128)(2,1)S(1)} %shard_map.133.late.refs_2_, f32[256,512]{1,0:T(8,128)S(1)} %get-tuple-element.37.refs_3_, ...), custom_call_target="tpu_custom_call" | custom-call | flops 1200000000 | bytes 3000000 | tf_op jit(solution)/shard_map/pallas_call | solution.py:58
  53.5 0.3 convert_element_type.12
  53.8 18.8 %all_to_all.10 = f16[4,272,512]{2,1,0:T(8,128)(2,1)S(1)} all-to-all(f16[4,272,512]{2,1,0:T(8,128)(2,1)S(1)} %convert_element_type.12), channel_id=1, replica_groups=mesh['yh'=2,'z'=8,'x'=4,'yl'=4,'core'=2] {'x'}, dimensions={0} | all-to-all | bytes 2228224 | tf_op jit(solution)/shard_map/all_to_all | solution.py:445
  72.6 0.3 convert_element_type.13.refs_0_
  72.9 0.8 shard_map.137
  73.7 0.8 convert_element_type.14
  74.5 9.6 %all-to-all-start.1 = ((f16[64,4,640]{2,1,0:T(4,128)(2,1)}), f16[64,4,640]{2,1,0:T(4,128)(2,1)S(1)}, u32[]{:S(2)}, u32[]{:S(2)}) async-start(f16[64,4,640]{2,1,0:T(4,128)(2,1)} %convert_element_type.14), calls=%async_computation.1 | async-start | bytes 655360 | tf_op jit(solution)/shard_map/all_to_all | solution.py:455
  84.2 0.9 shard_map.132
  85.1 1.4 %shard_map.134 = f32[128,512]{1,0:T(8,128)} custom-call(bf16[128,512]{1,0:T(8,128)(2,1)S(1)} %copy-done.2, bf16[128,512]{1,0:T(8,128)(2,1)S(1)} %copy-done.3, f32[1,512]{1,0:T(1,128)S(1)} %bitcast.8, bf16[272,1024]{1,0:T(8,128)(2,1)S(1)} %get-tuple-element.31.sent.refs_0_.refs_1_, bf16[128,1024]{1,0:T(8,128)(2,1)S(1)} %shard_map.133.late.refs_2_, ...), custom_call_target="tpu_custom_call" | custom-call | flops 1200000000 | bytes 3000000 | tf_op jit(solution)/shard_map/pallas_call | solution.py:58
  86.5 12.8 %all-to-all-done.1 = f16[64,4,640]{2,1,0:T(4,128)(2,1)S(1)} async-done(((f16[64,4,640]{2,1,0:T(4,128)(2,1)}), f16[64,4,640]{2,1,0:T(4,128)(2,1)S(1)}, u32[]{:S(2)}, u32[]{:S(2)}) %all-to-all-start.1) | async-done | bytes 327712 | tf_op jit(solution)/shard_map/all_to_all | solution.py:455
  99.3 0.1 convert_element_type.15.refs_0_
  99.4 1.0 shard_map.138
  (23 shorter events, 0.1 us)
Async XLA Ops:
  0.6 26.2 %copy-start = (bf16[3,512,512]{2,1,0:T(8,128)(2,1)S(1)}, bf16[3,512,512]{2,1,0:T(8,128)(2,1)}, u32[]{:S(2)}) copy-start(bf16[3,512,512]{2,1,0:T(8,128)(2,1)} %weight.3) | copy-start | bytes 4718596
  0.6 26.2 %copy-start.1 = (bf16[512,512]{1,0:T(8,128)(2,1)S(1)}, bf16[512,512]{1,0:T(8,128)(2,1)}, u32[]{:S(2)}) copy-start(bf16[512,512]{1,0:T(8,128)(2,1)} %output_weight.3) | copy-start | bytes 1572868
  0.7 26.2 %copy-start.3 = (bf16[128,512]{1,0:T(8,128)(2,1)S(1)}, bf16[128,512]{1,0:T(8,128)(2,1)}, u32[]{:S(2)}) copy-start(bf16[128,512]{1,0:T(8,128)(2,1)} %cotangent.3) | copy-start | bytes 393220
  0.7 26.2 %copy-start.4 = (s32[128,64]{0,1:T(8,128)S(1)}, s32[128,64]{0,1:T(8,128)}, u32[]{:S(2)}) copy-start(s32[128,64]{0,1:T(8,128)} %param.15) | copy-start | bytes 98308
  0.7 26.2 %copy-start.5 = (s32[128,64]{0,1:T(8,128)S(1)}, s32[128,64]{0,1:T(8,128)}, u32[]{:S(2)}) copy-start(s32[128,64]{0,1:T(8,128)} %param.16) | copy-start | bytes 98308
  2.8 25.3 %collective-permute-start = (bf16[16,1024]{1,0:T(8,128)(2,1)S(1)}, bf16[16,1024]{1,0:T(8,128)(2,1)S(1)}, u32[]{:S(2)}, u32[]{:S(2)}) collective-permute-start(bf16[16,1024]{1,0:T(8,128)(2,1)S(1)} %get-tuple-element.27), channel_id=1, source_target_pairs={{0,504},{8,16},{16,8},{24,32},{32,24},{40,48},{48,40},{56,64},{64,... | collective-permute-start | bytes 98312 | tf_op jit(solution)/shard_map/ppermute | solution.py:363
  20.3 7.8 %collective-permute-start.1 = (bf16[16,1024]{1,0:T(8,128)(2,1)S(1)}, bf16[16,1024]{1,0:T(8,128)(2,1)S(1)}, u32[]{:S(2)}, u32[]{:S(2)}) collective-permute-start(bf16[16,1024]{1,0:T(8,128)(2,1)S(1)} %get-tuple-element.28), channel_id=1, source_target_pairs={{0,7},{1,2},{2,1},{3,4},{4,3},{5,6},{6,5},{7,0},{8,15},{9,10},{10,... | collective-permute-start | bytes 98312 | tf_op jit(solution)/shard_map/ppermute | solution.py:363
  22.7 5.8 %collective-permute-start.2 = (bf16[16,1024]{1,0:T(8,128)(2,1)S(1)}, bf16[16,1024]{1,0:T(8,128)(2,1)S(1)}, u32[]{:S(2)}, u32[]{:S(2)}) collective-permute-start(bf16[16,1024]{1,0:T(8,128)(2,1)S(1)} %get-tuple-element.29), channel_id=1, source_target_pairs={{0,8},{8,0},{16,24},{24,16},{32,40},{40,32},{48,56},{56,48},{64,72... | collective-permute-start | bytes 98312 | tf_op jit(solution)/shard_map/ppermute | solution.py:363
  24.6 3.9 %collective-permute-start.3 = (bf16[16,1024]{1,0:T(8,128)(2,1)S(1)}, bf16[16,1024]{1,0:T(8,128)(2,1)S(1)}, u32[]{:S(2)}, u32[]{:S(2)}) collective-permute-start(bf16[16,1024]{1,0:T(8,128)(2,1)S(1)} %get-tuple-element.30), channel_id=1, source_target_pairs={{0,1},{1,0},{2,3},{3,2},{4,5},{5,4},{6,7},{7,6},{8,9},{9,8},{10,11... | collective-permute-start | bytes 98312 | tf_op jit(solution)/shard_map/ppermute | solution.py:363
  28.5 19.8 %copy-start.6 = (s32[4,16]{1,0:T(4,128)S(1)}, s32[4,16]{1,0:T(4,128)}, u32[]{:S(2)}) copy-start(s32[4,16]{1,0:T(4,128)} %refs_1_.2) | copy-start | bytes 772
  31.3 19.6 %copy-start.8 = (s32[768,1]{1,0:T(8,128)S(1)}, s32[768,1]{1,0:T(8,128)}, u32[]{:S(2)}) copy-start(s32[768,1]{1,0:T(8,128)} %constant.4.clone.refs_1_) | copy-start | bytes 9220
  31.3 19.6 %copy-start.9 = (s32[256,1]{1,0:T(8,128)S(1)}, s32[256,1]{1,0:T(8,128)}, u32[]{:S(2)}) copy-start(s32[256,1]{1,0:T(8,128)} %constant.5.clone.refs_2_) | copy-start | bytes 3076
  31.3 17.0 %collective-permute-start.7 = (bf16[272,1024]{1,0:T(8,128)(2,1)S(1)}, bf16[272,1024]{1,0:T(8,128)(2,1)S(1)}, u32[]{:S(2)}, u32[]{:S(2)}) collective-permute-start(bf16[272,1024]{1,0:T(8,128)(2,1)S(1)} %get-tuple-element.31.sent.refs_0_.refs_1_), channel_id=1, source_target_pairs={{0,1},{1,0},{2,3},{3,2},{4,5},{5,4},{6,7},{7,6},{8,9},{9,8},{10,11... | collective-permute-start | bytes 1671176 | tf_op jit(solution)/shard_map/ppermute | solution.py:363
  33.4 13.9 %collective-permute-start.4 = (bf16[16,1024]{1,0:T(8,128)(2,1)S(1)}, bf16[16,1024]{1,0:T(8,128)(2,1)S(1)}, u32[]{:S(2)}, u32[]{:S(2)}) collective-permute-start(bf16[16,1024]{1,0:T(8,128)(2,1)S(1)} %get-tuple-element.33), channel_id=1, source_target_pairs={{0,504},{8,16},{16,8},{24,32},{32,24},{40,48},{48,40},{56,64},{64,... | collective-permute-start | bytes 98312 | tf_op jit(solution)/shard_map/ppermute | solution.py:363
  39.4 7.9 %collective-permute-start.5 = (bf16[16,1024]{1,0:T(8,128)(2,1)S(1)}, bf16[16,1024]{1,0:T(8,128)(2,1)S(1)}, u32[]{:S(2)}, u32[]{:S(2)}) collective-permute-start(bf16[16,1024]{1,0:T(8,128)(2,1)S(1)} %get-tuple-element.34), channel_id=1, source_target_pairs={{0,7},{1,2},{2,1},{3,4},{4,3},{5,6},{6,5},{7,0},{8,15},{9,10},{10,... | collective-permute-start | bytes 98312 | tf_op jit(solution)/shard_map/ppermute | solution.py:363
  42.5 5.8 %collective-permute-start.6 = (bf16[16,1024]{1,0:T(8,128)(2,1)S(1)}, bf16[16,1024]{1,0:T(8,128)(2,1)S(1)}, u32[]{:S(2)}, u32[]{:S(2)}) collective-permute-start(bf16[16,1024]{1,0:T(8,128)(2,1)S(1)} %get-tuple-element.35), channel_id=1, source_target_pairs={{0,8},{8,0},{16,24},{24,16},{32,40},{40,32},{48,56},{56,48},{64,72... | collective-permute-start | bytes 98312 | tf_op jit(solution)/shard_map/ppermute | solution.py:363
  48.9 3.4 %collective-permute-start.8 = (bf16[128,1024]{1,0:T(8,128)(2,1)S(1)}, bf16[128,1024]{1,0:T(8,128)(2,1)S(1)}, u32[]{:S(2)}, u32[]{:S(2)}) collective-permute-start(bf16[128,1024]{1,0:T(8,128)(2,1)S(1)} %shard_map.133.late.refs_2_), channel_id=1, source_target_pairs={{0,1},{1,0},{2,3},{3,2},{4,5},{5,4},{6,7},{7,6},{8,9},{9,8},{10,11... | collective-permute-start | bytes 786440 | tf_op jit(solution)/shard_map/ppermute | solution.py:363
  72.9 11.2 %copy-start.2 = (bf16[128,512]{1,0:T(8,128)(2,1)S(1)}, bf16[128,512]{1,0:T(8,128)(2,1)}, u32[]{:S(2)}) copy-start(bf16[128,512]{1,0:T(8,128)(2,1)} %features.3) | copy-start | bytes 393220
  74.5 24.8 %all-to-all-start.1 = ((f16[64,4,640]{2,1,0:T(4,128)(2,1)}), f16[64,4,640]{2,1,0:T(4,128)(2,1)S(1)}, u32[]{:S(2)}, u32[]{:S(2)}) async-start(f16[64,4,640]{2,1,0:T(4,128)(2,1)} %convert_element_type.14), calls=%async_computation.1 | async-start | bytes 655360 | tf_op jit(solution)/shard_map/all_to_all | solution.py:455
  84.1 0.9 copy-start.7
